TPU v7x, 32 devices: a whole 2x2x4 slice. The times are simulated.
32 devices in a mesh: parts: 2 (over y), tile: 4 (over x, core), chan: 4 (over z).
Axes of the slice: x: 2, y: 2, z: 4, core: 2. Of those that a mesh axis runs over, the one named last changes fastest.
Arguments:
- weather: bfloat16 [768, 64, 1440], P('chan', 'parts', 'tile'), parts along dimension 1, may hold values from -6 to 6
- lon_taps: float32 [9, 768], P(None, 'chan'), may hold values from -4 to 4
- latitude_taps: float32 [9, 768], P(None, 'chan'), may hold values from -2 to 2
- norm_gain: float32 [768], replicated, may hold values from 0.1 to 1.9
- up_weight: bfloat16 [768, 3072], P(None, ('tile', 'chan')), may hold values from -0.21875 to 0.21875
- down_weight: bfloat16 [768, 3072], P(None, ('tile', 'chan')), may hold values from -0.109375 to 0.109375
Outputs:
- mixed: bfloat16 [768, 64, 1440], P('chan', 'parts', 'tile'), parts along dimension 1
There are 2 independent parts, one for each index of `parts`. A program takes and returns all parts, laid end to end along the dimension named above; an argument that names none is the same for every part. Nothing has to cross between parts.
All inputs are finite; a program needn't handle non-finite values.
Results may differ from a plain program's by a relative error of at most 0.0065.
Values may be sent and summed in bfloat16 or wider, within the bound.
No kernel may reach another device: no remote copies, remote signals or barrier semaphores. Data moves between devices by JAX's collectives and lax.ppermute only.
A program may use at most 128 MiB of HBM per device.

v0:
```python
import jax
import jax.numpy as jnp
from jax import lax
from jax.sharding import PartitionSpec as P

KERNEL_TAPS = 9
DILATION_STEP = 2


def with_halo(shard, sides, width):
    for axis, dim in sides:
        devices, length = (lax.axis_size(axis), shard.shape[dim])
        up = [(i, (i + 1) % devices) for i in range(devices)]
        down = [(j, i) for i, j in up]
        last = lax.slice_in_dim(shard, length - width, length, axis=dim)
        initial = lax.slice_in_dim(shard, 0, width, axis=dim)
        before = lax.ppermute(last, axis, up)
        after = lax.ppermute(initial, axis, down)
        shard = jnp.concatenate([before, shard, after], axis=dim)
    return shard


def layer_norm(values, norm_gain):
    as_float = values.astype(jnp.float32)
    center = jnp.mean(as_float, axis=0)
    deviation = as_float - center
    spread_sq = jnp.mean(deviation * deviation, axis=0)
    return (deviation * lax.rsqrt(spread_sq + 1e-06) * norm_gain[:, None]).astype(jnp.bfloat16)


def on_device(weather, lon_taps, latitude_taps, norm_gain, up_weight, down_weight):
    chan_count, row_total, column_total = weather.shape
    border_width = DILATION_STEP * (KERNEL_TAPS // 2)
    widened_field = with_halo(weather, (("tile", 2),), border_width)
    lon_sum = jnp.zeros(weather.shape, jnp.float32)
    for kernel_tap_index in range(KERNEL_TAPS):
        sliding_window = widened_field[
            :, :, DILATION_STEP * kernel_tap_index : DILATION_STEP * kernel_tap_index + column_total
        ].astype(jnp.float32)
        lon_sum = lon_sum + lon_taps[kernel_tap_index][:, None, None] * sliding_window
    padded_field = jnp.pad(lon_sum, ((0, 0), (border_width, border_width), (0, 0)))
    latitude_sum = jnp.zeros(weather.shape, jnp.float32)
    for kernel_tap_index in range(KERNEL_TAPS):
        latitude_sum = (
            latitude_sum
            + latitude_taps[kernel_tap_index][:, None, None]
            * padded_field[
                :,
                DILATION_STEP * kernel_tap_index : DILATION_STEP * kernel_tap_index + row_total,
                :,
            ]
        )
    spatial = latitude_sum.astype(jnp.bfloat16)
    group_count = lax.axis_size("chan")
    width_all = chan_count * group_count
    shard_width = up_weight.shape[1]
    by_cell = lax.all_to_all(spatial, "chan", split_axis=1, concat_axis=0, tiled=True)
    cell_count = by_cell.shape[1] * by_cell.shape[2]
    normed = layer_norm(by_cell.reshape(width_all, cell_count), norm_gain)
    expanded = lax.dot_general(
        lax.all_gather(up_weight, ("tile", "chan"), axis=1, tiled=True),
        normed,
        (((0,), (0,)), ((), ())),
        preferred_element_type=jnp.float32,
    )
    hidden = jax.nn.gelu(expanded, approximate=False).astype(jnp.bfloat16)
    down_all = lax.all_gather(down_weight, ("tile", "chan"), axis=1, tiled=True)
    tile_count = down_all.shape[1] // (group_count * shard_width)
    down_groups = down_all.reshape(width_all, tile_count, group_count, shard_width)
    hidden_groups = hidden.reshape(tile_count, group_count, shard_width, cell_count)
    summed = jnp.zeros((width_all, cell_count), jnp.float32)
    for group in range(group_count):
        group_value = jnp.einsum(
            "dts,tsc->dc",
            down_groups[:, :, group, :],
            hidden_groups[:, group],
            preferred_element_type=jnp.float32,
        ).astype(jnp.bfloat16)
        group_value = lax.optimization_barrier(group_value)
        summed = summed + group_value.astype(jnp.float32)
    update_cells = summed.astype(jnp.bfloat16).reshape(width_all, by_cell.shape[1], column_total)
    update = lax.all_to_all(update_cells, "chan", split_axis=0, concat_axis=1, tiled=True)
    return (weather.astype(jnp.float32) + update.astype(jnp.float32)).astype(jnp.bfloat16)


def solution(mesh):
    return jax.shard_map(
        on_device,
        mesh=mesh,
        in_specs=(
            P("chan", "parts", "tile"),
            P(None, "chan"),
            P(None, "chan"),
            P(),
            P(None, ("tile", "chan")),
            P(None, ("tile", "chan")),
        ),
        out_specs=P("chan", "parts", "tile"),
        check_vma=False,
    )
```

profile of v0, /device:TPU:0, one launch (start us, length us, event | category | flops | bytes accessed | tf_op | source)
XLA Modules:
  0.0 563.3 jit_solution(12894988400171444290)
XLA Ops:
  6.5 0.0 copy-start.1
  6.5 0.0 copy-start.2
  6.5 0.0 all-gather.3.cloned.1.call-start
  6.5 0.7 all-gather.3.cloned.1.call-update
  7.3 2.6 fusion.56
  9.9 1.3 copy.53
  11.2 2.4 collective-permute-start.1
  13.6 1.3 copy.52
  14.9 0.1 collective-permute-start
  14.9 0.0 copy-done.1
  14.9 0.0 copy-done.2
  15.0 4.3 collective-permute-done
  19.3 1.3 copy.36
  20.6 0.0 collective-permute-done.1
  20.6 1.3 copy.38
  22.0 36.4 %fusion.22 = f32[192,32,360]{2,1,0:T(8,128)} fusion(bf16[192,32,360]{2,1,0:T(8,128)(2,1)} %param.6, bf16[192,32,8]{2,1,0:T(8,128)(2,1)S(1)} %copy.38, bf16[192,32,8]{2,1,0:T(8,128)(2,1)S(1)} %copy.36, f32[192]{0:T(256)S(1)} %bitcast.205, f32[192]{0:T(256)S(1)} %bitcast.206, f32[192]{0:T(256)S(1)} %bitcast.199, f32[192]{0:T(256)S(1)} %bitcast.200, ...), kind=kLoop, calls=%fused_computation.38 | loop fusion | flops 110592000 | bytes 13474560 | tf_op jit(solution)/shard_map/add | solution.py:40
  58.4 34.3 %fusion.33 = bf16[192,32,360]{2,1,0:T(8,128)(2,1)S(1)} fusion(f32[192,32,360]{2,1,0:T(8,128)} %fusion.22, f32[192]{0:T(256)S(1)} %bitcast.196, f32[192]{0:T(256)S(1)} %bitcast.197, f32[192]{0:T(256)S(1)} %bitcast.190, f32[192]{0:T(256)S(1)} %bitcast.191, f32[192]{0:T(256)S(1)} %bitcast.192, f32[192]{0:T(256)S(1)} %bitcast.193, f32[192]{0:T(256)S(1)} %bitcast.194, ...), kind=kLoop, calls=%fused_computation.49 | loop fusion | flops 39813120 | bytes 13277952 | tf_op jit(solution)/shard_map/convert_element_type | solution.py:53
  92.7 4.0 copy.39
  96.7 5.0 all-to-all-start
  101.6 0.3 all-gather.5.cloned.1.call-start
  101.9 0.4 all-gather.5.cloned.1.call-update
  102.4 130.9 %all-to-all-done = bf16[192,32,360]{2,0,1:T(8,128)(2,1)} async-done(((bf16[192,32,360]{2,0,1:T(8,128)(2,1)}), bf16[192,32,360]{2,0,1:T(8,128)(2,1)}, u32[]{:S(2)}, u32[]{:S(2)}) %all-to-all-start) | async-done | bytes 4423712 | tf_op jit(solution)/shard_map/all_to_all | solution.py:57
  233.2 3.5 bitcast_convert_fusion.4
  236.7 5.0 fusion.55
  241.7 9.1 %copy.68 = f32[192,4,8,360]{3,2,0,1:T(8,128)} copy(f32[192,4,8,360]{3,0,2,1:T(8,128)S(1)} %bitcast_convert_fusion.4) | data formatting | bytes 17694720 | tf_op jit(solution)/shard_map/convert_element_type | solution.py:24
  250.8 5.0 multiply_reduce_fusion
  255.8 0.0 copy-start.3
  255.9 0.1 div.9
  255.9 11.5 %reshape.71 = f32[768,2880]{1,0:T(8,128)} reshape(f32[4,192,8,360]{3,2,1,0:T(8,128)} %bitcast.180) | data formatting | bytes 17694720 | tf_op jit(solution)/shard_map/convert_element_type | solution.py:24
  267.4 0.1 rsqrt.11
  267.5 0.0 copy-done.3
  267.5 7.2 %multiply_convert_fusion.1.clone.4 = bf16[768,2880]{1,0:T(8,128)(2,1)} fusion(f32[768,2880]{1,0:T(8,128)} %reshape.71, f32[768]{0:T(1024)S(1)} %copy-done.3, f32[2880]{0:T(1024)S(1)} %rsqrt.11, f32[2880]{0:T(1024)S(1)} %div.9), kind=kLoop, calls=%fused_computation.60.clone.clone.clone.clone.1 | loop fusion | flops 8847360 | bytes 13297152 | tf_op jit(solution)/shard_map/convert_element_type | solution.py:66
  274.7 0.0 all-gather.3.cloned.1.call-done
  274.7 102.8 %fusion.2 = bf16[3072,2880]{0,1:T(8,128)(2,1)} fusion(bf16[768,3072]{0,1:T(8,128)(2,1)} %all-gather.3.cloned.1.call-done, bf16[768,2880]{1,0:T(8,128)(2,1)} %multiply_convert_fusion.1.clone.4), kind=kOutput, calls=%fused_computation.3 | convolution fusion | flops 14164623360 | bytes 26836992 | tf_op jit(solution)/shard_map/dot_general | solution.py:60
  377.5 22.1 %copy.41 = bf16[3072,2880]{1,0:T(8,128)(2,1)} copy(bf16[3072,2880]{0,1:T(8,128)(2,1)} %fusion.2) | data formatting | bytes 35389440 | tf_op jit(solution)/shard_map/convert_element_type | solution.py:66
  399.7 0.0 all-gather.5.cloned.1.call-done
  399.7 0.0 copy-start
  399.7 0.0 copy-start.4
  399.7 8.7 %fusion.53 = bf16[768,2880]{0,1:T(8,128)(2,1)} fusion(bf16[4,4,192,2880]{3,2,1,0:T(8,128)(2,1)} %bitcast.184, bf16[768,4,4,192]{0,3,2,1:T(8,128)(2,1)} %bitcast.207), kind=kOutput, calls=%fused_computation.92 | convolution fusion | flops 3399598080 | bytes 10125312 | tf_op jit(solution)/shard_map/dts,tsc->dc/dot_general | solution.py:73
  408.4 0.1 copy-done
  408.5 1.9 copy-done.4
  410.5 5.5 fusion.52
  415.9 5.6 fusion.51
  421.5 5.7 %fusion.54 = bf16[768,2880]{0,1:T(8,128)(2,1)} fusion(bf16[4,4,192,2880]{3,2,1,0:T(8,128)(2,1)S(1)} %bitcast.187, bf16[768,4,4,192]{0,3,2,1:T(8,128)(2,1)S(1)} %bitcast.210), kind=kOutput, calls=%fused_computation.93 | convolution fusion | flops 3399598080 | bytes 10125312 | tf_op jit(solution)/shard_map/dts,tsc->dc/dot_general | solution.py:73
  427.2 10.3 %add_convert_fusion = bf16[768,2880]{0,1:T(8,128)(2,1)} fusion(bf16[768,2880]{0,1:T(8,128)(2,1)} %fusion.54, bf16[768,2880]{0,1:T(8,128)(2,1)} %fusion.53, bf16[768,2880]{0,1:T(8,128)(2,1)} %fusion.52, bf16[768,2880]{0,1:T(8,128)(2,1)} %fusion.51), kind=kLoop, calls=%fused_computation.65 | loop fusion | flops 17694720 | bytes 22118400 | tf_op jit(solution)/shard_map/convert_element_type | solution.py:81
  437.6 0.0 slice-start
  437.6 7.0 %copy.50 = bf16[768,8,360]{2,1,0:T(8,128)(2,1)} copy(bf16[768,8,360]{0,2,1:T(8,128)(2,1)} %bitcast.188) | data formatting | bytes 8847360 | tf_op jit(solution)/shard_map/reshape | solution.py:81
  444.5 0.0 slice-start.1
  444.5 108.1 %all_to_all.8 = bf16[768,8,360]{2,1,0:T(8,128)(2,1)S(1)} all-to-all(bf16[768,8,360]{2,1,0:T(8,128)(2,1)} %copy.50), channel_id=1, replica_groups=mesh['parts'=2,'tile'=4,'chan'=4] {'chan'}, dimensions={0} | all-to-all | bytes 8847360 | tf_op jit(solution)/shard_map/all_to_all | solution.py:82
  552.7 0.0 slice-done
  552.7 0.0 slice-done.1
  552.7 3.4 fusion.23
  (5 shorter events, 0.0 us)
Async XLA Ops:
  6.5 8.4 %copy-start.1 = (f32[9,192]{1,0:T(8,128)S(1)}, f32[9,192]{1,0:T(8,128)}, u32[]{:S(2)}) copy-start(f32[9,192]{1,0:T(8,128)} %param.7) | copy-start | bytes 20740
  6.5 8.4 %copy-start.2 = (f32[9,192]{1,0:T(8,128)S(1)}, f32[9,192]{1,0:T(8,128)}, u32[]{:S(2)}) copy-start(f32[9,192]{1,0:T(8,128)} %param.8) | copy-start | bytes 20740
  6.5 268.1 %all-gather.3.cloned.1.call-start = ((), (), s32[]{:S(2)}) async-start(), calls=%async_computation.2 | async-start | bytes 5013504 | tf_op jit(solution)/shard_map/all_gather | solution.py:61
  11.2 9.5 %collective-permute-start.1 = (bf16[192,32,8]{0,2,1:T(8,128)(2,1)S(1)}, bf16[192,32,8]{0,2,1:T(8,128)(2,1)S(1)}, u32[]{:S(2)}, u32[]{:S(2)}) collective-permute-start(bf16[192,32,8]{0,2,1:T(8,128)(2,1)S(1)} %copy.53), channel_id=1, source_target_pairs={{4,0},{8,4},{12,8},{0,12},{5,1},{9,5},{13,9},{1,13},{6,2},{10,6},{... | collective-permute-start | bytes 294920 | tf_op jit(solution)/shard_map/ppermute | solution.py:18
  14.9 4.4 collective-permute-start
  96.7 136.6 %all-to-all-start = ((bf16[192,32,360]{2,0,1:T(8,128)(2,1)}), bf16[192,32,360]{2,0,1:T(8,128)(2,1)}, u32[]{:S(2)}, u32[]{:S(2)}) async-start(bf16[192,32,360]{2,0,1:T(8,128)(2,1)} %copy.39), calls=%async_computation | async-start | bytes 9437184 | tf_op jit(solution)/shard_map/all_to_all | solution.py:57
  101.6 298.0 %all-gather.5.cloned.1.call-start = ((), (), s32[]{:S(2)}) async-start(), calls=%async_computation.3 | async-start | bytes 5013504 | tf_op jit(solution)/shard_map/all_gather | solution.py:67
  255.8 11.7 %copy-start.3 = (f32[768]{0:T(1024)S(1)}, f32[768]{0:T(1024)}, u32[]{:S(2)}) copy-start(f32[768]{0:T(1024)} %param.9) | copy-start | bytes 9220
  399.7 8.8 %copy-start = (bf16[3072,2880]{1,0:T(8,128)(2,1)S(1)}, bf16[3072,2880]{1,0:T(8,128)(2,1)}, u32[]{:S(2)}) copy-start(bf16[3072,2880]{1,0:T(8,128)(2,1)} %copy.41) | copy-start | bytes 53084164
  399.7 10.8 %copy-start.4 = (bf16[768,3072]{0,1:T(8,128)(2,1)S(1)}, bf16[768,3072]{0,1:T(8,128)(2,1)}, u32[]{:S(2)}) copy-start(bf16[768,3072]{0,1:T(8,128)(2,1)} %all-gather.5.cloned.1.call-done) | copy-start | bytes 14155780
  437.6 115.1 %slice-start = ((s8[4718592]{0:T(1024)(128)(4,1)}), s8[524288]{0:T(1024)(128)(4,1)S(1)}, s32[]{:S(2)}) async-start(s8[4718592]{0:T(1024)(128)(4,1)} %bitcast.181), calls=%async_computation.4 | async-start | bytes 1048576
  444.5 108.1 %slice-start.1 = ((s8[4718592]{0:T(1024)(128)(4,1)}), s8[4194304]{0:T(1024)(128)(4,1)S(1)}, s32[]{:S(2)}) async-start(s8[4718592]{0:T(1024)(128)(4,1)} %bitcast.181), calls=%async_computation.5 | async-start | bytes 8388608
Sparse Core Ops, SparseCore 0:
  9.7 56.0 all-gather.2
  104.8 103.3 all-gather.4
where the time goes:
time: 572 us; the launch traced here: 563 us
  waiting for transfers between devices  136 us (24%)
  matrix products  128 us (22%)
  blocking collectives  108 us (19%)
  other arithmetic  105 us (18%)
  local copies, waits for them, and re-layouts  63.8 us (11%)
  between operations  14 us (2%)
  starting transfers between devices  7.74 us (1%)
    all_to_all x1, waiting for transfers between devices, on_device(): lax.all_to_all(spatial, 'chan', split_axis=1, concat_axis=0, tiled=True)  131 us
    all_to_all x1, blocking collectives, on_device(): lax.all_to_all(update_cells, 'chan', split_axis=0, concat_axis=1, tiled=T...  108 us
    dot_general x1, matrix products, on_device(): lax.dot_general(lax.all_gather(up_weight, ('tile', 'chan'), axis=1, tiled...  103 us
    add x1, other arithmetic, on_device(): lon_sum + lon_taps[kernel_tap_index][:, None, None] * sliding_window  36.4 us
    convert_element_type x1, other arithmetic, on_device(): spatial = latitude_sum.astype(jnp.bfloat16)  34.3 us
    dot_general x4, matrix products, on_device(): jnp.einsum('dts,tsc->dc', down_groups[:, :, group, :], hidden_groups[:, g...  25.5 us
    convert_element_type x1, local copies, waits for them, and re-layouts, on_device(): hidden = jax.nn.gelu(expanded, approximate=False).astype(jnp.bfloat16)  22.1 us
    convert_element_type x2, local copies, waits for them, and re-layouts, layer_norm(): as_float = values.astype(jnp.float32)  20.6 us
  transfers between devices with their start and end apart: 5, of which 2 were waited for; matrix products, arithmetic and copies ran while one was open for 44% of the time, Pallas kernels for 0%

commit v1 on v0

v1 whole, which is shorter than its diff:
```python
import functools

import jax
import jax.numpy as jnp
from jax import lax
from jax.experimental import pallas as pl
from jax.experimental.pallas import tpu as pltpu
from jax.sharding import PartitionSpec as P

KERNEL_TAPS = 9
DILATION_STEP = 2
BORDER = DILATION_STEP * (KERNEL_TAPS // 2)
LANES = 128
CHUNKS = 4
VMEM_BYTES = 60 * 1024 * 1024


def round_up(value, step):
    return -(-value // step) * step


def conv_kernel(first_row, row_count, field_ref, before_ref, after_ref, lon_ref, lat_ref, out_ref, base_ref):
    row_total, _, width = field_ref.shape
    wide = base_ref.shape[2]
    low = max(0, first_row - BORDER)
    high = min(row_total, first_row + row_count + BORDER)
    for row in range(low, high):
        base_ref[row - low, :, 0:width] = field_ref[row].astype(jnp.float32)
        base_ref[row - low, :, width : width + BORDER] = after_ref[row].astype(jnp.float32)
        base_ref[row - low, :, wide - BORDER : wide] = before_ref[row].astype(jnp.float32)
    block = base_ref.shape[1]
    lon = [jnp.broadcast_to(lon_ref[:, t : t + 1], (block, wide)) for t in range(KERNEL_TAPS)]
    lat = [jnp.broadcast_to(lat_ref[:, t : t + 1], (block, wide)) for t in range(KERNEL_TAPS)]
    for out_row in range(row_count):
        total = None
        for t in range(KERNEL_TAPS):
            row = first_row + out_row + DILATION_STEP * (t - KERNEL_TAPS // 2)
            if low <= row < high:
                term = lat[t] * base_ref[row - low]
                total = term if total is None else total + term
        result = lon[KERNEL_TAPS // 2] * total
        for t in range(KERNEL_TAPS):
            shift = DILATION_STEP * (t - KERNEL_TAPS // 2)
            if shift:
                result = result + lon[t] * pltpu.roll(total, (-shift) % wide, 1)
        out_ref[out_row] = result[:, 0:width].astype(out_ref.dtype)


def convolve(field, before, after, lon_taps, lat_taps, first_row, row_count):
    row_total, chan_count, width = field.shape
    block = 32
    wide = round_up(width + 2 * BORDER, LANES)
    held_rows = min(row_total, first_row + row_count + BORDER) - max(0, first_row - BORDER)
    return pl.pallas_call(
        functools.partial(conv_kernel, first_row, row_count),
        grid=(chan_count // block,),
        in_specs=[
            pl.BlockSpec((row_total, block, width), lambda c: (0, c, 0)),
            pl.BlockSpec((row_total, block, BORDER), lambda c: (0, c, 0)),
            pl.BlockSpec((row_total, block, BORDER), lambda c: (0, c, 0)),
            pl.BlockSpec((block, KERNEL_TAPS), lambda c: (c, 0)),
            pl.BlockSpec((block, KERNEL_TAPS), lambda c: (c, 0)),
        ],
        out_specs=pl.BlockSpec((row_count, block, width), lambda c: (0, c, 0)),
        out_shape=jax.ShapeDtypeStruct((row_count, chan_count, width), jnp.bfloat16),
        scratch_shapes=[pltpu.VMEM((held_rows, block, wide), jnp.float32)],
        compiler_params=pltpu.CompilerParams(vmem_limit_bytes=VMEM_BYTES),
        name="conv",
    )(field, before, after, lon_taps, lat_taps)


def mlp_kernel(sources, x_ref, gain_ref, up_ref, down_ref, out_ref, values, normed, total):
    step = pl.program_id(0)
    rows = x_ref.shape[0] // sources
    chan_count, width = x_ref.shape[1:]
    wide = values.shape[1] // rows

    @pl.when(step == 0)
    def _():
        for source in range(sources):
            for row in range(rows):
                values[source * chan_count : (source + 1) * chan_count, row * wide : row * wide + width] = x_ref[
                    source * rows + row
                ].astype(jnp.float32)
        as_float = values[...]
        center = jnp.mean(as_float, axis=0, keepdims=True)
        deviation = as_float - center
        spread_sq = jnp.mean(deviation * deviation, axis=0, keepdims=True)
        normed[...] = (deviation * lax.rsqrt(spread_sq + 1e-06) * gain_ref[...]).astype(jnp.bfloat16)
        total[...] = jnp.zeros_like(total)

    expanded = jnp.dot(up_ref[...], normed[...], preferred_element_type=jnp.float32)
    hidden = (0.5 * expanded * (1.0 + lax.erf(expanded * 0.7071067811865476))).astype(jnp.bfloat16)
    total[...] += jnp.dot(down_ref[...], hidden, preferred_element_type=jnp.float32)

    @pl.when(step == pl.num_programs(0) - 1)
    def _():
        for source in range(sources):
            for row in range(rows):
                out_ref[source * rows + row] = total[
                    source * chan_count : (source + 1) * chan_count, row * wide : row * wide + width
                ].astype(out_ref.dtype)


def mlp(x, sources, gain, up_all, down_all):
    row_count, chan_count, width = x.shape
    width_all, hidden_total = down_all.shape
    block = 512
    lanes = (row_count // sources) * round_up(width, LANES)
    return pl.pallas_call(
        functools.partial(mlp_kernel, sources),
        grid=(hidden_total // block,),
        in_specs=[
            pl.BlockSpec((row_count, chan_count, width), lambda h: (0, 0, 0)),
            pl.BlockSpec((width_all, 1), lambda h: (0, 0)),
            pl.BlockSpec((block, width_all), lambda h: (h, 0)),
            pl.BlockSpec((width_all, block), lambda h: (0, h)),
        ],
        out_specs=pl.BlockSpec((row_count, chan_count, width), lambda h: (0, 0, 0)),
        out_shape=jax.ShapeDtypeStruct(x.shape, jnp.bfloat16),
        scratch_shapes=[
            pltpu.VMEM((width_all, lanes), jnp.float32),
            pltpu.VMEM((width_all, lanes), jnp.bfloat16),
            pltpu.VMEM((width_all, lanes), jnp.float32),
        ],
        compiler_params=pltpu.CompilerParams(vmem_limit_bytes=VMEM_BYTES),
        name="mlp",
    )(x, gain, up_all, down_all)


def add_kernel(update_ref, field_ref, *rest):
    out_ref = rest[-1]
    update = jnp.transpose(update_ref[...].astype(jnp.float32), (1, 0, 2))
    out_ref[...] = (field_ref[...].astype(jnp.float32) + update).astype(out_ref.dtype)


def add_rows(update, field, done, place):
    row_count, chan_count, width = update.shape
    block = 32
    rows_of = pl.BlockSpec((block, row_count, width), lambda c: (c, place, 0))
    specs = [pl.BlockSpec((row_count, block, width), lambda c: (0, c, 0)), rows_of]
    operands = [update, field]
    if done is not None:
        specs.append(pl.BlockSpec(memory_space=pl.ANY))
        operands.append(done)
    return pl.pallas_call(
        add_kernel,
        grid=(chan_count // block,),
        in_specs=specs,
        out_specs=rows_of,
        out_shape=jax.ShapeDtypeStruct(field.shape, jnp.bfloat16),
        input_output_aliases={2: 0} if done is not None else {},
        compiler_params=pltpu.CompilerParams(vmem_limit_bytes=VMEM_BYTES),
        name="add",
    )(*operands)


def gather_weights(shard):
    chans = lax.axis_size("chan")
    held = [shard[None]]
    for shift in range(1, chans):
        held.append(lax.ppermute(shard[None], "chan", [(i, (i + shift) % chans) for i in range(chans)]))
    held = jnp.concatenate(held, axis=0)
    tiles = lax.axis_size("tile")
    bit = tiles // 2
    while bit:
        held = jnp.concatenate([held, lax.ppermute(held, "tile", [(i, i ^ bit) for i in range(tiles)])], axis=0)
        bit //= 2
    return held


def on_device(weather, lon_taps, latitude_taps, norm_gain, up_weight, down_weight):
    chan_count, row_total, width = weather.shape
    sources = lax.axis_size("chan")
    tiles = lax.axis_size("tile")
    up = [(i, (i + 1) % tiles) for i in range(tiles)]
    down = [(j, i) for i, j in up]
    before = lax.ppermute(weather[:, :, width - BORDER :], "tile", up)
    after = lax.ppermute(weather[:, :, :BORDER], "tile", down)
    shard_width = up_weight.shape[1]
    weights = gather_weights(jnp.concatenate([up_weight.T, down_weight.T], axis=0))
    up_all = weights[:, :shard_width].reshape(-1, up_weight.shape[0])
    down_all = weights[:, shard_width:].reshape(-1, up_weight.shape[0]).T
    field = jnp.transpose(weather, (1, 0, 2))
    before = jnp.transpose(before, (1, 0, 2))
    after = jnp.transpose(after, (1, 0, 2))
    lon, lat = lon_taps.T, latitude_taps.T
    rows = row_total // CHUNKS
    by_cell = []
    for chunk in range(CHUNKS):
        spatial = convolve(field, before, after, lon, lat, chunk * rows, rows)
        by_cell.append(lax.all_to_all(spatial, "chan", split_axis=0, concat_axis=0, tiled=True))
    gain = norm_gain[:, None]
    updates = []
    for chunk in range(CHUNKS):
        update = mlp(by_cell[chunk], sources, gain, up_all, down_all)
        updates.append(lax.all_to_all(update, "chan", split_axis=0, concat_axis=0, tiled=True))
    mixed = None
    for chunk in range(CHUNKS):
        mixed = add_rows(updates[chunk], weather, mixed, chunk)
    return mixed


def solution(mesh):
    return jax.shard_map(
        on_device,
        mesh=mesh,
        in_specs=(
            P("chan", "parts", "tile"),
            P(None, "chan"),
            P(None, "chan"),
            P(),
            P(None, ("tile", "chan")),
            P(None, ("tile", "chan")),
        ),
        out_specs=P("chan", "parts", "tile"),
        check_vma=False,
    )
```

time: 572 us -> 393 us (0.69)
  the two profiles are of different devices: /device:TPU:0 before, /device:TPU:24 now
where the time goes in v1:
time: 393 us; the launch traced here: 387 us
  waiting for transfers between devices  178 us (45%)
  Pallas kernels  110 us (28%)
  starting transfers between devices  51.6 us (13%)
  local copies, waits for them, and re-layouts  43.5 us (11%)
  other arithmetic  4.18 us (1%)
    pallas_call x4, Pallas kernels, mlp(): pl.pallas_call(functools.partial(mlp_kernel, sources), grid=(hidden_total...  52.1 us
    ppermute x3, waiting for transfers between devices, gather_weights(): lax.ppermute(shard[None], 'chan', [(i, (i + shift) % chans) for i in rang...  50.5 us
    all_to_all x4, waiting for transfers between devices, on_device(): lax.all_to_all(update, 'chan', split_axis=0, concat_axis=0, tiled=True)  48.1 us
    all_to_all x4, waiting for transfers between devices, on_device(): lax.all_to_all(spatial, 'chan', split_axis=0, concat_axis=0, tiled=True)  40.8 us
    ppermute x1, waiting for transfers between devices, on_device(): before = lax.ppermute(weather[:, :, width - BORDER:], 'tile', up)  38.7 us
    pallas_call x4, Pallas kernels, convolve(): pl.pallas_call(functools.partial(conv_kernel, first_row, row_count), grid...  37.7 us
    all_to_all x4, starting transfers between devices, on_device(): lax.all_to_all(spatial, 'chan', split_axis=0, concat_axis=0, tiled=True)  23.2 us
    all_to_all x4, starting transfers between devices, on_device(): lax.all_to_all(update, 'chan', split_axis=0, concat_axis=0, tiled=True)  22.7 us
  transfers between devices with their start and end apart: 15, of which 10 were waited for; matrix products, arithmetic and copies ran while one was open for 11% of the time, Pallas kernels for 27%

profile of v1, /device:TPU:24, one launch (start us, length us, event | category | flops | bytes accessed | tf_op | source)
XLA Modules:
  0.0 387.2 jit_solution(17812062535949996158)
XLA Ops:
  0.0 1.2 maximum_bitcast_fusion
  1.2 0.1 collective-permute-start.2
  1.3 1.9 collective-permute-start.3
  3.2 0.4 collective-permute-start.4
  3.7 13.1 %collective-permute-done.2 = bf16[1,384,768]{2,1,0:T(8,128)(2,1)S(1)} collective-permute-done((bf16[1,384,768]{2,1,0:T(8,128)(2,1)S(1)}, bf16[1,384,768]{2,1,0:T(8,128)(2,1)S(1)}, u32[]{:S(2)}, u32[]{:S(2)}) %collective-permute-start.2) | collective-permute-done | bytes 589856 | tf_op jit(solution)/shard_map/ppermute | solution.py:162
  16.8 37.4 %collective-permute-done.3 = bf16[1,384,768]{2,1,0:T(8,128)(2,1)S(1)} collective-permute-done((bf16[1,384,768]{2,1,0:T(8,128)(2,1)S(1)}, bf16[1,384,768]{2,1,0:T(8,128)(2,1)S(1)}, u32[]{:S(2)}, u32[]{:S(2)}) %collective-permute-start.3) | collective-permute-done | bytes 589856 | tf_op jit(solution)/shard_map/ppermute | solution.py:162
  54.2 0.0 collective-permute-done.4
  54.2 1.8 pad_maximum_fusion
  56.0 1.5 collective-permute-start.5
  57.5 0.7 fusion.1
  58.2 1.3 copy.38
  59.5 0.1 collective-permute-start
  59.6 1.3 copy.39
  60.9 0.0 copy-start.17
  60.9 0.0 copy-start.18
  60.9 1.8 collective-permute-start.1
  62.7 6.2 %copy.41 = bf16[192,32,360]{2,0,1:T(8,128)(2,1)} copy(bf16[192,32,360]{2,1,0:T(8,128)(2,1)} %field_ref.7) | data formatting | bytes 8847360 | tf_op args[0]
  68.9 0.7 copy.31
  69.7 0.7 copy.32
  70.4 38.7 %collective-permute-done = bf16[192,32,8]{0,2,1:T(8,128)(2,1)S(1)} collective-permute-done((bf16[192,32,8]{0,2,1:T(8,128)(2,1)S(1)}, bf16[192,32,8]{0,2,1:T(8,128)(2,1)S(1)}, u32[]{:S(2)}, u32[]{:S(2)}) %collective-permute-start) | collective-permute-done | bytes 98336 | tf_op jit(solution)/shard_map/ppermute | solution.py:178
  109.1 1.5 copy.28
  110.6 0.0 collective-permute-done.1
  110.6 1.5 copy.30
  112.1 9.4 %conv.7 = bf16[8,192,360]{2,1,0:T(8,128)(2,1)} custom-call(bf16[32,192,360]{2,1,0:T(8,128)(2,1)} %bitcast.18, bf16[32,192,8]{2,1,0:T(8,128)(2,1)} %bitcast.30, bf16[32,192,8]{2,1,0:T(8,128)(2,1)} %bitcast.34, f32[192,9]{1,0:T(8,128)} %bitcast.39, f32[192,9]{1,0:T(8,128)} %bitcast.43), custom_call_target="tpu_custom_call" | custom-call | tf_op jit(solution)/shard_map/conv/pallas_call | solution.py:54
  121.5 6.3 %all-to-all-start.6 = ((bf16[8,192,360]{2,1,0:T(8,128)(2,1)}), bf16[8,192,360]{2,1,0:T(8,128)(2,1)S(1)}, u32[]{:S(2)}, u32[]{:S(2)}) async-start(bf16[8,192,360]{2,1,0:T(8,128)(2,1)} %conv.7), calls=%async_computation.6 | async-start | bytes 2359296 | tf_op jit(solution)/shard_map/all_to_all | solution.py:192
  127.8 1.1 constant_dynamic-update-slice_fusion.4
  128.9 1.1 constant_dynamic-update-slice_fusion.3
  130.0 1.1 constant_dynamic-update-slice_fusion.2
  131.1 1.1 constant_dynamic-update-slice_fusion.1
  132.2 0.0 collective-permute-done.5
  132.2 4.1 %constant_dynamic-update-slice_fusion = (bf16[8,384,768]{2,1,0:T(8,128)(2,1)}, bf16[16,384,768]{2,1,0:T(8,128)(2,1)}) fusion(bf16[8,384,768]{2,1,0:T(8,128)(2,1)} %get-tuple-element.11, bf16[4,384,768]{2,1,0:T(8,128)(2,1)} %collective-permute-done.5, bf16[16,384,768]{2,1,0:T(8,128)(2,1)} %get-tuple-element.12), kind=kLoop, calls=%fused_computation.3 | loop fusion | bytes 7077888 | tf_op jit(solution)/shard_map/concatenate | solution.py:167
  136.3 0.0 collective-permute-start.6
  136.3 9.5 %conv.6 = bf16[8,192,360]{2,1,0:T(8,128)(2,1)} custom-call(bf16[32,192,360]{2,1,0:T(8,128)(2,1)} %bitcast.19, bf16[32,192,8]{2,1,0:T(8,128)(2,1)} %bitcast.31, bf16[32,192,8]{2,1,0:T(8,128)(2,1)} %bitcast.35, f32[192,9]{1,0:T(8,128)} %bitcast.40, f32[192,9]{1,0:T(8,128)} %bitcast.44), custom_call_target="tpu_custom_call" | custom-call | tf_op jit(solution)/shard_map/conv/pallas_call | solution.py:54
  145.8 8.3 %all-to-all-done.6.x_ref = bf16[8,192,360]{2,1,0:T(8,128)(2,1)S(1)} async-done(((bf16[8,192,360]{2,1,0:T(8,128)(2,1)}), bf16[8,192,360]{2,1,0:T(8,128)(2,1)S(1)}, u32[]{:S(2)}, u32[]{:S(2)}) %all-to-all-start.6) | async-done | bytes 1105952 | tf_op jit(solution)/shard_map/all_to_all | solution.py:192
  154.1 5.2 %all-to-all-start.4 = ((bf16[8,192,360]{2,1,0:T(8,128)(2,1)}), bf16[8,192,360]{2,1,0:T(8,128)(2,1)S(1)}, u32[]{:S(2)}, u32[]{:S(2)}) async-start(bf16[8,192,360]{2,1,0:T(8,128)(2,1)} %conv.6), calls=%async_computation.4 | async-start | bytes 2359296 | tf_op jit(solution)/shard_map/all_to_all | solution.py:192
  159.4 9.5 %conv.5 = bf16[8,192,360]{2,1,0:T(8,128)(2,1)} custom-call(bf16[32,192,360]{2,1,0:T(8,128)(2,1)} %bitcast.20, bf16[32,192,8]{2,1,0:T(8,128)(2,1)} %bitcast.32, bf16[32,192,8]{2,1,0:T(8,128)(2,1)} %bitcast.36, f32[192,9]{1,0:T(8,128)} %bitcast.41, f32[192,9]{1,0:T(8,128)} %bitcast.45), custom_call_target="tpu_custom_call" | custom-call | tf_op jit(solution)/shard_map/conv/pallas_call | solution.py:54
  168.8 16.2 %all-to-all-done.4.x_ref = bf16[8,192,360]{2,1,0:T(8,128)(2,1)S(1)} async-done(((bf16[8,192,360]{2,1,0:T(8,128)(2,1)}), bf16[8,192,360]{2,1,0:T(8,128)(2,1)S(1)}, u32[]{:S(2)}, u32[]{:S(2)}) %all-to-all-start.4) | async-done | bytes 1105952 | tf_op jit(solution)/shard_map/all_to_all | solution.py:192
  185.0 5.9 %all-to-all-start.2 = ((bf16[8,192,360]{2,1,0:T(8,128)(2,1)}), bf16[8,192,360]{2,1,0:T(8,128)(2,1)S(1)}, u32[]{:S(2)}, u32[]{:S(2)}) async-start(bf16[8,192,360]{2,1,0:T(8,128)(2,1)} %conv.5), calls=%async_computation.2 | async-start | bytes 2359296 | tf_op jit(solution)/shard_map/all_to_all | solution.py:192
  190.9 9.3 %conv.4 = bf16[8,192,360]{2,1,0:T(8,128)(2,1)} custom-call(bf16[32,192,360]{2,1,0:T(8,128)(2,1)} %bitcast.21, bf16[32,192,8]{2,1,0:T(8,128)(2,1)} %bitcast.33, bf16[32,192,8]{2,1,0:T(8,128)(2,1)} %bitcast.37, f32[192,9]{1,0:T(8,128)} %bitcast.42, f32[192,9]{1,0:T(8,128)} %bitcast.46), custom_call_target="tpu_custom_call" | custom-call | tf_op jit(solution)/shard_map/conv/pallas_call | solution.py:54
  200.2 16.3 %all-to-all-done.2.x_ref = bf16[8,192,360]{2,1,0:T(8,128)(2,1)S(1)} async-done(((bf16[8,192,360]{2,1,0:T(8,128)(2,1)}), bf16[8,192,360]{2,1,0:T(8,128)(2,1)S(1)}, u32[]{:S(2)}, u32[]{:S(2)}) %all-to-all-start.2) | async-done | bytes 1105952 | tf_op jit(solution)/shard_map/all_to_all | solution.py:192
  216.5 5.9 %all-to-all-start = ((bf16[8,192,360]{2,1,0:T(8,128)(2,1)}), bf16[8,192,360]{2,1,0:T(8,128)(2,1)S(1)}, u32[]{:S(2)}, u32[]{:S(2)}) async-start(bf16[8,192,360]{2,1,0:T(8,128)(2,1)} %conv.4), calls=%async_computation | async-start | bytes 2359296 | tf_op jit(solution)/shard_map/all_to_all | solution.py:192
  222.4 0.9 broadcast_in_dim.11.gain_ref
  223.3 0.0 collective-permute-done.6
  223.3 4.8 %constant_dynamic-update-slice_fusion.5 = bf16[16,384,768]{2,1,0:T(8,128)(2,1)} fusion(bf16[16,384,768]{2,1,0:T(8,128)(2,1)} %get-tuple-element.10, bf16[8,384,768]{2,1,0:T(8,128)(2,1)} %collective-permute-done.6), kind=kLoop, calls=%fused_computation.8 | loop fusion | bytes 9437184 | tf_op jit(solution)/shard_map/concatenate | solution.py:167
  228.2 8.5 %fusion = (bf16[16,192,768]{2,1,0:T(8,128)(2,1)}, bf16[16,192,768]{2,1,0:T(8,128)(2,1)}) fusion(bf16[16,384,768]{2,1,0:T(8,128)(2,1)} %constant_dynamic-update-slice_fusion.5), kind=kLoop, calls=%fused_computation.14 | loop fusion | bytes 18874368 | tf_op jit(solution)/shard_map/slice | solution.py:183
  236.7 6.6 %copy.33 = bf16[3072,768]{0,1:T(8,128)(2,1)} copy(bf16[3072,768]{1,0:T(8,128)(2,1)} %bitcast.38) | data formatting | bytes 9437184 | tf_op jit(solution)/shard_map/reshape | solution.py:183
  243.3 13.0 %mlp.7 = bf16[8,192,360]{2,1,0:T(8,128)(2,1)} custom-call(bf16[8,192,360]{2,1,0:T(8,128)(2,1)} %copy-done.1, f32[768,1]{1,0:T(8,128)} %broadcast_in_dim.11.gain_ref, bf16[3072,768]{1,0:T(8,128)(2,1)} %bitcast.22, bf16[768,3072]{1,0:T(8,128)(2,1)} %bitcast.26), custom_call_target="tpu_custom_call" | custom-call | tf_op jit(solution)/shard_map/mlp/pallas_call | solution.py:110
  256.4 0.0 all-to-all-done.x_ref
  256.4 5.1 %all-to-all-start.7 = ((bf16[8,192,360]{2,1,0:T(8,128)(2,1)}), bf16[8,192,360]{2,1,0:T(8,128)(2,1)S(1)}, u32[]{:S(2)}, u32[]{:S(2)}) async-start(bf16[8,192,360]{2,1,0:T(8,128)(2,1)} %mlp.7), calls=%async_computation.7 | async-start | bytes 2359296 | tf_op jit(solution)/shard_map/all_to_all | solution.py:197
  261.5 13.0 %mlp.6 = bf16[8,192,360]{2,1,0:T(8,128)(2,1)} custom-call(bf16[8,192,360]{2,1,0:T(8,128)(2,1)} %copy-done.3, f32[768,1]{1,0:T(8,128)} %broadcast_in_dim.11.gain_ref, bf16[3072,768]{1,0:T(8,128)(2,1)} %bitcast.23, bf16[768,3072]{1,0:T(8,128)(2,1)} %bitcast.27), custom_call_target="tpu_custom_call" | custom-call | tf_op jit(solution)/shard_map/mlp/pallas_call | solution.py:110
  274.5 12.1 %all-to-all-done.7.update_ref = bf16[8,192,360]{2,1,0:T(8,128)(2,1)S(1)} async-done(((bf16[8,192,360]{2,1,0:T(8,128)(2,1)}), bf16[8,192,360]{2,1,0:T(8,128)(2,1)S(1)}, u32[]{:S(2)}, u32[]{:S(2)}) %all-to-all-start.7) | async-done | bytes 1105952 | tf_op jit(solution)/shard_map/all_to_all | solution.py:197
  286.6 5.9 %all-to-all-start.5 = ((bf16[8,192,360]{2,1,0:T(8,128)(2,1)}), bf16[8,192,360]{2,1,0:T(8,128)(2,1)S(1)}, u32[]{:S(2)}, u32[]{:S(2)}) async-start(bf16[8,192,360]{2,1,0:T(8,128)(2,1)} %mlp.6), calls=%async_computation.5 | async-start | bytes 2359296 | tf_op jit(solution)/shard_map/all_to_all | solution.py:197
  292.4 13.1 %mlp.5 = bf16[8,192,360]{2,1,0:T(8,128)(2,1)} custom-call(bf16[8,192,360]{2,1,0:T(8,128)(2,1)} %copy-done.2, f32[768,1]{1,0:T(8,128)} %broadcast_in_dim.11.gain_ref, bf16[3072,768]{1,0:T(8,128)(2,1)} %bitcast.24, bf16[768,3072]{1,0:T(8,128)(2,1)} %bitcast.28), custom_call_target="tpu_custom_call" | custom-call | tf_op jit(solution)/shard_map/mlp/pallas_call | solution.py:110
  305.5 12.6 %all-to-all-done.5.update_ref = bf16[8,192,360]{2,1,0:T(8,128)(2,1)S(1)} async-done(((bf16[8,192,360]{2,1,0:T(8,128)(2,1)}), bf16[8,192,360]{2,1,0:T(8,128)(2,1)S(1)}, u32[]{:S(2)}, u32[]{:S(2)}) %all-to-all-start.5) | async-done | bytes 1105952 | tf_op jit(solution)/shard_map/all_to_all | solution.py:197
  318.1 5.9 %all-to-all-start.3 = ((bf16[8,192,360]{2,1,0:T(8,128)(2,1)}), bf16[8,192,360]{2,1,0:T(8,128)(2,1)S(1)}, u32[]{:S(2)}, u32[]{:S(2)}) async-start(bf16[8,192,360]{2,1,0:T(8,128)(2,1)} %mlp.5), calls=%async_computation.3 | async-start | bytes 2359296 | tf_op jit(solution)/shard_map/all_to_all | solution.py:197
  324.0 13.0 %mlp.4 = bf16[8,192,360]{2,1,0:T(8,128)(2,1)} custom-call(bf16[8,192,360]{2,1,0:T(8,128)(2,1)} %copy-done.4, f32[768,1]{1,0:T(8,128)} %broadcast_in_dim.11.gain_ref, bf16[3072,768]{1,0:T(8,128)(2,1)} %bitcast.25, bf16[768,3072]{1,0:T(8,128)(2,1)} %bitcast.29), custom_call_target="tpu_custom_call" | custom-call | tf_op jit(solution)/shard_map/mlp/pallas_call | solution.py:110
  336.9 12.7 %all-to-all-done.3.update_ref = bf16[8,192,360]{2,1,0:T(8,128)(2,1)S(1)} async-done(((bf16[8,192,360]{2,1,0:T(8,128)(2,1)}), bf16[8,192,360]{2,1,0:T(8,128)(2,1)S(1)}, u32[]{:S(2)}, u32[]{:S(2)}) %all-to-all-start.3) | async-done | bytes 1105952 | tf_op jit(solution)/shard_map/all_to_all | solution.py:197
  349.6 5.9 %all-to-all-start.1 = ((bf16[8,192,360]{2,1,0:T(8,128)(2,1)}), bf16[8,192,360]{2,1,0:T(8,128)(2,1)S(1)}, u32[]{:S(2)}, u32[]{:S(2)}) async-start(bf16[8,192,360]{2,1,0:T(8,128)(2,1)} %mlp.4), calls=%async_computation.1 | async-start | bytes 2359296 | tf_op jit(solution)/shard_map/all_to_all | solution.py:197
  355.5 5.0 %add.4.rest_0_ = bf16[192,32,360]{2,1,0:T(8,128)(2,1)} custom-call(bf16[8,192,360]{2,1,0:T(8,128)(2,1)} %copy-done.5, bf16[192,32,360]{2,1,0:T(8,128)(2,1)} %field_ref.7), custom_call_target="tpu_custom_call" | custom-call | tf_op jit(solution)/shard_map/add/pallas_call | solution.py:146
  360.5 5.0 %add.5.rest_0_ = bf16[192,32,360]{2,1,0:T(8,128)(2,1)} custom-call(bf16[8,192,360]{2,1,0:T(8,128)(2,1)} %copy-done.6, bf16[192,32,360]{2,1,0:T(8,128)(2,1)} %field_ref.7, bf16[192,32,360]{2,1,0:T(8,128)(2,1)} %add.4.rest_0_), custom_call_target="tpu_custom_call", output_to_operand_aliasing={{}: (2, {})} | custom-call | tf_op jit(solution)/shard_map/add/pallas_call | solution.py:146
  365.5 5.0 %add.6.rest_0_ = bf16[192,32,360]{2,1,0:T(8,128)(2,1)} custom-call(bf16[8,192,360]{2,1,0:T(8,128)(2,1)} %copy-done.7, bf16[192,32,360]{2,1,0:T(8,128)(2,1)} %field_ref.7, bf16[192,32,360]{2,1,0:T(8,128)(2,1)} %add.5.rest_0_), custom_call_target="tpu_custom_call", output_to_operand_aliasing={{}: (2, {})} | custom-call | tf_op jit(solution)/shard_map/add/pallas_call | solution.py:146
  370.4 10.7 %all-to-all-done.1.update_ref = bf16[8,192,360]{2,1,0:T(8,128)(2,1)S(1)} async-done(((bf16[8,192,360]{2,1,0:T(8,128)(2,1)}), bf16[8,192,360]{2,1,0:T(8,128)(2,1)S(1)}, u32[]{:S(2)}, u32[]{:S(2)}) %all-to-all-start.1) | async-done | bytes 1105952 | tf_op jit(solution)/shard_map/all_to_all | solution.py:197
  381.2 1.1 copy-done.8
  382.2 5.0 %add.7 = bf16[192,32,360]{2,1,0:T(8,128)(2,1)} custom-call(bf16[8,192,360]{2,1,0:T(8,128)(2,1)} %copy-done.8, bf16[192,32,360]{2,1,0:T(8,128)(2,1)} %field_ref.7, bf16[192,32,360]{2,1,0:T(8,128)(2,1)} %add.6.rest_0_), custom_call_target="tpu_custom_call", output_to_operand_aliasing={{}: (2, {})} | custom-call | tf_op jit(solution)/shard_map/add/pallas_call | solution.py:146
  (37 shorter events, 0.1 us)
Async XLA Ops:
  0.0 57.5 %copy-start = (bf16[192,32,360]{2,1,0:T(8,128)(2,1)S(1)}, bf16[192,32,360]{2,1,0:T(8,128)(2,1)}, u32[]{:S(2)}) copy-start(bf16[192,32,360]{2,1,0:T(8,128)(2,1)} %field_ref.7) | copy-start | bytes 13271044
  1.2 15.5 %collective-permute-start.2 = (bf16[1,384,768]{2,1,0:T(8,128)(2,1)S(1)}, bf16[1,384,768]{2,1,0:T(8,128)(2,1)S(1)}, u32[]{:S(2)}, u32[]{:S(2)}) collective-permute-start(bf16[1,384,768]{2,1,0:T(8,128)(2,1)S(1)} %maximum_bitcast_fusion), channel_id=1, source_target_pairs={{0,1},{1,2},{2,3},{3,0},{4,5},{5,6},{6,7},{7,4},{8,9},{9,10},{10,1... | collective-permute-start | bytes 1769480 | tf_op jit(solution)/shard_map/ppermute | solution.py:162
  1.3 52.9 %collective-permute-start.3 = (bf16[1,384,768]{2,1,0:T(8,128)(2,1)S(1)}, bf16[1,384,768]{2,1,0:T(8,128)(2,1)S(1)}, u32[]{:S(2)}, u32[]{:S(2)}) collective-permute-start(bf16[1,384,768]{2,1,0:T(8,128)(2,1)S(1)} %maximum_bitcast_fusion), channel_id=1, source_target_pairs={{0,2},{1,3},{2,0},{3,1},{4,6},{5,7},{6,4},{7,5},{8,10},{9,11},{10,... | collective-permute-start | bytes 1769480 | tf_op jit(solution)/shard_map/ppermute | solution.py:162
  3.2 51.0 %collective-permute-start.4 = (bf16[1,384,768]{2,1,0:T(8,128)(2,1)S(1)}, bf16[1,384,768]{2,1,0:T(8,128)(2,1)S(1)}, u32[]{:S(2)}, u32[]{:S(2)}) collective-permute-start(bf16[1,384,768]{2,1,0:T(8,128)(2,1)S(1)} %maximum_bitcast_fusion), channel_id=1, source_target_pairs={{0,3},{1,0},{2,1},{3,2},{4,7},{5,4},{6,5},{7,6},{8,11},{9,8},{10,9... | collective-permute-start | bytes 1769480 | tf_op jit(solution)/shard_map/ppermute | solution.py:162
  16.8 41.5 %copy-start.13 = (bf16[1,384,768]{2,1,0:T(8,128)(2,1)}, bf16[1,384,768]{2,1,0:T(8,128)(2,1)S(1)}, u32[]{:S(2)}) copy-start(bf16[1,384,768]{2,1,0:T(8,128)(2,1)S(1)} %collective-permute-done.2) | copy-start | bytes 1769476
  54.2 1.8 copy-start.11
  54.2 1.8 copy-start.9
  56.0 76.2 %collective-permute-start.5 = (bf16[4,384,768]{2,1,0:T(8,128)(2,1)}, bf16[4,384,768]{2,1,0:T(8,128)(2,1)}, u32[]{:S(2)}, u32[]{:S(2)}) collective-permute-start(bf16[4,384,768]{2,1,0:T(8,128)(2,1)} %pad_maximum_fusion), channel_id=1, source_target_pairs={{0,8},{4,12},{8,0},{12,4},{1,9},{5,13},{9,1},{13,5},{2,10},{6,14},... | collective-permute-start | bytes 7077896 | tf_op jit(solution)/shard_map/ppermute | solution.py:167
  59.5 49.5 %collective-permute-start = (bf16[192,32,8]{0,2,1:T(8,128)(2,1)S(1)}, bf16[192,32,8]{0,2,1:T(8,128)(2,1)S(1)}, u32[]{:S(2)}, u32[]{:S(2)}) collective-permute-start(bf16[192,32,8]{0,2,1:T(8,128)(2,1)S(1)} %copy.38), channel_id=1, source_target_pairs={{0,4},{4,8},{8,12},{12,0},{1,5},{5,9},{9,13},{13,1},{2,6},{6,10},{... | collective-permute-start | bytes 294920 | tf_op jit(solution)/shard_map/ppermute | solution.py:178
  60.9 8.0 %copy-start.17 = (f32[9,192]{1,0:T(8,128)S(1)}, f32[9,192]{1,0:T(8,128)}, u32[]{:S(2)}) copy-start(f32[9,192]{1,0:T(8,128)} %param.7) | copy-start | bytes 20740
  60.9 8.8 %copy-start.18 = (f32[9,192]{1,0:T(8,128)S(1)}, f32[9,192]{1,0:T(8,128)}, u32[]{:S(2)}) copy-start(f32[9,192]{1,0:T(8,128)} %param.8) | copy-start | bytes 20740
  60.9 49.7 %collective-permute-start.1 = (bf16[192,32,8]{0,2,1:T(8,128)(2,1)S(1)}, bf16[192,32,8]{0,2,1:T(8,128)(2,1)S(1)}, u32[]{:S(2)}, u32[]{:S(2)}) collective-permute-start(bf16[192,32,8]{0,2,1:T(8,128)(2,1)S(1)} %copy.39), channel_id=1, source_target_pairs={{4,0},{8,4},{12,8},{0,12},{5,1},{9,5},{13,9},{1,13},{6,2},{10,6},{... | collective-permute-start | bytes 294920 | tf_op jit(solution)/shard_map/ppermute | solution.py:179
  112.1 15.7 %copy-start.15 = (bf16[768,192]{0,1:T(8,128)(2,1)S(1)}, bf16[768,192]{0,1:T(8,128)(2,1)}, u32[]{:S(2)}) copy-start(bf16[768,192]{0,1:T(8,128)(2,1)} %param.11) | copy-start | bytes 884740
  112.1 15.7 %copy-start.16 = (bf16[768,192]{0,1:T(8,128)(2,1)S(1)}, bf16[768,192]{0,1:T(8,128)(2,1)}, u32[]{:S(2)}) copy-start(bf16[768,192]{0,1:T(8,128)(2,1)} %param.10) | copy-start | bytes 884740
  112.1 16.8 %copy-start.14 = (bf16[1,384,768]{2,1,0:T(8,128)(2,1)S(1)}, bf16[1,384,768]{2,1,0:T(8,128)(2,1)}, u32[]{:S(2)}) copy-start(bf16[1,384,768]{2,1,0:T(8,128)(2,1)} %copy-done.13) | copy-start | bytes 1769476
  121.5 8.5 %copy-start.12 = (bf16[1,384,768]{2,1,0:T(8,128)(2,1)S(1)}, bf16[1,384,768]{2,1,0:T(8,128)(2,1)}, u32[]{:S(2)}) copy-start(bf16[1,384,768]{2,1,0:T(8,128)(2,1)} %copy-done.11) | copy-start | bytes 1769476
  121.5 9.6 %copy-start.10 = (bf16[1,384,768]{2,1,0:T(8,128)(2,1)S(1)}, bf16[1,384,768]{2,1,0:T(8,128)(2,1)}, u32[]{:S(2)}) copy-start(bf16[1,384,768]{2,1,0:T(8,128)(2,1)} %copy-done.9) | copy-start | bytes 1769476
  121.5 32.6 %all-to-all-start.6 = ((bf16[8,192,360]{2,1,0:T(8,128)(2,1)}), bf16[8,192,360]{2,1,0:T(8,128)(2,1)S(1)}, u32[]{:S(2)}, u32[]{:S(2)}) async-start(bf16[8,192,360]{2,1,0:T(8,128)(2,1)} %conv.7), calls=%async_computation.6 | async-start | bytes 2359296 | tf_op jit(solution)/shard_map/all_to_all | solution.py:192
  136.3 87.0 %collective-permute-start.6 = (bf16[8,384,768]{2,1,0:T(8,128)(2,1)}, bf16[8,384,768]{2,1,0:T(8,128)(2,1)}, u32[]{:S(2)}, u32[]{:S(2)}) collective-permute-start(bf16[8,384,768]{2,1,0:T(8,128)(2,1)} %get-tuple-element.9), channel_id=1, source_target_pairs={{0,4},{4,0},{8,12},{12,8},{1,5},{5,1},{9,13},{13,9},{2,6},{6,2},{1... | collective-permute-start | bytes 14155784 | tf_op jit(solution)/shard_map/ppermute | solution.py:167
  154.1 14.7 %copy-start.1 = (bf16[8,192,360]{2,1,0:T(8,128)(2,1)}, bf16[8,192,360]{2,1,0:T(8,128)(2,1)S(1)}, u32[]{:S(2)}) copy-start(bf16[8,192,360]{2,1,0:T(8,128)(2,1)S(1)} %all-to-all-done.6.x_ref) | copy-start | bytes 3317764
  154.1 30.9 %all-to-all-start.4 = ((bf16[8,192,360]{2,1,0:T(8,128)(2,1)}), bf16[8,192,360]{2,1,0:T(8,128)(2,1)S(1)}, u32[]{:S(2)}, u32[]{:S(2)}) async-start(bf16[8,192,360]{2,1,0:T(8,128)(2,1)} %conv.6), calls=%async_computation.4 | async-start | bytes 2359296 | tf_op jit(solution)/shard_map/all_to_all | solution.py:192
  185.0 15.2 %copy-start.3 = (bf16[8,192,360]{2,1,0:T(8,128)(2,1)}, bf16[8,192,360]{2,1,0:T(8,128)(2,1)S(1)}, u32[]{:S(2)}) copy-start(bf16[8,192,360]{2,1,0:T(8,128)(2,1)S(1)} %all-to-all-done.4.x_ref) | copy-start | bytes 3317764
  185.0 31.5 %all-to-all-start.2 = ((bf16[8,192,360]{2,1,0:T(8,128)(2,1)}), bf16[8,192,360]{2,1,0:T(8,128)(2,1)S(1)}, u32[]{:S(2)}, u32[]{:S(2)}) async-start(bf16[8,192,360]{2,1,0:T(8,128)(2,1)} %conv.5), calls=%async_computation.2 | async-start | bytes 2359296 | tf_op jit(solution)/shard_map/all_to_all | solution.py:192
  190.9 31.5 %copy-start.19 = (f32[768]{0:T(1024)S(1)}, f32[768]{0:T(1024)}, u32[]{:S(2)}) copy-start(f32[768]{0:T(1024)} %param.9) | copy-start | bytes 9220
  216.5 11.6 %copy-start.2 = (bf16[8,192,360]{2,1,0:T(8,128)(2,1)}, bf16[8,192,360]{2,1,0:T(8,128)(2,1)S(1)}, u32[]{:S(2)}) copy-start(bf16[8,192,360]{2,1,0:T(8,128)(2,1)S(1)} %all-to-all-done.2.x_ref) | copy-start | bytes 3317764
  216.5 39.8 %all-to-all-start = ((bf16[8,192,360]{2,1,0:T(8,128)(2,1)}), bf16[8,192,360]{2,1,0:T(8,128)(2,1)S(1)}, u32[]{:S(2)}, u32[]{:S(2)}) async-start(bf16[8,192,360]{2,1,0:T(8,128)(2,1)} %conv.4), calls=%async_computation | async-start | bytes 2359296 | tf_op jit(solution)/shard_map/all_to_all | solution.py:192
  256.4 18.1 %copy-start.4 = (bf16[8,192,360]{2,1,0:T(8,128)(2,1)}, bf16[8,192,360]{2,1,0:T(8,128)(2,1)S(1)}, u32[]{:S(2)}) copy-start(bf16[8,192,360]{2,1,0:T(8,128)(2,1)S(1)} %all-to-all-done.x_ref) | copy-start | bytes 3317764
  256.4 30.2 %all-to-all-start.7 = ((bf16[8,192,360]{2,1,0:T(8,128)(2,1)}), bf16[8,192,360]{2,1,0:T(8,128)(2,1)S(1)}, u32[]{:S(2)}, u32[]{:S(2)}) async-start(bf16[8,192,360]{2,1,0:T(8,128)(2,1)} %mlp.7), calls=%async_computation.7 | async-start | bytes 2359296 | tf_op jit(solution)/shard_map/all_to_all | solution.py:197
  286.6 19.0 %copy-start.5 = (bf16[8,192,360]{2,1,0:T(8,128)(2,1)}, bf16[8,192,360]{2,1,0:T(8,128)(2,1)S(1)}, u32[]{:S(2)}) copy-start(bf16[8,192,360]{2,1,0:T(8,128)(2,1)S(1)} %all-to-all-done.7.update_ref) | copy-start | bytes 3317764
  286.6 31.5 %all-to-all-start.5 = ((bf16[8,192,360]{2,1,0:T(8,128)(2,1)}), bf16[8,192,360]{2,1,0:T(8,128)(2,1)S(1)}, u32[]{:S(2)}, u32[]{:S(2)}) async-start(bf16[8,192,360]{2,1,0:T(8,128)(2,1)} %mlp.6), calls=%async_computation.5 | async-start | bytes 2359296 | tf_op jit(solution)/shard_map/all_to_all | solution.py:197
  318.1 18.8 %copy-start.6 = (bf16[8,192,360]{2,1,0:T(8,128)(2,1)}, bf16[8,192,360]{2,1,0:T(8,128)(2,1)S(1)}, u32[]{:S(2)}) copy-start(bf16[8,192,360]{2,1,0:T(8,128)(2,1)S(1)} %all-to-all-done.5.update_ref) | copy-start | bytes 3317764
  318.1 31.5 %all-to-all-start.3 = ((bf16[8,192,360]{2,1,0:T(8,128)(2,1)}), bf16[8,192,360]{2,1,0:T(8,128)(2,1)S(1)}, u32[]{:S(2)}, u32[]{:S(2)}) async-start(bf16[8,192,360]{2,1,0:T(8,128)(2,1)} %mlp.5), calls=%async_computation.3 | async-start | bytes 2359296 | tf_op jit(solution)/shard_map/all_to_all | solution.py:197
  349.6 10.8 %copy-start.7 = (bf16[8,192,360]{2,1,0:T(8,128)(2,1)}, bf16[8,192,360]{2,1,0:T(8,128)(2,1)S(1)}, u32[]{:S(2)}) copy-start(bf16[8,192,360]{2,1,0:T(8,128)(2,1)S(1)} %all-to-all-done.3.update_ref) | copy-start | bytes 3317764
  349.6 31.5 %all-to-all-start.1 = ((bf16[8,192,360]{2,1,0:T(8,128)(2,1)}), bf16[8,192,360]{2,1,0:T(8,128)(2,1)S(1)}, u32[]{:S(2)}, u32[]{:S(2)}) async-start(bf16[8,192,360]{2,1,0:T(8,128)(2,1)} %mlp.4), calls=%async_computation.1 | async-start | bytes 2359296 | tf_op jit(solution)/shard_map/all_to_all | solution.py:197
  381.2 1.1 copy-start.8

commit v2 on v0

v2 whole, which is shorter than its diff:
```python
import functools

import jax
import jax.numpy as jnp
from jax import lax
from jax.experimental import pallas as pl
from jax.experimental.pallas import tpu as pltpu
from jax.sharding import PartitionSpec as P

KERNEL_TAPS = 9
DILATION_STEP = 2
BORDER = DILATION_STEP * (KERNEL_TAPS // 2)
LANES = 128
SUBLANES = 8
CHUNKS = 4
PARAMS = pltpu.CompilerParams(vmem_limit_bytes=60 * 1024 * 1024)


def microseconds(count):
    return pl.CostEstimate(flops=int(count * 1.15e8), bytes_accessed=1024, transcendentals=0)


def round_up(value, step):
    return -(-value // step) * step


class Packing:
    def __init__(self, chan_count, cells):
        self.block = 64 if chan_count % 64 == 0 else 32
        self.blocks = chan_count // self.block
        unit = LANES * SUBLANES // self.block
        used = round_up(cells, unit)
        self.full = used // LANES
        self.groups = []
        row, offset, size = self.full * self.block, 0, LANES // 2
        while size >= unit:
            if used % LANES & size:
                self.groups.append((row, offset, size))
                row += self.block * size // LANES
                offset += size
            size //= 2
        self.rows = row
        self.wide = round_up(cells, LANES)

    def store(self, ref, lead, load):
        for i in range(self.full):
            ref[lead, i * self.block : (i + 1) * self.block, :] = load(i).astype(ref.dtype)
        if not self.groups:
            return
        tail = load(self.full)
        for row, offset, size in self.groups:
            count = self.block * size // LANES
            lane = lax.broadcasted_iota(jnp.int32, (count, LANES), 1)
            packed = None
            for g in range(LANES // size):
                piece = tail[g * count : (g + 1) * count]
                if (g * size - offset) % LANES:
                    piece = pltpu.roll(piece, (g * size - offset) % LANES, 1)
                packed = piece if packed is None else jnp.where(lane >= g * size, piece, packed)
            ref[lead, row : row + count, :] = packed.astype(ref.dtype)

    def load(self, ref, lead, store):
        for i in range(self.full):
            store(i, ref[lead, i * self.block : (i + 1) * self.block, :].astype(jnp.float32))
        if not self.groups:
            return
        lane = lax.broadcasted_iota(jnp.int32, (self.block, LANES), 1)
        tail = None
        for row, offset, size in self.groups:
            count = self.block * size // LANES
            packed = ref[lead, row : row + count, :].astype(jnp.float32)
            pieces = []
            for g in range(LANES // size):
                turn = (offset - g * size) % LANES
                pieces.append(pltpu.roll(packed, turn, 1) if turn else packed)
            whole = jnp.concatenate(pieces, axis=0)
            tail = whole if tail is None else jnp.where(lane >= offset, whole, tail)
        store(self.full, tail)


def conv_kernel(packing, sources, rows, first_row, low, me_ref, *refs):
    field_refs, (lon_ref, lat_ref), out_refs = refs[: -sources - 4], refs[-sources - 4 : -sources - 2], refs[-sources - 2 : -2]
    base_ref, cells_ref = refs[-2:]
    width = field_refs[0].shape[2]
    held_rows, block, wide = base_ref.shape
    group = field_refs[0].shape[0]
    for held in range(held_rows):
        field_ref, before_ref, after_ref = field_refs[held // group * 3 : held // group * 3 + 3]
        row = held % group
        base_ref[held, :, 0:width] = field_ref[row].astype(jnp.float32)
        base_ref[held, :, width : width + BORDER] = after_ref[row].astype(jnp.float32)
        base_ref[held, :, wide - BORDER : wide] = before_ref[row].astype(jnp.float32)
    me = me_ref[0]
    part = 16

    def some_channels(index, _):
        chans = pl.ds(pl.multiple_of(index * part, part), part)
        lon = [jnp.broadcast_to(lon_ref[chans, t : t + 1], (part, wide)) for t in range(KERNEL_TAPS)]
        lat = [jnp.broadcast_to(lat_ref[chans, t : t + 1], (part, wide)) for t in range(KERNEL_TAPS)]
        for out_row in range(sources * rows):
            total = None
            for t in range(KERNEL_TAPS):
                held = first_row + out_row + DILATION_STEP * (t - KERNEL_TAPS // 2) - low
                if 0 <= held < held_rows:
                    term = lat[t] * base_ref[held, chans, :]
                    total = term if total is None else total + term
            result = lon[KERNEL_TAPS // 2] * total
            for t in range(KERNEL_TAPS):
                turn = DILATION_STEP * (KERNEL_TAPS // 2 - t)
                if turn:
                    result = result + lon[t] * pltpu.roll(total, turn % wide, 1)
            receiver, row = divmod(out_row, rows)
            shift = lax.rem(receiver + sources - me, sources)
            cells_ref[shift, chans, row * width : (row + 1) * width] = result[:, 0:width]
        return 0

    lax.fori_loop(0, block // part, some_channels, 0)
    for shift in range(sources):
        packing.store(out_refs[shift], 0, lambda i: cells_ref[shift, :, i * LANES : (i + 1) * LANES])


def convolve(packing, me, sources, field, before, after, lon_taps, lat_taps, place, row_count):
    row_total, chan_count, width = field.shape
    block = packing.block
    wide = round_up(width + 2 * BORDER, LANES)
    piece = jax.ShapeDtypeStruct((packing.blocks, packing.rows, LANES), jnp.bfloat16)
    reach = -(-BORDER // row_count)
    places = range(max(0, place - reach), min(row_total // row_count, place + reach + 1))
    specs, operands = [], []
    for near in places:
        for array in (field, before, after):
            specs.append(pl.BlockSpec((row_count, block, array.shape[2]), lambda c, me, near=near: (near, c, 0)))
            operands.append(array)
    taps = pl.BlockSpec((block, KERNEL_TAPS), lambda c, me: (c, 0))
    return pl.pallas_call(
        functools.partial(
            conv_kernel, packing, sources, row_count // sources, place * row_count, places[0] * row_count
        ),
        grid_spec=pltpu.PrefetchScalarGridSpec(
            num_scalar_prefetch=1,
            grid=(packing.blocks,),
            in_specs=[*specs, taps, taps],
            out_specs=[pl.BlockSpec((1, packing.rows, LANES), lambda c, me: (c, 0, 0))] * sources,
            scratch_shapes=[
                pltpu.VMEM((len(places) * row_count, block, wide), jnp.float32),
                pltpu.VMEM((sources, block, packing.wide), jnp.float32),
            ],
        ),
        out_shape=[piece] * sources,
        compiler_params=PARAMS,
        cost_estimate=microseconds(12),
        name="conv",
    )(me, *operands, lon_taps, lat_taps)


def mlp_kernel(packing, sources, me_ref, *refs):
    x_refs, (gain_ref, up_ref, down_ref) = refs[:sources], refs[sources : sources + 3]
    out_refs, (values, normed, total) = refs[sources + 3 : -3], refs[-3:]
    step = pl.program_id(0)
    me = me_ref[0]
    block = packing.block
    chan_count = packing.blocks * block

    def channels(owner, lead):
        return pl.ds(pl.multiple_of(owner * chan_count + lead * block, SUBLANES), block)

    @pl.when(step == 0)
    def _():
        for shift in range(sources):
            sender = lax.rem(me + sources - shift, sources)
            for lead in range(packing.blocks):

                def put(i, piece, at=channels(sender, lead)):
                    values[at, i * LANES : (i + 1) * LANES] = piece

                packing.load(x_refs[shift], lead, put)
        as_float = values[...]
        center = jnp.mean(as_float, axis=0, keepdims=True)
        deviation = as_float - center
        spread_sq = jnp.mean(deviation * deviation, axis=0, keepdims=True)
        normed[...] = (deviation * lax.rsqrt(spread_sq + 1e-06) * gain_ref[...]).astype(jnp.bfloat16)
        total[...] = jnp.zeros_like(total)

    expanded = jnp.dot(up_ref[...], normed[...], preferred_element_type=jnp.float32)
    hidden = (0.5 * expanded * (1.0 + lax.erf(expanded * 0.7071067811865476))).astype(jnp.bfloat16)
    total[...] += jnp.dot(down_ref[...], hidden, preferred_element_type=jnp.float32)

    @pl.when(step == pl.num_programs(0) - 1)
    def _():
        for shift in range(sources):
            owner = lax.rem(me + shift, sources)
            for lead in range(packing.blocks):
                at = channels(owner, lead)
                packing.store(out_refs[shift], lead, lambda i: total[at, i * LANES : (i + 1) * LANES])


def mlp(packing, me, pieces, gain, up_all, down_all):
    sources = len(pieces)
    width_all, hidden_total = down_all.shape
    block = 512
    whole = pl.BlockSpec(pieces[0].shape, lambda h, me: (0, 0, 0))
    return pl.pallas_call(
        functools.partial(mlp_kernel, packing, sources),
        grid_spec=pltpu.PrefetchScalarGridSpec(
            num_scalar_prefetch=1,
            grid=(hidden_total // block,),
            in_specs=[whole] * sources
            + [
                pl.BlockSpec((width_all, 1), lambda h, me: (0, 0)),
                pl.BlockSpec((block, width_all), lambda h, me: (h, 0)),
                pl.BlockSpec((width_all, block), lambda h, me: (0, h)),
            ],
            out_specs=[whole] * sources,
            scratch_shapes=[
                pltpu.VMEM((width_all, packing.wide), jnp.float32),
                pltpu.VMEM((width_all, packing.wide), jnp.bfloat16),
                pltpu.VMEM((width_all, packing.wide), jnp.float32),
            ],
        ),
        out_shape=[jax.ShapeDtypeStruct(pieces[0].shape, jnp.bfloat16)] * sources,
        compiler_params=PARAMS,
        cost_estimate=microseconds(13),
        name="mlp",
    )(me, *pieces, gain, up_all, down_all)


def add_kernel(packing, sources, me_ref, *refs):
    piece_refs, field_ref = refs[:sources], refs[sources]
    out_ref, cells_ref, update_ref = refs[-3:]
    me = me_ref[0]
    rows = update_ref.shape[0] // sources
    width = field_ref.shape[2]
    for shift in range(sources):
        sender = lax.rem(me + sources - shift, sources)

        def put(i, piece):
            cells_ref[:, i * LANES : (i + 1) * LANES] = piece

        packing.load(piece_refs[shift], 0, put)
        for row in range(rows):
            update_ref[sender * rows + row] = cells_ref[:, row * width : (row + 1) * width]
    update = jnp.transpose(update_ref[...], (1, 0, 2))
    out_ref[...] = (field_ref[...].astype(jnp.float32) + update).astype(out_ref.dtype)


def add_rows(packing, me, pieces, field, done, place, row_count):
    sources = len(pieces)
    width = field.shape[2]
    block = packing.block
    rows_of = pl.BlockSpec((block, row_count, width), lambda c, me: (c, place, 0))
    specs = [pl.BlockSpec((1, packing.rows, LANES), lambda c, me: (c, 0, 0))] * sources + [rows_of]
    operands = [me, *pieces, field]
    if done is not None:
        specs.append(pl.BlockSpec(memory_space=pl.ANY))
        operands.append(done)
    return pl.pallas_call(
        functools.partial(add_kernel, packing, sources),
        grid_spec=pltpu.PrefetchScalarGridSpec(
            num_scalar_prefetch=1,
            grid=(packing.blocks,),
            in_specs=specs,
            out_specs=rows_of,
            scratch_shapes=[
                pltpu.VMEM((block, packing.wide), jnp.float32),
                pltpu.VMEM((row_count, block, width), jnp.float32),
            ],
        ),
        out_shape=jax.ShapeDtypeStruct(field.shape, jnp.bfloat16),
        input_output_aliases={len(operands) - 1: 0} if done is not None else {},
        compiler_params=PARAMS,
        cost_estimate=microseconds(4),
        name="add",
    )(*operands)


def prepare_kernel(held_ref, received_ref, *refs):
    up_ref, down_ref = refs[-2:]
    half = held_ref.shape[1] // 2
    up_ref[0:half] = held_ref[0, 0:half]
    up_ref[half:] = received_ref[0, 0:half]
    down_ref[:, 0:half] = held_ref[0, half:].T
    down_ref[:, half:] = received_ref[0, half:].T


def prepare(held, received, total, done, place):
    count, rows, width = held.shape
    if rows % LANES:
        both = jnp.concatenate([held, received], axis=0)
        half = rows // 2
        return both[:, :half].reshape(total, width), both[:, half:].reshape(total, width).T
    source = pl.BlockSpec((1, rows, width), lambda i: (i, 0, 0))
    return pl.pallas_call(
        prepare_kernel,
        grid=(count,),
        in_specs=[source, source] + [pl.BlockSpec(memory_space=pl.ANY)] * len(done),
        out_specs=[
            pl.BlockSpec((rows, width), lambda i: (place + i, 0)),
            pl.BlockSpec((width, rows), lambda i: (0, place + i)),
        ],
        out_shape=[
            jax.ShapeDtypeStruct((total, width), held.dtype),
            jax.ShapeDtypeStruct((width, total), held.dtype),
        ],
        input_output_aliases={2: 0, 3: 1} if done else {},
        compiler_params=PARAMS,
        cost_estimate=microseconds(count),
        name="prepare",
    )(held, received, *done)


def shifted(array, axis, shift):
    count = lax.axis_size(axis)
    return lax.ppermute(array, axis, [(i, (i + shift) % count) for i in range(count)])


def exchanged(array, axis, bit):
    return lax.ppermute(array, axis, [(i, i ^ bit) for i in range(lax.axis_size(axis))])


def after_all(arrays, *others):
    return lax.optimization_barrier((arrays, others))[0]


def on_device(weather, lon_taps, latitude_taps, norm_gain, up_weight, down_weight):
    chan_count, row_total, width = weather.shape
    sources, tiles = lax.axis_size("chan"), lax.axis_size("tile")
    me = lax.axis_index("chan").astype(jnp.int32)[None]
    with jax.named_scope("halo"):
        before = shifted(weather[:, :, width - BORDER :], "tile", 1)
        after = shifted(weather[:, :, :BORDER], "tile", tiles - 1)
    shard = jnp.concatenate([up_weight.T, down_weight.T], axis=0)[None]
    with jax.named_scope("wz"):
        far = [shard]
        bit = sources // 2
        while bit > 1:
            far = far + [exchanged(piece, "chan", bit) for piece in far]
            bit //= 2
        near = exchanged(shard, "chan", 1)
    bits = []
    bit = tiles // 2
    while bit > 1:
        bits.append(bit)
        bit //= 2
    with jax.named_scope("wx0"):
        across = exchanged(shard, "tile", bits[0])
    field = jnp.transpose(weather, (1, 0, 2))
    before = jnp.transpose(before, (1, 0, 2))
    after = jnp.transpose(after, (1, 0, 2))
    lon, lat = lon_taps.T, latitude_taps.T
    rows = row_total // CHUNKS
    hidden_total = sources * tiles * up_weight.shape[1]
    packing = Packing(chan_count, rows // sources * width)

    def spread(chunk):
        pieces = convolve(packing, me, sources, field, before, after, lon, lat, chunk, rows)
        with jax.named_scope(f"in{chunk}"):
            return [pieces[0]] + [shifted(pieces[s], "chan", s) for s in range(1, sources)]

    by_cell = [spread(0)]
    lon, far, near, across = after_all((lon, far, near, across), by_cell[0][0])
    with jax.named_scope("wz1"):
        rest = [exchanged(piece, "chan", 1) for piece in far[1:]]
    by_cell.append(spread(1))
    lon, rest = after_all((lon, rest), by_cell[1][0], by_cell[0][1:])
    others = jnp.concatenate([*far[1:], near, *rest], axis=0)
    with jax.named_scope("wx1"):
        others_across = exchanged(others, "tile", bits[0])
    by_cell.append(spread(2))
    lon, others, across = after_all((lon, others, across), by_cell[2][0], by_cell[1][1:])
    if len(bits) == 1:
        held = jnp.concatenate([shard, others, across], axis=0)
        with jax.named_scope("wc0"):
            received = exchanged(held, "tile", 1)
    by_cell.append(spread(3))
    others_across = after_all(others_across, by_cell[3][:2], by_cell[2][1:])
    weights, place = (), 0
    if len(bits) == 1:
        weights, place = prepare(held, received, hidden_total, (), 0), held.shape[0]
        held = others_across
    else:
        held = jnp.concatenate([shard, others, across, others_across], axis=0)
        for bit in bits[1:]:
            held = jnp.concatenate([held, exchanged(held, "tile", bit)], axis=0)
    with jax.named_scope("wc1"):
        received = exchanged(held, "tile", 1)
    up_all, down_all = prepare(held, received, hidden_total, weights, place)
    gain = norm_gain[:, None]
    updates = []
    for chunk in range(CHUNKS):
        pieces = mlp(packing, me, by_cell[chunk], gain, up_all, down_all)
        with jax.named_scope(f"out{chunk}"):
            updates.append([pieces[0]] + [shifted(pieces[s], "chan", s) for s in range(1, sources)])
        gain = after_all(gain, pieces[0], updates[chunk - 1][1:] if chunk else by_cell[CHUNKS - 1][1:])
    mixed = None
    for chunk in range(CHUNKS):
        mixed = add_rows(packing, me, updates[chunk], weather, mixed, chunk, rows)
    return mixed


def solution(mesh):
    return jax.shard_map(
        on_device,
        mesh=mesh,
        in_specs=(
            P("chan", "parts", "tile"),
            P(None, "chan"),
            P(None, "chan"),
            P(),
            P(None, ("tile", "chan")),
            P(None, ("tile", "chan")),
        ),
        out_specs=P("chan", "parts", "tile"),
        check_vma=False,
    )
```

time: 572 us -> 272 us (0.48)
  the two profiles are of different devices: /device:TPU:0 before, /device:TPU:24 now
where the time goes in v2:
time: 272 us; the launch traced here: 271 us
  Pallas kernels  138 us (51%)
  waiting for transfers between devices  64.5 us (24%)
  starting transfers between devices  36.7 us (13%)
  local copies, waits for them, and re-layouts  27.6 us (10%)
  other arithmetic  4.03 us (1%)
    ppermute x26, waiting for transfers between devices, shifted(): lax.ppermute(array, axis, [(i, (i + shift) % count) for i in range(count)])  64.5 us
    pallas_call x4, Pallas kernels, convolve(): pl.pallas_call(functools.partial(conv_kernel, packing, sources, row_count...  55.9 us
    pallas_call x4, Pallas kernels, mlp(): pl.pallas_call(functools.partial(mlp_kernel, packing, sources), grid_spec...  52.6 us
    ppermute x26, starting transfers between devices, shifted(): lax.ppermute(array, axis, [(i, (i + shift) % count) for i in range(count)])  32.7 us
    unnamed x59, local copies, waits for them, and re-layouts  17.3 us
    pallas_call x4, Pallas kernels, add_rows(): pl.pallas_call(functools.partial(add_kernel, packing, sources), grid_spec...  16.8 us
    pallas_call x2, Pallas kernels, prepare(): pl.pallas_call(prepare_kernel, grid=(count,), in_specs=[source, source] +...  12.7 us
  transfers between devices with their start and end apart: 33, of which 9 were waited for; matrix products, arithmetic and copies ran while one was open for 9% of the time, Pallas kernels for 49%

profile of v2, /device:TPU:24, one launch (start us, length us, event | category | flops | bytes accessed | tf_op | source)
XLA Modules:
  0.0 271.3 jit_solution(14731734574070783992)
XLA Ops:
  0.0 1.9 maximum_bitcast_fusion
  1.9 1.5 collective-permute-start.4
  4.2 2.6 fusion
  6.8 1.3 copy.38
  8.1 1.3 copy.37
  10.0 6.3 %copy.40 = bf16[192,32,360]{2,0,1:T(8,128)(2,1)} copy(bf16[192,32,360]{2,1,0:T(8,128)(2,1)} %refs_4_.7) | data formatting | bytes 8847360 | tf_op args[0]
  16.2 0.7 copy.31
  17.0 0.7 copy.32
  17.7 1.3 collective-permute-done.1
  19.0 1.5 copy.30
  20.5 1.5 copy.28
  22.0 13.7 %conv.4 = (bf16[3,360,128]{2,1,0:T(8,128)(2,1)}, bf16[3,360,128]{2,1,0:T(8,128)(2,1)}, bf16[3,360,128]{2,1,0:T(8,128)(2,1)}, bf16[3,360,128]{2,1,0:T(8,128)(2,1)}) custom-call(s32[1]{0:T(128)} %bitcast.me_ref, bf16[32,192,360]{2,1,0:T(8,128)(2,1)} %bitcast.12, bf16[32,192,8]{2,1,0:T(8,128)(2,1)} %bitcast.32, bf16[32,192,8]{2,1,0:T(8,128)(2,1)} %bitcast.22, ...), custom_call_target="tpu_custom_call" | custom-call | flops 1380000000 | bytes 1024 | tf_op jit(solution)/shard_map/conv/pallas_call | solution.py:135
  36.2 2.3 collective-permute-start.6
  38.6 0.7 collective-permute-start.7
  39.3 1.4 collective-permute-start.8
  40.7 1.9 constant_dynamic-update-slice_fusion.2
  42.6 1.9 constant_dynamic-update-slice_fusion.1
  44.6 14.3 %conv.5 = (bf16[3,360,128]{2,1,0:T(8,128)(2,1)}, bf16[3,360,128]{2,1,0:T(8,128)(2,1)}, bf16[3,360,128]{2,1,0:T(8,128)(2,1)}, bf16[3,360,128]{2,1,0:T(8,128)(2,1)}) custom-call(s32[1]{0:T(128)} %bitcast.me_ref, bf16[32,192,360]{2,1,0:T(8,128)(2,1)} %bitcast.14, bf16[32,192,8]{2,1,0:T(8,128)(2,1)} %bitcast.34, bf16[32,192,8]{2,1,0:T(8,128)(2,1)} %bitcast.24, ...), custom_call_target="tpu_custom_call" | custom-call | flops 1380000000 | bytes 1024 | tf_op jit(solution)/shard_map/conv/pallas_call | solution.py:135
  58.8 5.4 %collective-permute-done.6.refs_1_ = bf16[3,360,128]{2,1,0:T(8,128)(2,1)S(1)} collective-permute-done((bf16[3,360,128]{2,1,0:T(8,128)(2,1)}, bf16[3,360,128]{2,1,0:T(8,128)(2,1)S(1)}, u32[]{:S(2)}, u32[]{:S(2)}) %collective-permute-start.6) | collective-permute-done | bytes 276512 | tf_op jit(solution)/shard_map/in0/ppermute | solution.py:313
  64.3 5.7 %collective-permute-done.8.refs_3_ = bf16[3,360,128]{2,1,0:T(8,128)(2,1)S(1)} collective-permute-done((bf16[3,360,128]{2,1,0:T(8,128)(2,1)}, bf16[3,360,128]{2,1,0:T(8,128)(2,1)S(1)}, u32[]{:S(2)}, u32[]{:S(2)}) %collective-permute-start.8) | collective-permute-done | bytes 276512 | tf_op jit(solution)/shard_map/in0/ppermute | solution.py:313
  70.0 0.9 constant_dynamic-update-slice_fusion
  70.9 1.1 collective-permute-start.15
  72.0 1.6 collective-permute-start.9
  73.6 0.6 collective-permute-start.11
  74.2 14.3 %conv.6 = (bf16[3,360,128]{2,1,0:T(8,128)(2,1)}, bf16[3,360,128]{2,1,0:T(8,128)(2,1)}, bf16[3,360,128]{2,1,0:T(8,128)(2,1)}, bf16[3,360,128]{2,1,0:T(8,128)(2,1)}) custom-call(s32[1]{0:T(128)} %bitcast.me_ref, bf16[32,192,360]{2,1,0:T(8,128)(2,1)} %bitcast.17, bf16[32,192,8]{2,1,0:T(8,128)(2,1)} %bitcast.37, bf16[32,192,8]{2,1,0:T(8,128)(2,1)} %bitcast.27, ...), custom_call_target="tpu_custom_call" | custom-call | flops 1380000000 | bytes 1024 | tf_op jit(solution)/shard_map/conv/pallas_call | solution.py:135
  88.5 8.9 %collective-permute-done.10.refs_2_ = bf16[3,360,128]{2,1,0:T(8,128)(2,1)S(1)} collective-permute-done((bf16[3,360,128]{2,1,0:T(8,128)(2,1)}, bf16[3,360,128]{2,1,0:T(8,128)(2,1)S(1)}, u32[]{:S(2)}, u32[]{:S(2)}) %collective-permute-start.10) | collective-permute-done | bytes 276512 | tf_op jit(solution)/shard_map/in1/ppermute | solution.py:313
  97.4 0.8 copy-done.18
  98.2 2.1 pad_maximum_fusion.held_ref
  100.5 2.6 collective-permute-start.17
  103.1 1.9 collective-permute-start.18
  105.0 13.7 %conv.7 = (bf16[3,360,128]{2,1,0:T(8,128)(2,1)}, bf16[3,360,128]{2,1,0:T(8,128)(2,1)}, bf16[3,360,128]{2,1,0:T(8,128)(2,1)}, bf16[3,360,128]{2,1,0:T(8,128)(2,1)}) custom-call(s32[1]{0:T(128)} %bitcast.me_ref, bf16[32,192,360]{2,1,0:T(8,128)(2,1)} %bitcast.20, bf16[32,192,8]{2,1,0:T(8,128)(2,1)} %bitcast.40, bf16[32,192,8]{2,1,0:T(8,128)(2,1)} %bitcast.30, ...), custom_call_target="tpu_custom_call" | custom-call | flops 1380000000 | bytes 1024 | tf_op jit(solution)/shard_map/conv/pallas_call | solution.py:135
  118.7 1.9 collective-permute-start.12
  120.6 7.8 %collective-permute-done.17.refs_2_ = bf16[3,360,128]{2,1,0:T(8,128)(2,1)S(1)} collective-permute-done((bf16[3,360,128]{2,1,0:T(8,128)(2,1)}, bf16[3,360,128]{2,1,0:T(8,128)(2,1)S(1)}, u32[]{:S(2)}, u32[]{:S(2)}) %collective-permute-start.17) | collective-permute-done | bytes 276512 | tf_op jit(solution)/shard_map/in2/ppermute | solution.py:313
  128.5 5.6 %collective-permute-done.12.refs_1_ = bf16[3,360,128]{2,1,0:T(8,128)(2,1)S(1)} collective-permute-done((bf16[3,360,128]{2,1,0:T(8,128)(2,1)}, bf16[3,360,128]{2,1,0:T(8,128)(2,1)S(1)}, u32[]{:S(2)}, u32[]{:S(2)}) %collective-permute-start.12) | collective-permute-done | bytes 276512 | tf_op jit(solution)/shard_map/in3/ppermute | solution.py:313
  134.2 1.0 copy.33.refs_4_
  135.2 1.1 collective-permute-start.13
  136.3 7.6 %prepare.2 = (bf16[3072,768]{1,0:T(8,128)(2,1)}, bf16[768,3072]{1,0:T(8,128)(2,1)}) custom-call(bf16[5,384,768]{2,1,0:T(8,128)(2,1)} %copy-done, bf16[5,384,768]{2,1,0:T(8,128)(2,1)} %collective-permute-done.20.received_ref), custom_call_target="tpu_custom_call" | custom-call | flops 575000000 | bytes 1024 | tf_op jit(solution)/shard_map/prepare/pallas_call | solution.py:292
  143.9 5.1 %prepare.3 = (bf16[3072,768]{1,0:T(8,128)(2,1)}, bf16[768,3072]{1,0:T(8,128)(2,1)}) custom-call(bf16[3,384,768]{2,1,0:T(8,128)(2,1)} %collective-permute-done.15.held_ref, bf16[3,384,768]{2,1,0:T(8,128)(2,1)} %collective-permute-done.19.received_ref, bf16[3072,768]{1,0:T(8,128)(2,1)} %get-tuple-element.80.refs_0_, ...), custom_call_target="tpu_custom_call", output_to_operand_aliasing={{0}: (2, {}), {1}: (3, {})} | custom-call | flops 345000000 | bytes 1024 | tf_op jit(solution)/shard_map/prepare/pallas_call | solution.py:292
  149.1 13.2 %mlp.4 = (bf16[3,360,128]{2,1,0:T(8,128)(2,1)}, bf16[3,360,128]{2,1,0:T(8,128)(2,1)}, bf16[3,360,128]{2,1,0:T(8,128)(2,1)}, bf16[3,360,128]{2,1,0:T(8,128)(2,1)}) custom-call(s32[1]{0:T(128)} %bitcast.me_ref, bf16[3,360,128]{2,1,0:T(8,128)(2,1)} %get-tuple-element.54.refs_0_, bf16[3,360,128]{2,1,0:T(8,128)(2,1)} %copy-done.10, ...), custom_call_target="tpu_custom_call" | custom-call | flops 1495000064 | bytes 1024 | tf_op jit(solution)/shard_map/mlp/pallas_call | solution.py:202
  162.2 3.8 %collective-permute-start.21 = (bf16[3,360,128]{2,1,0:T(8,128)(2,1)}, bf16[3,360,128]{2,1,0:T(8,128)(2,1)S(1)}, u32[]{:S(2)}, u32[]{:S(2)}) collective-permute-start(bf16[3,360,128]{2,1,0:T(8,128)(2,1)} %get-tuple-element.87), channel_id=1, source_target_pairs={{0,1},{1,2},{2,3},{3,0},{4,5},{5,6},{6,7},{7,4},{8,9},{9,10},{10,1... | collective-permute-start | bytes 829448 | tf_op jit(solution)/shard_map/out0/ppermute | solution.py:313
  166.1 0.6 collective-permute-start.23
  166.7 1.0 copy.34.refs_4_
  167.6 13.2 %mlp.5 = (bf16[3,360,128]{2,1,0:T(8,128)(2,1)}, bf16[3,360,128]{2,1,0:T(8,128)(2,1)}, bf16[3,360,128]{2,1,0:T(8,128)(2,1)}, bf16[3,360,128]{2,1,0:T(8,128)(2,1)}) custom-call(s32[1]{0:T(128)} %bitcast.me_ref, bf16[3,360,128]{2,1,0:T(8,128)(2,1)} %get-tuple-element.57.refs_0_, bf16[3,360,128]{2,1,0:T(8,128)(2,1)} %copy-done.14, ...), custom_call_target="tpu_custom_call" | custom-call | flops 1495000064 | bytes 1024 | tf_op jit(solution)/shard_map/mlp/pallas_call | solution.py:202
  180.8 3.2 %collective-permute-start.24 = (bf16[3,360,128]{2,1,0:T(8,128)(2,1)}, bf16[3,360,128]{2,1,0:T(8,128)(2,1)S(1)}, u32[]{:S(2)}, u32[]{:S(2)}) collective-permute-start(bf16[3,360,128]{2,1,0:T(8,128)(2,1)} %get-tuple-element.92), channel_id=1, source_target_pairs={{0,1},{1,2},{2,3},{3,0},{4,5},{5,6},{6,7},{7,4},{8,9},{9,10},{10,1... | collective-permute-start | bytes 829448 | tf_op jit(solution)/shard_map/out1/ppermute | solution.py:313
  184.0 1.1 collective-permute-start.25
  185.1 1.0 collective-permute-start.26
  186.2 17.2 %collective-permute-done.22.refs_2_ = bf16[3,360,128]{2,1,0:T(8,128)(2,1)S(1)} collective-permute-done((bf16[3,360,128]{2,1,0:T(8,128)(2,1)}, bf16[3,360,128]{2,1,0:T(8,128)(2,1)S(1)}, u32[]{:S(2)}, u32[]{:S(2)}) %collective-permute-start.22) | collective-permute-done | bytes 276512 | tf_op jit(solution)/shard_map/out0/ppermute | solution.py:313
  203.4 1.0 copy.35.refs_4_
  204.3 13.1 %mlp.6 = (bf16[3,360,128]{2,1,0:T(8,128)(2,1)}, bf16[3,360,128]{2,1,0:T(8,128)(2,1)}, bf16[3,360,128]{2,1,0:T(8,128)(2,1)}, bf16[3,360,128]{2,1,0:T(8,128)(2,1)}) custom-call(s32[1]{0:T(128)} %bitcast.me_ref, bf16[3,360,128]{2,1,0:T(8,128)(2,1)} %get-tuple-element.65.refs_0_, bf16[3,360,128]{2,1,0:T(8,128)(2,1)} %copy-done.15, ...), custom_call_target="tpu_custom_call" | custom-call | flops 1495000064 | bytes 1024 | tf_op jit(solution)/shard_map/mlp/pallas_call | solution.py:202
  217.6 2.1 collective-permute-start.31
  219.7 2.0 collective-permute-start.32
  221.7 0.9 copy.36.refs_4_
  222.6 13.1 %mlp.7 = (bf16[3,360,128]{2,1,0:T(8,128)(2,1)}, bf16[3,360,128]{2,1,0:T(8,128)(2,1)}, bf16[3,360,128]{2,1,0:T(8,128)(2,1)}, bf16[3,360,128]{2,1,0:T(8,128)(2,1)}) custom-call(s32[1]{0:T(128)} %bitcast.me_ref, bf16[3,360,128]{2,1,0:T(8,128)(2,1)} %get-tuple-element.70.refs_0_, bf16[3,360,128]{2,1,0:T(8,128)(2,1)} %copy-done.12, ...), custom_call_target="tpu_custom_call" | custom-call | flops 1495000064 | bytes 1024 | tf_op jit(solution)/shard_map/mlp/pallas_call | solution.py:202
  235.8 1.9 collective-permute-start.27
  237.7 2.0 collective-permute-start.29
  239.7 4.2 %add.4.refs_5_ = bf16[192,32,360]{2,1,0:T(8,128)(2,1)} custom-call(s32[1]{0:T(128)} %bitcast.me_ref, bf16[3,360,128]{2,1,0:T(8,128)(2,1)} %get-tuple-element.84.refs_0_, bf16[3,360,128]{2,1,0:T(8,128)(2,1)} %copy-done.20, bf16[3,360,128]{2,1,0:T(8,128)(2,1)} %copy-done.21, bf16[3,360,128]{2,1,0:T(8,128)(2,1)} %copy-done.22, bf16[192,32,360]{2,1,0:T(8,128)(2,1)} %refs_4_.7), custom_call_target="tpu_custom_call" | custom-call | flops 460000000 | bytes 1024 | tf_op jit(solution)/shard_map/add/pallas_call | solution.py:256
  243.9 4.2 %add.5.refs_5_ = bf16[192,32,360]{2,1,0:T(8,128)(2,1)} custom-call(s32[1]{0:T(128)} %bitcast.me_ref, bf16[3,360,128]{2,1,0:T(8,128)(2,1)} %get-tuple-element.86.refs_0_, bf16[3,360,128]{2,1,0:T(8,128)(2,1)} %copy-done.1, bf16[3,360,128]{2,1,0:T(8,128)(2,1)} %copy-done.2, bf16[3,360,128]{2,1,0:T(8,128)(2,1)} %copy-done.3, ...), custom_call_target="tpu_custom_call", output_to_operand_aliasing={{}: (6, {})} | custom-call | flops 460000000 | bytes 1024 | tf_op jit(solution)/shard_map/add/pallas_call | solution.py:256
  248.1 8.8 %collective-permute-done.31.refs_2_ = bf16[3,360,128]{2,1,0:T(8,128)(2,1)S(1)} collective-permute-done((bf16[3,360,128]{2,1,0:T(8,128)(2,1)}, bf16[3,360,128]{2,1,0:T(8,128)(2,1)S(1)}, u32[]{:S(2)}, u32[]{:S(2)}) %collective-permute-start.31) | collective-permute-done | bytes 276512 | tf_op jit(solution)/shard_map/out2/ppermute | solution.py:313
  256.9 0.7 copy-done.5
  257.6 0.7 copy-done.6
  258.3 4.2 %add.6.refs_5_ = bf16[192,32,360]{2,1,0:T(8,128)(2,1)} custom-call(s32[1]{0:T(128)} %bitcast.me_ref, bf16[3,360,128]{2,1,0:T(8,128)(2,1)} %get-tuple-element.91.refs_0_, bf16[3,360,128]{2,1,0:T(8,128)(2,1)} %copy-done.4, bf16[3,360,128]{2,1,0:T(8,128)(2,1)} %copy-done.5, bf16[3,360,128]{2,1,0:T(8,128)(2,1)} %copy-done.6, ...), custom_call_target="tpu_custom_call", output_to_operand_aliasing={{}: (6, {})} | custom-call | flops 460000000 | bytes 1024 | tf_op jit(solution)/shard_map/add/pallas_call | solution.py:256
  262.5 3.7 %collective-permute-done.28.refs_2_ = bf16[3,360,128]{2,1,0:T(8,128)(2,1)S(1)} collective-permute-done((bf16[3,360,128]{2,1,0:T(8,128)(2,1)}, bf16[3,360,128]{2,1,0:T(8,128)(2,1)S(1)}, u32[]{:S(2)}, u32[]{:S(2)}) %collective-permute-start.28) | collective-permute-done | bytes 276512 | tf_op jit(solution)/shard_map/out3/ppermute | solution.py:313
  266.2 0.7 copy-done.8
  267.1 4.2 %add.7 = bf16[192,32,360]{2,1,0:T(8,128)(2,1)} custom-call(s32[1]{0:T(128)} %bitcast.me_ref, bf16[3,360,128]{2,1,0:T(8,128)(2,1)} %get-tuple-element.96.refs_0_, bf16[3,360,128]{2,1,0:T(8,128)(2,1)} %copy-done.7, bf16[3,360,128]{2,1,0:T(8,128)(2,1)} %copy-done.8, bf16[3,360,128]{2,1,0:T(8,128)(2,1)} %copy-done.9, ...), custom_call_target="tpu_custom_call", output_to_operand_aliasing={{}: (6, {})} | custom-call | flops 460000000 | bytes 1024 | tf_op jit(solution)/shard_map/add/pallas_call | solution.py:256
  (86 shorter events, 2.5 us)
Async XLA Ops:
  1.9 33.8 %collective-permute-start.4 = (bf16[1,384,768]{2,1,0:T(8,128)(2,1)}, bf16[1,384,768]{2,1,0:T(8,128)(2,1)}, u32[]{:S(2)}, u32[]{:S(2)}) collective-permute-start(bf16[1,384,768]{2,1,0:T(8,128)(2,1)} %maximum_bitcast_fusion), channel_id=1, source_target_pairs={{0,8},{4,12},{8,0},{12,4},{1,9},{5,13},{9,1},{13,5},{2,10},{6,14},... | collective-permute-start | bytes 1769480 | tf_op jit(solution)/shard_map/wx0/ppermute | solution.py:317
  3.4 32.3 %collective-permute-start.3 = (bf16[1,384,768]{2,1,0:T(8,128)(2,1)}, bf16[1,384,768]{2,1,0:T(8,128)(2,1)}, u32[]{:S(2)}, u32[]{:S(2)}) collective-permute-start(bf16[1,384,768]{2,1,0:T(8,128)(2,1)} %maximum_bitcast_fusion), channel_id=1, source_target_pairs={{0,1},{1,0},{2,3},{3,2},{4,5},{5,4},{6,7},{7,6},{8,9},{9,8},{10,11... | collective-permute-start | bytes 1769480 | tf_op jit(solution)/shard_map/wz/ppermute | solution.py:317
  3.9 31.9 %collective-permute-start.2 = (bf16[1,384,768]{2,1,0:T(8,128)(2,1)}, bf16[1,384,768]{2,1,0:T(8,128)(2,1)}, u32[]{:S(2)}, u32[]{:S(2)}) collective-permute-start(bf16[1,384,768]{2,1,0:T(8,128)(2,1)} %maximum_bitcast_fusion), channel_id=1, source_target_pairs={{0,2},{1,3},{2,0},{3,1},{4,6},{5,7},{6,4},{7,5},{8,10},{9,11},{10,... | collective-permute-start | bytes 1769480 | tf_op jit(solution)/shard_map/wz/ppermute | solution.py:317
  8.1 10.9 %collective-permute-start.1 = (bf16[192,32,8]{0,2,1:T(8,128)(2,1)S(1)}, bf16[192,32,8]{0,2,1:T(8,128)(2,1)S(1)}, u32[]{:S(2)}, u32[]{:S(2)}) collective-permute-start(bf16[192,32,8]{0,2,1:T(8,128)(2,1)S(1)} %copy.38), channel_id=1, source_target_pairs={{0,12},{4,0},{8,4},{12,8},{1,13},{5,1},{9,5},{13,9},{2,14},{6,2},{... | collective-permute-start | bytes 294920 | tf_op jit(solution)/shard_map/halo/ppermute | solution.py:313
  9.4 11.1 %collective-permute-start = (bf16[192,32,8]{0,2,1:T(8,128)(2,1)S(1)}, bf16[192,32,8]{0,2,1:T(8,128)(2,1)S(1)}, u32[]{:S(2)}, u32[]{:S(2)}) collective-permute-start(bf16[192,32,8]{0,2,1:T(8,128)(2,1)S(1)} %copy.37), channel_id=1, source_target_pairs={{0,4},{4,8},{8,12},{12,0},{1,5},{5,9},{9,13},{13,1},{2,6},{6,10},{... | collective-permute-start | bytes 294920 | tf_op jit(solution)/shard_map/halo/ppermute | solution.py:313
  10.0 6.3 %copy-start.23 = (f32[9,192]{1,0:T(8,128)S(1)}, f32[9,192]{1,0:T(8,128)}, u32[]{:S(2)}) copy-start(f32[9,192]{1,0:T(8,128)} %param.7) | copy-start | bytes 20740
  10.0 7.0 %copy-start.24 = (f32[9,192]{1,0:T(8,128)S(1)}, f32[9,192]{1,0:T(8,128)}, u32[]{:S(2)}) copy-start(f32[9,192]{1,0:T(8,128)} %param.8) | copy-start | bytes 20740
  35.7 34.3 %collective-permute-start.5 = (bf16[1,384,768]{2,1,0:T(8,128)(2,1)}, bf16[1,384,768]{2,1,0:T(8,128)(2,1)S(1)}, u32[]{:S(2)}, u32[]{:S(2)}) collective-permute-start(bf16[1,384,768]{2,1,0:T(8,128)(2,1)} %collective-permute-done.2), channel_id=1, source_target_pairs={{0,1},{1,0},{2,3},{3,2},{4,5},{5,4},{6,7},{7,6},{8,9},{9,8},{10,11... | collective-permute-start | bytes 1769480 | tf_op jit(solution)/shard_map/wz1/ppermute | solution.py:317
  36.2 28.0 %collective-permute-start.6 = (bf16[3,360,128]{2,1,0:T(8,128)(2,1)}, bf16[3,360,128]{2,1,0:T(8,128)(2,1)S(1)}, u32[]{:S(2)}, u32[]{:S(2)}) collective-permute-start(bf16[3,360,128]{2,1,0:T(8,128)(2,1)} %get-tuple-element.58), channel_id=1, source_target_pairs={{0,1},{1,2},{2,3},{3,0},{4,5},{5,6},{6,7},{7,4},{8,9},{9,10},{10,1... | collective-permute-start | bytes 829448 | tf_op jit(solution)/shard_map/in0/ppermute | solution.py:313
  38.6 25.7 %collective-permute-start.7 = (bf16[3,360,128]{2,1,0:T(8,128)(2,1)}, bf16[3,360,128]{2,1,0:T(8,128)(2,1)S(1)}, u32[]{:S(2)}, u32[]{:S(2)}) collective-permute-start(bf16[3,360,128]{2,1,0:T(8,128)(2,1)} %get-tuple-element.59), channel_id=1, source_target_pairs={{0,2},{1,3},{2,0},{3,1},{4,6},{5,7},{6,4},{7,5},{8,10},{9,11},{10,... | collective-permute-start | bytes 829448 | tf_op jit(solution)/shard_map/in0/ppermute | solution.py:313
  39.3 30.7 %collective-permute-start.8 = (bf16[3,360,128]{2,1,0:T(8,128)(2,1)}, bf16[3,360,128]{2,1,0:T(8,128)(2,1)S(1)}, u32[]{:S(2)}, u32[]{:S(2)}) collective-permute-start(bf16[3,360,128]{2,1,0:T(8,128)(2,1)} %get-tuple-element.60), channel_id=1, source_target_pairs={{0,3},{1,0},{2,1},{3,2},{4,7},{5,4},{6,5},{7,6},{8,11},{9,8},{10,9... | collective-permute-start | bytes 829448 | tf_op jit(solution)/shard_map/in0/ppermute | solution.py:313
  64.3 24.2 %copy-start.10 = (bf16[3,360,128]{2,1,0:T(8,128)(2,1)}, bf16[3,360,128]{2,1,0:T(8,128)(2,1)S(1)}, u32[]{:S(2)}) copy-start(bf16[3,360,128]{2,1,0:T(8,128)(2,1)S(1)} %collective-permute-done.6.refs_1_) | copy-start | bytes 829444
  64.3 24.2 %copy-start.11 = (bf16[3,360,128]{2,1,0:T(8,128)(2,1)}, bf16[3,360,128]{2,1,0:T(8,128)(2,1)S(1)}, u32[]{:S(2)}) copy-start(bf16[3,360,128]{2,1,0:T(8,128)(2,1)S(1)} %collective-permute-done.7.refs_2_) | copy-start | bytes 829444
  70.0 18.5 %copy-start.13 = (bf16[3,360,128]{2,1,0:T(8,128)(2,1)}, bf16[3,360,128]{2,1,0:T(8,128)(2,1)S(1)}, u32[]{:S(2)}) copy-start(bf16[3,360,128]{2,1,0:T(8,128)(2,1)S(1)} %collective-permute-done.8.refs_3_) | copy-start | bytes 829444
  70.9 63.2 %collective-permute-start.15 = (bf16[3,384,768]{2,1,0:T(8,128)(2,1)}, bf16[3,384,768]{2,1,0:T(8,128)(2,1)}, u32[]{:S(2)}, u32[]{:S(2)}) collective-permute-start(bf16[3,384,768]{2,1,0:T(8,128)(2,1)} %constant_dynamic-update-slice_fusion), channel_id=1, source_target_pairs={{0,8},{4,12},{8,0},{12,4},{1,9},{5,13},{9,1},{13,5},{2,10},{6,14},... | collective-permute-start | bytes 5308424 | tf_op jit(solution)/shard_map/wx1/ppermute | solution.py:317
  72.0 16.5 %collective-permute-start.9 = (bf16[3,360,128]{2,1,0:T(8,128)(2,1)}, bf16[3,360,128]{2,1,0:T(8,128)(2,1)S(1)}, u32[]{:S(2)}, u32[]{:S(2)}) collective-permute-start(bf16[3,360,128]{2,1,0:T(8,128)(2,1)} %get-tuple-element.66), channel_id=1, source_target_pairs={{0,1},{1,2},{2,3},{3,0},{4,5},{5,6},{6,7},{7,4},{8,9},{9,10},{10,1... | collective-permute-start | bytes 829448 | tf_op jit(solution)/shard_map/in1/ppermute | solution.py:313
  73.6 23.8 %collective-permute-start.10 = (bf16[3,360,128]{2,1,0:T(8,128)(2,1)}, bf16[3,360,128]{2,1,0:T(8,128)(2,1)S(1)}, u32[]{:S(2)}, u32[]{:S(2)}) collective-permute-start(bf16[3,360,128]{2,1,0:T(8,128)(2,1)} %get-tuple-element.67), channel_id=1, source_target_pairs={{0,2},{1,3},{2,0},{3,1},{4,6},{5,7},{6,4},{7,5},{8,10},{9,11},{10,... | collective-permute-start | bytes 829448 | tf_op jit(solution)/shard_map/in1/ppermute | solution.py:313
  73.6 23.8 %collective-permute-start.11 = (bf16[3,360,128]{2,1,0:T(8,128)(2,1)}, bf16[3,360,128]{2,1,0:T(8,128)(2,1)S(1)}, u32[]{:S(2)}, u32[]{:S(2)}) collective-permute-start(bf16[3,360,128]{2,1,0:T(8,128)(2,1)} %get-tuple-element.68), channel_id=1, source_target_pairs={{0,3},{1,0},{2,1},{3,2},{4,7},{5,4},{6,5},{7,6},{8,11},{9,8},{10,9... | collective-permute-start | bytes 829448 | tf_op jit(solution)/shard_map/in1/ppermute | solution.py:313
  88.5 11.8 %copy-start.14 = (bf16[3,360,128]{2,1,0:T(8,128)(2,1)}, bf16[3,360,128]{2,1,0:T(8,128)(2,1)S(1)}, u32[]{:S(2)}) copy-start(bf16[3,360,128]{2,1,0:T(8,128)(2,1)S(1)} %collective-permute-done.9.refs_1_) | copy-start | bytes 829444
  97.4 2.9 %copy-start.16 = (bf16[3,360,128]{2,1,0:T(8,128)(2,1)}, bf16[3,360,128]{2,1,0:T(8,128)(2,1)S(1)}, u32[]{:S(2)}) copy-start(bf16[3,360,128]{2,1,0:T(8,128)(2,1)S(1)} %collective-permute-done.10.refs_2_) | copy-start | bytes 829444
  97.4 0.8 copy-start.18
  100.3 18.4 %copy-start = (bf16[5,384,768]{2,1,0:T(8,128)(2,1)}, bf16[5,384,768]{2,1,0:T(8,128)(2,1)S(1)}, u32[]{:S(2)}) copy-start(bf16[5,384,768]{2,1,0:T(8,128)(2,1)S(1)} %pad_maximum_fusion.held_ref) | copy-start | bytes 8847364
  100.3 36.0 %collective-permute-start.20 = (bf16[5,384,768]{2,1,0:T(8,128)(2,1)S(1)}, bf16[5,384,768]{2,1,0:T(8,128)(2,1)}, u32[]{:S(2)}, u32[]{:S(2)}) collective-permute-start(bf16[5,384,768]{2,1,0:T(8,128)(2,1)S(1)} %pad_maximum_fusion.held_ref), channel_id=1, source_target_pairs={{0,4},{4,0},{8,12},{12,8},{1,5},{5,1},{9,13},{13,9},{2,6},{6,2},{1... | collective-permute-start | bytes 8847368 | tf_op jit(solution)/shard_map/wc0/ppermute | solution.py:317
  100.4 18.3 %collective-permute-start.16 = (bf16[3,360,128]{2,1,0:T(8,128)(2,1)}, bf16[3,360,128]{2,1,0:T(8,128)(2,1)S(1)}, u32[]{:S(2)}, u32[]{:S(2)}) collective-permute-start(bf16[3,360,128]{2,1,0:T(8,128)(2,1)} %get-tuple-element.74), channel_id=1, source_target_pairs={{0,1},{1,2},{2,3},{3,0},{4,5},{5,6},{6,7},{7,4},{8,9},{9,10},{10,1... | collective-permute-start | bytes 829448 | tf_op jit(solution)/shard_map/in2/ppermute | solution.py:313
  100.5 28.0 %collective-permute-start.17 = (bf16[3,360,128]{2,1,0:T(8,128)(2,1)}, bf16[3,360,128]{2,1,0:T(8,128)(2,1)S(1)}, u32[]{:S(2)}, u32[]{:S(2)}) collective-permute-start(bf16[3,360,128]{2,1,0:T(8,128)(2,1)} %get-tuple-element.75), channel_id=1, source_target_pairs={{0,2},{1,3},{2,0},{3,1},{4,6},{5,7},{6,4},{7,5},{8,10},{9,11},{10,... | collective-permute-start | bytes 829448 | tf_op jit(solution)/shard_map/in2/ppermute | solution.py:313
  103.1 31.1 %copy-start.25 = (f32[768]{0:T(1024)S(1)}, f32[768]{0:T(1024)}, u32[]{:S(2)}) copy-start(f32[768]{0:T(1024)} %param.9) | copy-start | bytes 9220
  103.1 25.4 %collective-permute-start.18 = (bf16[3,360,128]{2,1,0:T(8,128)(2,1)}, bf16[3,360,128]{2,1,0:T(8,128)(2,1)S(1)}, u32[]{:S(2)}, u32[]{:S(2)}) collective-permute-start(bf16[3,360,128]{2,1,0:T(8,128)(2,1)} %get-tuple-element.76), channel_id=1, source_target_pairs={{0,3},{1,0},{2,1},{3,2},{4,7},{5,4},{6,5},{7,6},{8,11},{9,8},{10,9... | collective-permute-start | bytes 829448 | tf_op jit(solution)/shard_map/in2/ppermute | solution.py:313
  118.7 25.2 %copy-start.15 = (bf16[3,360,128]{2,1,0:T(8,128)(2,1)}, bf16[3,360,128]{2,1,0:T(8,128)(2,1)S(1)}, u32[]{:S(2)}) copy-start(bf16[3,360,128]{2,1,0:T(8,128)(2,1)S(1)} %collective-permute-done.16.refs_1_) | copy-start | bytes 829444
  118.7 15.4 %collective-permute-start.12 = (bf16[3,360,128]{2,1,0:T(8,128)(2,1)}, bf16[3,360,128]{2,1,0:T(8,128)(2,1)S(1)}, u32[]{:S(2)}, u32[]{:S(2)}) collective-permute-start(bf16[3,360,128]{2,1,0:T(8,128)(2,1)} %get-tuple-element.71), channel_id=1, source_target_pairs={{0,1},{1,2},{2,3},{3,0},{4,5},{5,6},{6,7},{7,4},{8,9},{9,10},{10,1... | collective-permute-start | bytes 829448 | tf_op jit(solution)/shard_map/in3/ppermute | solution.py:313
  128.5 5.6 %copy-start.17 = (bf16[3,360,128]{2,1,0:T(8,128)(2,1)}, bf16[3,360,128]{2,1,0:T(8,128)(2,1)S(1)}, u32[]{:S(2)}) copy-start(bf16[3,360,128]{2,1,0:T(8,128)(2,1)S(1)} %collective-permute-done.17.refs_2_) | copy-start | bytes 829444
  128.5 5.6 %copy-start.19 = (bf16[3,360,128]{2,1,0:T(8,128)(2,1)}, bf16[3,360,128]{2,1,0:T(8,128)(2,1)S(1)}, u32[]{:S(2)}) copy-start(bf16[3,360,128]{2,1,0:T(8,128)(2,1)S(1)} %collective-permute-done.18.refs_3_) | copy-start | bytes 829444
  134.1 9.8 %copy-start.12 = (bf16[3,360,128]{2,1,0:T(8,128)(2,1)}, bf16[3,360,128]{2,1,0:T(8,128)(2,1)S(1)}, u32[]{:S(2)}) copy-start(bf16[3,360,128]{2,1,0:T(8,128)(2,1)S(1)} %collective-permute-done.12.refs_1_) | copy-start | bytes 829444
  134.1 9.8 %collective-permute-start.19 = (bf16[3,384,768]{2,1,0:T(8,128)(2,1)}, bf16[3,384,768]{2,1,0:T(8,128)(2,1)}, u32[]{:S(2)}, u32[]{:S(2)}) collective-permute-start(bf16[3,384,768]{2,1,0:T(8,128)(2,1)} %collective-permute-done.15.held_ref), channel_id=1, source_target_pairs={{0,4},{4,0},{8,12},{12,8},{1,5},{5,1},{9,13},{13,9},{2,6},{6,2},{1... | collective-permute-start | bytes 5308424 | tf_op jit(solution)/shard_map/wc1/ppermute | solution.py:317
  135.2 31.5 %collective-permute-start.13 = (bf16[3,360,128]{2,1,0:T(8,128)(2,1)}, bf16[3,360,128]{2,1,0:T(8,128)(2,1)}, u32[]{:S(2)}, u32[]{:S(2)}) collective-permute-start(bf16[3,360,128]{2,1,0:T(8,128)(2,1)} %get-tuple-element.72), channel_id=1, source_target_pairs={{0,2},{1,3},{2,0},{3,1},{4,6},{5,7},{6,4},{7,5},{8,10},{9,11},{10,... | collective-permute-start | bytes 829448 | tf_op jit(solution)/shard_map/in3/ppermute | solution.py:313
  136.3 30.4 %collective-permute-start.14 = (bf16[3,360,128]{2,1,0:T(8,128)(2,1)}, bf16[3,360,128]{2,1,0:T(8,128)(2,1)}, u32[]{:S(2)}, u32[]{:S(2)}) collective-permute-start(bf16[3,360,128]{2,1,0:T(8,128)(2,1)} %get-tuple-element.73), channel_id=1, source_target_pairs={{0,3},{1,0},{2,1},{3,2},{4,7},{5,4},{6,5},{7,6},{8,11},{9,8},{10,9... | collective-permute-start | bytes 829448 | tf_op jit(solution)/shard_map/in3/ppermute | solution.py:313
  162.2 22.9 %collective-permute-start.21 = (bf16[3,360,128]{2,1,0:T(8,128)(2,1)}, bf16[3,360,128]{2,1,0:T(8,128)(2,1)S(1)}, u32[]{:S(2)}, u32[]{:S(2)}) collective-permute-start(bf16[3,360,128]{2,1,0:T(8,128)(2,1)} %get-tuple-element.87), channel_id=1, source_target_pairs={{0,1},{1,2},{2,3},{3,0},{4,5},{5,6},{6,7},{7,4},{8,9},{9,10},{10,1... | collective-permute-start | bytes 829448 | tf_op jit(solution)/shard_map/out0/ppermute | solution.py:313
  166.1 37.3 %collective-permute-start.22 = (bf16[3,360,128]{2,1,0:T(8,128)(2,1)}, bf16[3,360,128]{2,1,0:T(8,128)(2,1)S(1)}, u32[]{:S(2)}, u32[]{:S(2)}) collective-permute-start(bf16[3,360,128]{2,1,0:T(8,128)(2,1)} %get-tuple-element.88), channel_id=1, source_target_pairs={{0,2},{1,3},{2,0},{3,1},{4,6},{5,7},{6,4},{7,5},{8,10},{9,11},{10,... | collective-permute-start | bytes 829448 | tf_op jit(solution)/shard_map/out0/ppermute | solution.py:313
  166.1 37.3 %collective-permute-start.23 = (bf16[3,360,128]{2,1,0:T(8,128)(2,1)}, bf16[3,360,128]{2,1,0:T(8,128)(2,1)S(1)}, u32[]{:S(2)}, u32[]{:S(2)}) collective-permute-start(bf16[3,360,128]{2,1,0:T(8,128)(2,1)} %get-tuple-element.89), channel_id=1, source_target_pairs={{0,3},{1,0},{2,1},{3,2},{4,7},{5,4},{6,5},{7,6},{8,11},{9,8},{10,9... | collective-permute-start | bytes 829448 | tf_op jit(solution)/shard_map/out0/ppermute | solution.py:313
  180.8 36.7 %collective-permute-start.24 = (bf16[3,360,128]{2,1,0:T(8,128)(2,1)}, bf16[3,360,128]{2,1,0:T(8,128)(2,1)S(1)}, u32[]{:S(2)}, u32[]{:S(2)}) collective-permute-start(bf16[3,360,128]{2,1,0:T(8,128)(2,1)} %get-tuple-element.92), channel_id=1, source_target_pairs={{0,1},{1,2},{2,3},{3,0},{4,5},{5,6},{6,7},{7,4},{8,9},{9,10},{10,1... | collective-permute-start | bytes 829448 | tf_op jit(solution)/shard_map/out1/ppermute | solution.py:313
  184.0 33.6 %collective-permute-start.25 = (bf16[3,360,128]{2,1,0:T(8,128)(2,1)}, bf16[3,360,128]{2,1,0:T(8,128)(2,1)S(1)}, u32[]{:S(2)}, u32[]{:S(2)}) collective-permute-start(bf16[3,360,128]{2,1,0:T(8,128)(2,1)} %get-tuple-element.93), channel_id=1, source_target_pairs={{0,2},{1,3},{2,0},{3,1},{4,6},{5,7},{6,4},{7,5},{8,10},{9,11},{10,... | collective-permute-start | bytes 829448 | tf_op jit(solution)/shard_map/out1/ppermute | solution.py:313
  185.1 32.3 %copy-start.20 = (bf16[3,360,128]{2,1,0:T(8,128)(2,1)}, bf16[3,360,128]{2,1,0:T(8,128)(2,1)S(1)}, u32[]{:S(2)}) copy-start(bf16[3,360,128]{2,1,0:T(8,128)(2,1)S(1)} %collective-permute-done.21.refs_1_) | copy-start | bytes 829444
  185.1 32.5 %collective-permute-start.26 = (bf16[3,360,128]{2,1,0:T(8,128)(2,1)}, bf16[3,360,128]{2,1,0:T(8,128)(2,1)S(1)}, u32[]{:S(2)}, u32[]{:S(2)}) collective-permute-start(bf16[3,360,128]{2,1,0:T(8,128)(2,1)} %get-tuple-element.94), channel_id=1, source_target_pairs={{0,3},{1,0},{2,1},{3,2},{4,7},{5,4},{6,5},{7,6},{8,11},{9,8},{10,9... | collective-permute-start | bytes 829448 | tf_op jit(solution)/shard_map/out1/ppermute | solution.py:313
  203.4 14.1 %copy-start.21 = (bf16[3,360,128]{2,1,0:T(8,128)(2,1)}, bf16[3,360,128]{2,1,0:T(8,128)(2,1)S(1)}, u32[]{:S(2)}) copy-start(bf16[3,360,128]{2,1,0:T(8,128)(2,1)S(1)} %collective-permute-done.22.refs_2_) | copy-start | bytes 829444
  203.4 14.1 %copy-start.22 = (bf16[3,360,128]{2,1,0:T(8,128)(2,1)}, bf16[3,360,128]{2,1,0:T(8,128)(2,1)S(1)}, u32[]{:S(2)}) copy-start(bf16[3,360,128]{2,1,0:T(8,128)(2,1)S(1)} %collective-permute-done.23.refs_3_) | copy-start | bytes 829444
  217.5 20.2 %collective-permute-start.30 = (bf16[3,360,128]{2,1,0:T(8,128)(2,1)}, bf16[3,360,128]{2,1,0:T(8,128)(2,1)S(1)}, u32[]{:S(2)}, u32[]{:S(2)}) collective-permute-start(bf16[3,360,128]{2,1,0:T(8,128)(2,1)} %get-tuple-element.100), channel_id=1, source_target_pairs={{0,1},{1,2},{2,3},{3,0},{4,5},{5,6},{6,7},{7,4},{8,9},{9,10},{10,1... | collective-permute-start | bytes 829448 | tf_op jit(solution)/shard_map/out2/ppermute | solution.py:313
  217.6 18.2 %copy-start.1 = (bf16[3,360,128]{2,1,0:T(8,128)(2,1)}, bf16[3,360,128]{2,1,0:T(8,128)(2,1)S(1)}, u32[]{:S(2)}) copy-start(bf16[3,360,128]{2,1,0:T(8,128)(2,1)S(1)} %collective-permute-done.24.refs_1_) | copy-start | bytes 829444
  217.6 18.2 %copy-start.2 = (bf16[3,360,128]{2,1,0:T(8,128)(2,1)}, bf16[3,360,128]{2,1,0:T(8,128)(2,1)S(1)}, u32[]{:S(2)}) copy-start(bf16[3,360,128]{2,1,0:T(8,128)(2,1)S(1)} %collective-permute-done.25.refs_2_) | copy-start | bytes 829444
  217.6 18.2 %copy-start.3 = (bf16[3,360,128]{2,1,0:T(8,128)(2,1)}, bf16[3,360,128]{2,1,0:T(8,128)(2,1)S(1)}, u32[]{:S(2)}) copy-start(bf16[3,360,128]{2,1,0:T(8,128)(2,1)S(1)} %collective-permute-done.26.refs_3_) | copy-start | bytes 829444
  217.6 39.3 %collective-permute-start.31 = (bf16[3,360,128]{2,1,0:T(8,128)(2,1)}, bf16[3,360,128]{2,1,0:T(8,128)(2,1)S(1)}, u32[]{:S(2)}, u32[]{:S(2)}) collective-permute-start(bf16[3,360,128]{2,1,0:T(8,128)(2,1)} %get-tuple-element.101), channel_id=1, source_target_pairs={{0,2},{1,3},{2,0},{3,1},{4,6},{5,7},{6,4},{7,5},{8,10},{9,11},{10,... | collective-permute-start | bytes 829448 | tf_op jit(solution)/shard_map/out2/ppermute | solution.py:313
  219.7 37.2 %collective-permute-start.32 = (bf16[3,360,128]{2,1,0:T(8,128)(2,1)}, bf16[3,360,128]{2,1,0:T(8,128)(2,1)S(1)}, u32[]{:S(2)}, u32[]{:S(2)}) collective-permute-start(bf16[3,360,128]{2,1,0:T(8,128)(2,1)} %get-tuple-element.102), channel_id=1, source_target_pairs={{0,3},{1,0},{2,1},{3,2},{4,7},{5,4},{6,5},{7,6},{8,11},{9,8},{10,9... | collective-permute-start | bytes 829448 | tf_op jit(solution)/shard_map/out2/ppermute | solution.py:313
  235.8 26.7 %collective-permute-start.27 = (bf16[3,360,128]{2,1,0:T(8,128)(2,1)}, bf16[3,360,128]{2,1,0:T(8,128)(2,1)S(1)}, u32[]{:S(2)}, u32[]{:S(2)}) collective-permute-start(bf16[3,360,128]{2,1,0:T(8,128)(2,1)} %get-tuple-element.97), channel_id=1, source_target_pairs={{0,1},{1,2},{2,3},{3,0},{4,5},{5,6},{6,7},{7,4},{8,9},{9,10},{10,1... | collective-permute-start | bytes 829448 | tf_op jit(solution)/shard_map/out3/ppermute | solution.py:313
  237.7 28.6 %collective-permute-start.28 = (bf16[3,360,128]{2,1,0:T(8,128)(2,1)}, bf16[3,360,128]{2,1,0:T(8,128)(2,1)S(1)}, u32[]{:S(2)}, u32[]{:S(2)}) collective-permute-start(bf16[3,360,128]{2,1,0:T(8,128)(2,1)} %get-tuple-element.98), channel_id=1, source_target_pairs={{0,2},{1,3},{2,0},{3,1},{4,6},{5,7},{6,4},{7,5},{8,10},{9,11},{10,... | collective-permute-start | bytes 829448 | tf_op jit(solution)/shard_map/out3/ppermute | solution.py:313
  237.7 6.2 %copy-start.4 = (bf16[3,360,128]{2,1,0:T(8,128)(2,1)}, bf16[3,360,128]{2,1,0:T(8,128)(2,1)S(1)}, u32[]{:S(2)}) copy-start(bf16[3,360,128]{2,1,0:T(8,128)(2,1)S(1)} %collective-permute-done.30.refs_1_) | copy-start | bytes 829444
  237.7 28.6 %collective-permute-start.29 = (bf16[3,360,128]{2,1,0:T(8,128)(2,1)}, bf16[3,360,128]{2,1,0:T(8,128)(2,1)S(1)}, u32[]{:S(2)}, u32[]{:S(2)}) collective-permute-start(bf16[3,360,128]{2,1,0:T(8,128)(2,1)} %get-tuple-element.99), channel_id=1, source_target_pairs={{0,3},{1,0},{2,1},{3,2},{4,7},{5,4},{6,5},{7,6},{8,11},{9,8},{10,9... | collective-permute-start | bytes 829448 | tf_op jit(solution)/shard_map/out3/ppermute | solution.py:313
  256.9 0.7 copy-start.5
  257.6 0.7 copy-start.6
  262.5 3.7 %copy-start.7 = (bf16[3,360,128]{2,1,0:T(8,128)(2,1)}, bf16[3,360,128]{2,1,0:T(8,128)(2,1)S(1)}, u32[]{:S(2)}) copy-start(bf16[3,360,128]{2,1,0:T(8,128)(2,1)S(1)} %collective-permute-done.27.refs_1_) | copy-start | bytes 829444
  266.2 0.7 copy-start.8
  266.2 0.8 copy-start.9

commit v3 on v2

--- a/solution.py
+++ b/solution.py
@@ -17,7 +17,7 @@
 
 
 def microseconds(count):
-    return pl.CostEstimate(flops=int(count * 1.15e8), bytes_accessed=1024, transcendentals=0)
+    return pl.CostEstimate(flops=int(count * 1.15e9), bytes_accessed=1024, transcendentals=0)
 
 
 def round_up(value, step):
@@ -78,9 +78,8 @@
         store(self.full, tail)
 
 
-def conv_kernel(packing, sources, rows, first_row, low, me_ref, *refs):
-    field_refs, (lon_ref, lat_ref), out_refs = refs[: -sources - 4], refs[-sources - 4 : -sources - 2], refs[-sources - 2 : -2]
-    base_ref, cells_ref = refs[-2:]
+def conv_kernel(packing, sources, rows, first_row, low, *refs):
+    *field_refs, lon_ref, lat_ref, out_ref, base_ref, cells_ref = refs
     width = field_refs[0].shape[2]
     held_rows, block, wide = base_ref.shape
     group = field_refs[0].shape[0]
@@ -90,7 +89,6 @@
         base_ref[held, :, 0:width] = field_ref[row].astype(jnp.float32)
         base_ref[held, :, width : width + BORDER] = after_ref[row].astype(jnp.float32)
         base_ref[held, :, wide - BORDER : wide] = before_ref[row].astype(jnp.float32)
-    me = me_ref[0]
     part = 16
 
     def some_channels(index, _):
@@ -104,76 +102,73 @@
                 if 0 <= held < held_rows:
                     term = lat[t] * base_ref[held, chans, :]
                     total = term if total is None else total + term
-            result = lon[KERNEL_TAPS // 2] * total
-            for t in range(KERNEL_TAPS):
-                turn = DILATION_STEP * (KERNEL_TAPS // 2 - t)
-                if turn:
-                    result = result + lon[t] * pltpu.roll(total, turn % wide, 1)
+            near = [total if turn == 0 else pltpu.roll(total, turn % wide, 1) for turn in (2, 0, -2)]
+            result = None
+            for a, turn in enumerate((6, 0, -6)):
+                term = lon[3 * a] * near[0] + lon[3 * a + 1] * near[1] + lon[3 * a + 2] * near[2]
+                term = pltpu.roll(term, turn % wide, 1) if turn else term
+                result = term if result is None else result + term
             receiver, row = divmod(out_row, rows)
-            shift = lax.rem(receiver + sources - me, sources)
-            cells_ref[shift, chans, row * width : (row + 1) * width] = result[:, 0:width]
+            cells_ref[receiver, chans, row * width : (row + 1) * width] = result[:, 0:width]
         return 0
 
     lax.fori_loop(0, block // part, some_channels, 0)
-    for shift in range(sources):
-        packing.store(out_refs[shift], 0, lambda i: cells_ref[shift, :, i * LANES : (i + 1) * LANES])
-
-
-def convolve(packing, me, sources, field, before, after, lon_taps, lat_taps, place, row_count):
+    for receiver in range(sources):
+        packing.store(out_ref.at[receiver], 0, lambda i: cells_ref[receiver, :, i * LANES : (i + 1) * LANES])
+
+
+def convolve(packing, sources, field, before, after, lon_taps, lat_taps, place, row_count):
     row_total, chan_count, width = field.shape
     block = packing.block
     wide = round_up(width + 2 * BORDER, LANES)
-    piece = jax.ShapeDtypeStruct((packing.blocks, packing.rows, LANES), jnp.bfloat16)
     reach = -(-BORDER // row_count)
-    places = range(max(0, place - reach), min(row_total // row_count, place + reach + 1))
+    places = range(max(0, place - reach), min(row_total // row_count, place + 1 + reach))
     specs, operands = [], []
     for near in places:
         for array in (field, before, after):
-            specs.append(pl.BlockSpec((row_count, block, array.shape[2]), lambda c, me, near=near: (near, c, 0)))
+            specs.append(pl.BlockSpec((row_count, block, array.shape[2]), lambda c, near=near: (near, c, 0)))
             operands.append(array)
-    taps = pl.BlockSpec((block, KERNEL_TAPS), lambda c, me: (c, 0))
+    taps = pl.BlockSpec((block, KERNEL_TAPS), lambda c: (c, 0))
     return pl.pallas_call(
         functools.partial(
             conv_kernel, packing, sources, row_count // sources, place * row_count, places[0] * row_count
         ),
-        grid_spec=pltpu.PrefetchScalarGridSpec(
-            num_scalar_prefetch=1,
-            grid=(packing.blocks,),
-            in_specs=[*specs, taps, taps],
-            out_specs=[pl.BlockSpec((1, packing.rows, LANES), lambda c, me: (c, 0, 0))] * sources,
-            scratch_shapes=[
-                pltpu.VMEM((len(places) * row_count, block, wide), jnp.float32),
-                pltpu.VMEM((sources, block, packing.wide), jnp.float32),
-            ],
-        ),
-        out_shape=[piece] * sources,
+        grid=(packing.blocks,),
+        in_specs=[*specs, taps, taps],
+        out_specs=pl.BlockSpec((sources, 1, packing.rows, LANES), lambda c: (0, c, 0, 0)),
+        out_shape=jax.ShapeDtypeStruct((sources, packing.blocks, packing.rows, LANES), jnp.bfloat16),
+        scratch_shapes=[
+            pltpu.VMEM((len(places) * row_count, block, wide), jnp.float32),
+            pltpu.VMEM((sources, block, packing.wide), jnp.float32),
+        ],
         compiler_params=PARAMS,
         cost_estimate=microseconds(12),
         name="conv",
-    )(me, *operands, lon_taps, lat_taps)
-
-
-def mlp_kernel(packing, sources, me_ref, *refs):
-    x_refs, (gain_ref, up_ref, down_ref) = refs[:sources], refs[sources : sources + 3]
-    out_refs, (values, normed, total) = refs[sources + 3 : -3], refs[-3:]
+    )(*operands, lon_taps, lat_taps)
+
+
+def mlp_kernel(packing, sources, counts, me_ref, *refs):
+    x_ref, gain_ref = refs[:2]
+    weight_refs = refs[2 : 2 + 2 * len(counts)]
+    out_refs, (values, normed, total) = refs[-sources - 3 : -3], refs[-3:]
     step = pl.program_id(0)
     me = me_ref[0]
     block = packing.block
     chan_count = packing.blocks * block
 
     def channels(owner, lead):
-        return pl.ds(pl.multiple_of(owner * chan_count + lead * block, SUBLANES), block)
+        start = owner * chan_count + lead * block
+        return pl.ds(start if isinstance(start, int) else pl.multiple_of(start, SUBLANES), block)
 
     @pl.when(step == 0)
     def _():
-        for shift in range(sources):
-            sender = lax.rem(me + sources - shift, sources)
+        for sender in range(sources):
             for lead in range(packing.blocks):
 
                 def put(i, piece, at=channels(sender, lead)):
                     values[at, i * LANES : (i + 1) * LANES] = piece
 
-                packing.load(x_refs[shift], lead, put)
+                packing.load(x_ref.at[sender], lead, put)
         as_float = values[...]
         center = jnp.mean(as_float, axis=0, keepdims=True)
         deviation = as_float - center
@@ -181,9 +176,28 @@
         normed[...] = (deviation * lax.rsqrt(spread_sq + 1e-06) * gain_ref[...]).astype(jnp.bfloat16)
         total[...] = jnp.zeros_like(total)
 
-    expanded = jnp.dot(up_ref[...], normed[...], preferred_element_type=jnp.float32)
-    hidden = (0.5 * expanded * (1.0 + lax.erf(expanded * 0.7071067811865476))).astype(jnp.bfloat16)
-    total[...] += jnp.dot(down_ref[...], hidden, preferred_element_type=jnp.float32)
+    first = 0
+    for index, count in enumerate(counts):
+
+        @pl.when(jnp.logical_and(step >= first, step < first + count))
+        def _(pair=weight_refs[2 * index : 2 * index + 2]):
+            hidden, down = [], []
+            for ref in pair:
+                whole = ref[...]
+                half = whole.shape[1] // 2
+                up_rows = whole[:, :half].reshape(-1, whole.shape[2])
+                expanded = jnp.dot(up_rows, normed[...], preferred_element_type=jnp.float32)
+                gelu = 0.5 * expanded * (1.0 + lax.erf(expanded * 0.7071067811865476))
+                hidden.append(gelu.astype(jnp.bfloat16))
+                down.append(whole[:, half:].reshape(-1, whole.shape[2]))
+            total[...] += lax.dot_general(
+                jnp.concatenate(down, axis=0),
+                jnp.concatenate(hidden, axis=0),
+                (((0,), (0,)), ((), ())),
+                preferred_element_type=jnp.float32,
+            )
+
+        first += count
 
     @pl.when(step == pl.num_programs(0) - 1)
     def _():
@@ -194,22 +208,31 @@
                 packing.store(out_refs[shift], lead, lambda i: total[at, i * LANES : (i + 1) * LANES])
 
 
-def mlp(packing, me, pieces, gain, up_all, down_all):
-    sources = len(pieces)
-    width_all, hidden_total = down_all.shape
-    block = 512
-    whole = pl.BlockSpec(pieces[0].shape, lambda h, me: (0, 0, 0))
+def mlp(packing, me, by_cell, gain, weights):
+    sources = by_cell.shape[0]
+    width_all = gain.shape[0]
+    rows = weights[0].shape[1]
+    group = 1
+    while rows * group < 384 and weights[0].shape[0] % (2 * group) == 0:
+        group *= 2
+    counts = [held.shape[0] // group for held in weights[::2]]
+    starts = [sum(counts[:i]) for i in range(len(counts))]
+    specs = []
+    for start, count in zip(starts, counts):
+        spec = pl.BlockSpec(
+            (group, rows, width_all),
+            lambda h, me, start=start, count=count: (jnp.clip(h - start, 0, count - 1), 0, 0),
+        )
+        specs += [spec, spec]
+    shape = by_cell.shape[1:]
+    whole = pl.BlockSpec(shape, lambda h, me: (0, 0, 0))
+    cells = pl.BlockSpec(by_cell.shape, lambda h, me: (0, 0, 0, 0))
     return pl.pallas_call(
-        functools.partial(mlp_kernel, packing, sources),
+        functools.partial(mlp_kernel, packing, sources, counts),
         grid_spec=pltpu.PrefetchScalarGridSpec(
             num_scalar_prefetch=1,
-            grid=(hidden_total // block,),
-            in_specs=[whole] * sources
-            + [
-                pl.BlockSpec((width_all, 1), lambda h, me: (0, 0)),
-                pl.BlockSpec((block, width_all), lambda h, me: (h, 0)),
-                pl.BlockSpec((width_all, block), lambda h, me: (0, h)),
-            ],
+            grid=(sum(counts),),
+            in_specs=[cells, pl.BlockSpec((width_all, 1), lambda h, me: (0, 0)), *specs],
             out_specs=[whole] * sources,
             scratch_shapes=[
                 pltpu.VMEM((width_all, packing.wide), jnp.float32),
@@ -217,11 +240,11 @@
                 pltpu.VMEM((width_all, packing.wide), jnp.float32),
             ],
         ),
-        out_shape=[jax.ShapeDtypeStruct(pieces[0].shape, jnp.bfloat16)] * sources,
+        out_shape=[jax.ShapeDtypeStruct(shape, jnp.bfloat16)] * sources,
         compiler_params=PARAMS,
-        cost_estimate=microseconds(13),
+        cost_estimate=microseconds(1),
         name="mlp",
-    )(me, *pieces, gain, up_all, down_all)
+    )(me, by_cell, gain, *weights)
 
 
 def add_kernel(packing, sources, me_ref, *refs):
@@ -273,41 +296,6 @@
     )(*operands)
 
 
-def prepare_kernel(held_ref, received_ref, *refs):
-    up_ref, down_ref = refs[-2:]
-    half = held_ref.shape[1] // 2
-    up_ref[0:half] = held_ref[0, 0:half]
-    up_ref[half:] = received_ref[0, 0:half]
-    down_ref[:, 0:half] = held_ref[0, half:].T
-    down_ref[:, half:] = received_ref[0, half:].T
-
-
-def prepare(held, received, total, done, place):
-    count, rows, width = held.shape
-    if rows % LANES:
-        both = jnp.concatenate([held, received], axis=0)
-        half = rows // 2
-        return both[:, :half].reshape(total, width), both[:, half:].reshape(total, width).T
-    source = pl.BlockSpec((1, rows, width), lambda i: (i, 0, 0))
-    return pl.pallas_call(
-        prepare_kernel,
-        grid=(count,),
-        in_specs=[source, source] + [pl.BlockSpec(memory_space=pl.ANY)] * len(done),
-        out_specs=[
-            pl.BlockSpec((rows, width), lambda i: (place + i, 0)),
-            pl.BlockSpec((width, rows), lambda i: (0, place + i)),
-        ],
-        out_shape=[
-            jax.ShapeDtypeStruct((total, width), held.dtype),
-            jax.ShapeDtypeStruct((width, total), held.dtype),
-        ],
-        input_output_aliases={2: 0, 3: 1} if done else {},
-        compiler_params=PARAMS,
-        cost_estimate=microseconds(count),
-        name="prepare",
-    )(held, received, *done)
-
-
 def shifted(array, axis, shift):
     count = lax.axis_size(axis)
     return lax.ppermute(array, axis, [(i, (i + shift) % count) for i in range(count)])
@@ -315,6 +303,37 @@
 
 def exchanged(array, axis, bit):
     return lax.ppermute(array, axis, [(i, i ^ bit) for i in range(lax.axis_size(axis))])
+
+
+def stack_kernel(counts, *refs):
+    *in_refs, out_ref = refs
+    step, first = pl.program_id(0), 0
+    for ref, count in zip(in_refs, counts):
+
+        @pl.when(jnp.logical_and(step >= first, step < first + count))
+        def _(ref=ref):
+            out_ref[...] = ref[...]
+
+        first += count
+
+
+def stacked(*arrays):
+    counts = [array.shape[0] for array in arrays]
+    block = (1, *arrays[0].shape[1:])
+    specs = [
+        pl.BlockSpec(block, lambda i, start=sum(counts[:k]), count=count: (jnp.clip(i - start, 0, count - 1), 0, 0))
+        for k, count in enumerate(counts)
+    ]
+    return pl.pallas_call(
+        functools.partial(stack_kernel, counts),
+        grid=(sum(counts),),
+        in_specs=specs,
+        out_specs=pl.BlockSpec(block, lambda i: (i, 0, 0)),
+        out_shape=jax.ShapeDtypeStruct((sum(counts), *block[1:]), arrays[0].dtype),
+        compiler_params=PARAMS,
+        cost_estimate=microseconds(1),
+        name="stack",
+    )(*arrays)
 
 
 def after_all(arrays, *others):
@@ -348,49 +367,49 @@
     after = jnp.transpose(after, (1, 0, 2))
     lon, lat = lon_taps.T, latitude_taps.T
     rows = row_total // CHUNKS
-    hidden_total = sources * tiles * up_weight.shape[1]
     packing = Packing(chan_count, rows // sources * width)
 
-    def spread(chunk):
-        pieces = convolve(packing, me, sources, field, before, after, lon, lat, chunk, rows)
-        with jax.named_scope(f"in{chunk}"):
-            return [pieces[0]] + [shifted(pieces[s], "chan", s) for s in range(1, sources)]
-
-    by_cell = [spread(0)]
-    lon, far, near, across = after_all((lon, far, near, across), by_cell[0][0])
+    def spread(place):
+        spatial = convolve(packing, sources, field, before, after, lon, lat, place, rows)
+        with jax.named_scope(f"in{place}"):
+            return spatial, lax.all_to_all(spatial, "chan", split_axis=0, concat_axis=0, tiled=True)
+
+    by_cell = []
+    spatial, cells = spread(0)
+    by_cell.append(cells)
+    lon, far, near, across = after_all((lon, far, near, across), spatial)
     with jax.named_scope("wz1"):
         rest = [exchanged(piece, "chan", 1) for piece in far[1:]]
-    by_cell.append(spread(1))
-    lon, rest = after_all((lon, rest), by_cell[1][0], by_cell[0][1:])
-    others = jnp.concatenate([*far[1:], near, *rest], axis=0)
+    spatial, cells = spread(1)
+    by_cell.append(cells)
+    lon, rest, across = after_all((lon, rest, across), spatial, by_cell[0])
+    others = stacked(*far[1:], near, *rest)
     with jax.named_scope("wx1"):
         others_across = exchanged(others, "tile", bits[0])
-    by_cell.append(spread(2))
-    lon, others, across = after_all((lon, others, across), by_cell[2][0], by_cell[1][1:])
-    if len(bits) == 1:
-        held = jnp.concatenate([shard, others, across], axis=0)
-        with jax.named_scope("wc0"):
-            received = exchanged(held, "tile", 1)
-    by_cell.append(spread(3))
-    others_across = after_all(others_across, by_cell[3][:2], by_cell[2][1:])
-    weights, place = (), 0
-    if len(bits) == 1:
-        weights, place = prepare(held, received, hidden_total, (), 0), held.shape[0]
-        held = others_across
-    else:
-        held = jnp.concatenate([shard, others, across, others_across], axis=0)
-        for bit in bits[1:]:
-            held = jnp.concatenate([held, exchanged(held, "tile", bit)], axis=0)
+    spatial, cells = spread(2)
+    by_cell.append(cells)
+    lon, others = after_all((lon, others), spatial, by_cell[1])
+    held = stacked(shard, across, others)
+    for bit in bits[1:]:
+        held = stacked(held, exchanged(held, "tile", bit))
+    with jax.named_scope("wc0"):
+        received = exchanged(held, "tile", 1)
+    spatial, cells = spread(3)
+    by_cell.append(cells)
+    others_across = after_all(others_across, spatial)
+    for bit in bits[1:]:
+        others_across = stacked(others_across, exchanged(others_across, "tile", bit))
     with jax.named_scope("wc1"):
-        received = exchanged(held, "tile", 1)
-    up_all, down_all = prepare(held, received, hidden_total, weights, place)
+        others_received = exchanged(others_across, "tile", 1)
+    weights = [held, received, others_across, others_received]
     gain = norm_gain[:, None]
+    me = after_all(me, by_cell[2])
     updates = []
     for chunk in range(CHUNKS):
-        pieces = mlp(packing, me, by_cell[chunk], gain, up_all, down_all)
+        pieces = mlp(packing, me, by_cell[chunk], gain, weights)
         with jax.named_scope(f"out{chunk}"):
             updates.append([pieces[0]] + [shifted(pieces[s], "chan", s) for s in range(1, sources)])
-        gain = after_all(gain, pieces[0], updates[chunk - 1][1:] if chunk else by_cell[CHUNKS - 1][1:])
+        me = after_all(me, pieces[0], updates[chunk - 1][1:] if chunk else by_cell[CHUNKS - 1])
     mixed = None
     for chunk in range(CHUNKS):
         mixed = add_rows(packing, me, updates[chunk], weather, mixed, chunk, rows)

time: 272 us -> 263 us (0.967)
  Pallas kernels: 138 us -> 128 us
  starting transfers between devices: 36.7 us -> 46.4 us
  local copies, waits for them, and re-layouts: 27.6 us -> 21.4 us
  other arithmetic: 4.03 us -> 0.04 us
    all_to_all x0 -> x4, waiting for transfers between devices: none -> 43.4 us  [spread(): lax.all_to_all(spatial, 'chan', split_axis=0, concat_axis=0, tiled=True)]
    ppermute x26 -> x14, waiting for transfers between devices: 64.5 us -> 22.1 us  [shifted(): lax.ppermute(array, axis, [(i, (i + shift) % count) for i in range(count)])]
    all_to_all x0 -> x4, starting transfers between devices: none -> 26.1 us  [spread(): lax.all_to_all(spatial, 'chan', split_axis=0, concat_axis=0, tiled=True)]
    ppermute x26 -> x14, starting transfers between devices: 32.7 us -> 15.3 us  [shifted(): lax.ppermute(array, axis, [(i, (i + shift) % count) for i in range(count)])]
    pallas_call x4, Pallas kernels: 55.9 us -> 40.6 us  [convolve(): pl.pallas_call(functools.partial(conv_kernel, packing, sources, row_count...]
    pallas_call x6, Pallas kernels: 65.4 us -> 69.9 us  [the longest x4 62.1 us: mlp(): pl.pallas_call(functools.partial(mlp_kernel, packing, sources, counts), g...]
    optimization_barrier x3 -> x0, local copies, waits for them, and re-layouts: 2.85 us -> none  [after_all(): return lax.optimization_barrier((arrays, others))[0]]
    unnamed x59 -> x51, local copies, waits for them, and re-layouts: 17.3 us -> 14.8 us
  transfers between devices with their start and end apart: 33 -> 25, of which waited for: 9 -> 7; matrix products, arithmetic and copies ran while one was open for 9% -> 5% of each run, Pallas kernels for 49% -> 47%
where the time goes in v3:
time: 263 us; the launch traced here: 262 us
  Pallas kernels  128 us (49%)
  waiting for transfers between devices  66.6 us (25%)
  starting transfers between devices  46.4 us (18%)
  local copies, waits for them, and re-layouts  21.4 us (8%)
    pallas_call x4, Pallas kernels, mlp(): pl.pallas_call(functools.partial(mlp_kernel, packing, sources, counts), g...  62.1 us
    all_to_all x4, waiting for transfers between devices, spread(): lax.all_to_all(spatial, 'chan', split_axis=0, concat_axis=0, tiled=True)  43.4 us
    pallas_call x4, Pallas kernels, convolve(): pl.pallas_call(functools.partial(conv_kernel, packing, sources, row_count...  40.6 us
    all_to_all x4, starting transfers between devices, spread(): lax.all_to_all(spatial, 'chan', split_axis=0, concat_axis=0, tiled=True)  26.1 us
    ppermute x14, waiting for transfers between devices, shifted(): lax.ppermute(array, axis, [(i, (i + shift) % count) for i in range(count)])  22.1 us
    pallas_call x4, Pallas kernels, add_rows(): pl.pallas_call(functools.partial(add_kernel, packing, sources), grid_spec...  17 us
    ppermute x14, starting transfers between devices, shifted(): lax.ppermute(array, axis, [(i, (i + shift) % count) for i in range(count)])  15.3 us
    unnamed x51, local copies, waits for them, and re-layouts  14.8 us
  transfers between devices with their start and end apart: 25, of which 7 were waited for; matrix products, arithmetic and copies ran while one was open for 5% of the time, Pallas kernels for 47%

profile of v3, /device:TPU:24, one launch (start us, length us, event | category | flops | bytes accessed | tf_op | source)
XLA Modules:
  0.0 262.3 jit_solution(18153358610208005751)
XLA Ops:
  0.0 2.6 fusion
  2.6 0.0 copy-start.5
  2.6 1.9 copy.35
  4.5 0.0 collective-permute-start
  4.5 1.3 copy.36
  5.8 1.8 collective-permute-start.1
  7.7 0.0 copy-start.7
  7.7 0.0 copy-start.8
  7.7 0.4 collective-permute-start.2
  8.1 0.2 collective-permute-start.3
  8.3 1.7 collective-permute-start.4
  10.0 6.2 %copy.38 = bf16[192,32,360]{2,0,1:T(8,128)(2,1)} copy(bf16[192,32,360]{2,1,0:T(8,128)(2,1)} %refs_4_.7) | data formatting | bytes 8847360 | tf_op args[0]
  16.3 0.8 copy.30
  17.0 0.8 copy.29
  17.8 0.0 collective-permute-done
  17.8 1.6 copy.26
  19.4 1.5 copy.28
  20.8 9.8 %conv.4 = bf16[4,3,360,128]{3,2,1,0:T(8,128)(2,1)} custom-call(bf16[32,192,360]{2,1,0:T(8,128)(2,1)} %bitcast.12, bf16[32,192,8]{2,1,0:T(8,128)(2,1)} %bitcast.22, bf16[32,192,8]{2,1,0:T(8,128)(2,1)} %bitcast.32, bf16[32,192,360]{2,1,0:T(8,128)(2,1)} %bitcast.13, bf16[32,192,8]{2,1,0:T(8,128)(2,1)} %bitcast.23, bf16[32,192,8]{2,1,0:T(8,128)(2,1)} %bitcast.33, ...), custom_call_target="tpu_custom_call" | custom-call | flops 13799999488 | bytes 1024 | tf_op jit(solution)/shard_map/conv/pallas_call | solution.py:132
  30.6 7.1 %all-to-all-start = ((bf16[4,3,360,128]{3,2,1,0:T(8,128)(2,1)}), bf16[4,3,360,128]{3,2,1,0:T(8,128)(2,1)S(1)}, u32[]{:S(2)}, u32[]{:S(2)}) async-start(bf16[4,3,360,128]{3,2,1,0:T(8,128)(2,1)} %conv.4), calls=%async_computation | async-start | bytes 2211840 | tf_op jit(solution)/shard_map/in0/all_to_all | solution.py:375
  37.7 0.0 collective-permute-done.2.refs_0_
  37.7 0.0 collective-permute-done.3.refs_1_
  37.7 0.0 collective-permute-done.4.refs_1_
  37.8 0.6 collective-permute-start.5
  38.4 10.4 %conv.5 = bf16[4,3,360,128]{3,2,1,0:T(8,128)(2,1)} custom-call(bf16[32,192,360]{2,1,0:T(8,128)(2,1)} %bitcast.14, bf16[32,192,8]{2,1,0:T(8,128)(2,1)} %bitcast.24, bf16[32,192,8]{2,1,0:T(8,128)(2,1)} %bitcast.34, bf16[32,192,360]{2,1,0:T(8,128)(2,1)} %bitcast.15, bf16[32,192,8]{2,1,0:T(8,128)(2,1)} %bitcast.25, bf16[32,192,8]{2,1,0:T(8,128)(2,1)} %bitcast.35, ...), custom_call_target="tpu_custom_call" | custom-call | flops 13799999488 | bytes 1024 | tf_op jit(solution)/shard_map/conv/pallas_call | solution.py:132
  48.8 12.2 %all-to-all-done.refs_0_ = bf16[4,3,360,128]{3,2,1,0:T(8,128)(2,1)S(1)} async-done(((bf16[4,3,360,128]{3,2,1,0:T(8,128)(2,1)}), bf16[4,3,360,128]{3,2,1,0:T(8,128)(2,1)S(1)}, u32[]{:S(2)}, u32[]{:S(2)}) %all-to-all-start) | async-done | bytes 1105952 | tf_op jit(solution)/shard_map/in0/all_to_all | solution.py:375
  61.0 5.9 %all-to-all-start.2 = ((bf16[4,3,360,128]{3,2,1,0:T(8,128)(2,1)}), bf16[4,3,360,128]{3,2,1,0:T(8,128)(2,1)S(1)}, u32[]{:S(2)}, u32[]{:S(2)}) async-start(bf16[4,3,360,128]{3,2,1,0:T(8,128)(2,1)} %conv.5), calls=%async_computation.2 | async-start | bytes 2211840 | tf_op jit(solution)/shard_map/in1/all_to_all | solution.py:375
  66.8 1.1 collective-permute-done.5.refs_2_
  67.9 0.8 copy-done.10
  68.8 3.2 %stack.2.refs_2_ = bf16[3,384,768]{2,1,0:T(8,128)(2,1)} custom-call(bf16[1,384,768]{2,1,0:T(8,128)(2,1)} %collective-permute-done.2.refs_0_, bf16[1,384,768]{2,1,0:T(8,128)(2,1)} %collective-permute-done.3.refs_1_, bf16[1,384,768]{2,1,0:T(8,128)(2,1)} %copy-done.10), custom_call_target="tpu_custom_call" | custom-call | flops 1150000000 | bytes 1024 | tf_op jit(solution)/shard_map/stack/pallas_call | solution.py:327
  72.0 1.5 collective-permute-start.7
  73.4 10.4 %conv.6 = bf16[4,3,360,128]{3,2,1,0:T(8,128)(2,1)} custom-call(bf16[32,192,360]{2,1,0:T(8,128)(2,1)} %bitcast.17, bf16[32,192,8]{2,1,0:T(8,128)(2,1)} %bitcast.27, bf16[32,192,8]{2,1,0:T(8,128)(2,1)} %bitcast.37, bf16[32,192,360]{2,1,0:T(8,128)(2,1)} %bitcast.18, bf16[32,192,8]{2,1,0:T(8,128)(2,1)} %bitcast.28, bf16[32,192,8]{2,1,0:T(8,128)(2,1)} %bitcast.38, ...), custom_call_target="tpu_custom_call" | custom-call | flops 13799999488 | bytes 1024 | tf_op jit(solution)/shard_map/conv/pallas_call | solution.py:132
  83.8 7.0 %all-to-all-done.2.refs_0_ = bf16[4,3,360,128]{3,2,1,0:T(8,128)(2,1)S(1)} async-done(((bf16[4,3,360,128]{3,2,1,0:T(8,128)(2,1)}), bf16[4,3,360,128]{3,2,1,0:T(8,128)(2,1)S(1)}, u32[]{:S(2)}, u32[]{:S(2)}) %all-to-all-start.2) | async-done | bytes 1105952 | tf_op jit(solution)/shard_map/in1/all_to_all | solution.py:375
  90.9 6.6 %all-to-all-start.1 = ((bf16[4,3,360,128]{3,2,1,0:T(8,128)(2,1)}), bf16[4,3,360,128]{3,2,1,0:T(8,128)(2,1)}, u32[]{:S(2)}, u32[]{:S(2)}) async-start(bf16[4,3,360,128]{3,2,1,0:T(8,128)(2,1)} %conv.6), calls=%async_computation.1 | async-start | bytes 2211840 | tf_op jit(solution)/shard_map/in2/all_to_all | solution.py:375
  97.4 4.7 %stack.3.refs_2_ = bf16[5,384,768]{2,1,0:T(8,128)(2,1)} custom-call(bf16[1,384,768]{2,1,0:T(8,128)(2,1)} %copy-done.3, bf16[1,384,768]{2,1,0:T(8,128)(2,1)} %copy-done.4, bf16[3,384,768]{2,1,0:T(8,128)(2,1)} %stack.2.refs_2_), custom_call_target="tpu_custom_call" | custom-call | flops 1150000000 | bytes 1024 | tf_op jit(solution)/shard_map/stack/pallas_call | solution.py:327
  102.1 10.0 %conv.7 = bf16[4,3,360,128]{3,2,1,0:T(8,128)(2,1)} custom-call(bf16[32,192,360]{2,1,0:T(8,128)(2,1)} %bitcast.20, bf16[32,192,8]{2,1,0:T(8,128)(2,1)} %bitcast.30, bf16[32,192,8]{2,1,0:T(8,128)(2,1)} %bitcast.40, bf16[32,192,360]{2,1,0:T(8,128)(2,1)} %bitcast.21, bf16[32,192,8]{2,1,0:T(8,128)(2,1)} %bitcast.31, bf16[32,192,8]{2,1,0:T(8,128)(2,1)} %bitcast.41, ...), custom_call_target="tpu_custom_call" | custom-call | flops 13799999488 | bytes 1024 | tf_op jit(solution)/shard_map/conv/pallas_call | solution.py:132
  112.1 0.6 collective-permute-start.8
  112.7 8.5 %all-to-all-done.1.refs_0_ = bf16[4,3,360,128]{3,2,1,0:T(8,128)(2,1)} async-done(((bf16[4,3,360,128]{3,2,1,0:T(8,128)(2,1)}), bf16[4,3,360,128]{3,2,1,0:T(8,128)(2,1)}, u32[]{:S(2)}, u32[]{:S(2)}) %all-to-all-start.1) | async-done | bytes 1105952 | tf_op jit(solution)/shard_map/in2/all_to_all | solution.py:375
  121.1 6.6 %all-to-all-start.3 = ((bf16[4,3,360,128]{3,2,1,0:T(8,128)(2,1)}), bf16[4,3,360,128]{3,2,1,0:T(8,128)(2,1)}, u32[]{:S(2)}, u32[]{:S(2)}) async-start(bf16[4,3,360,128]{3,2,1,0:T(8,128)(2,1)} %conv.7), calls=%async_computation.3 | async-start | bytes 2211840 | tf_op jit(solution)/shard_map/in3/all_to_all | solution.py:375
  127.7 0.9 broadcast_in_dim.12.refs_1_
  128.7 1.6 copy-done
  130.3 15.4 %mlp.4 = (bf16[3,360,128]{2,1,0:T(8,128)(2,1)}, bf16[3,360,128]{2,1,0:T(8,128)(2,1)}, bf16[3,360,128]{2,1,0:T(8,128)(2,1)}, bf16[3,360,128]{2,1,0:T(8,128)(2,1)}) custom-call(s32[1]{0:T(128)} %bitcast.me_ref, bf16[4,3,360,128]{3,2,1,0:T(8,128)(2,1)} %copy-done.1, f32[768,1]{1,0:T(8,128)} %broadcast_in_dim.12.refs_1_, bf16[5,384,768]{2,1,0:T(8,128)(2,1)} %stack.3.refs_2_, ...), custom_call_target="tpu_custom_call" | custom-call | flops 1150000000 | bytes 1024 | tf_op jit(solution)/shard_map/mlp/pallas_call | solution.py:230
  145.7 0.6 collective-permute-start.10
  146.3 0.2 collective-permute-start.11
  146.5 3.6 %collective-permute-start.9 = (bf16[3,360,128]{2,1,0:T(8,128)(2,1)}, bf16[3,360,128]{2,1,0:T(8,128)(2,1)S(1)}, u32[]{:S(2)}, u32[]{:S(2)}) collective-permute-start(bf16[3,360,128]{2,1,0:T(8,128)(2,1)} %get-tuple-element.50), channel_id=1, source_target_pairs={{0,1},{1,2},{2,3},{3,0},{4,5},{5,6},{6,7},{7,4},{8,9},{9,10},{10,1... | collective-permute-start | bytes 829448 | tf_op jit(solution)/shard_map/out0/ppermute | solution.py:301
  150.1 15.7 %all-to-all-done.3.refs_0_ = bf16[4,3,360,128]{3,2,1,0:T(8,128)(2,1)} async-done(((bf16[4,3,360,128]{3,2,1,0:T(8,128)(2,1)}), bf16[4,3,360,128]{3,2,1,0:T(8,128)(2,1)}, u32[]{:S(2)}, u32[]{:S(2)}) %all-to-all-start.3) | async-done | bytes 1105952 | tf_op jit(solution)/shard_map/in3/all_to_all | solution.py:375
  165.8 15.4 %mlp.5 = (bf16[3,360,128]{2,1,0:T(8,128)(2,1)}, bf16[3,360,128]{2,1,0:T(8,128)(2,1)}, bf16[3,360,128]{2,1,0:T(8,128)(2,1)}, bf16[3,360,128]{2,1,0:T(8,128)(2,1)}) custom-call(s32[1]{0:T(128)} %bitcast.me_ref, bf16[4,3,360,128]{3,2,1,0:T(8,128)(2,1)} %copy-done.2, f32[768,1]{1,0:T(8,128)} %broadcast_in_dim.12.refs_1_, bf16[5,384,768]{2,1,0:T(8,128)(2,1)} %stack.3.refs_2_, ...), custom_call_target="tpu_custom_call" | custom-call | flops 1150000000 | bytes 1024 | tf_op jit(solution)/shard_map/mlp/pallas_call | solution.py:230
  181.2 0.1 collective-permute-start.13
  181.3 2.0 collective-permute-start.14
  183.3 15.6 %mlp.6 = (bf16[3,360,128]{2,1,0:T(8,128)(2,1)}, bf16[3,360,128]{2,1,0:T(8,128)(2,1)}, bf16[3,360,128]{2,1,0:T(8,128)(2,1)}, bf16[3,360,128]{2,1,0:T(8,128)(2,1)}) custom-call(s32[1]{0:T(128)} %bitcast.me_ref, bf16[4,3,360,128]{3,2,1,0:T(8,128)(2,1)} %all-to-all-done.1.refs_0_, f32[768,1]{1,0:T(8,128)} %broadcast_in_dim.12.refs_1_, ...), custom_call_target="tpu_custom_call" | custom-call | flops 1150000000 | bytes 1024 | tf_op jit(solution)/shard_map/mlp/pallas_call | solution.py:230
  199.0 2.4 collective-permute-start.15
  201.4 0.6 collective-permute-start.16
  202.0 1.9 collective-permute-start.17
  203.9 12.7 %collective-permute-done.13.refs_2_ = bf16[3,360,128]{2,1,0:T(8,128)(2,1)S(1)} collective-permute-done((bf16[3,360,128]{2,1,0:T(8,128)(2,1)}, bf16[3,360,128]{2,1,0:T(8,128)(2,1)S(1)}, u32[]{:S(2)}, u32[]{:S(2)}) %collective-permute-start.13) | collective-permute-done | bytes 276512 | tf_op jit(solution)/shard_map/out1/ppermute | solution.py:301
  216.6 15.6 %mlp.7 = (bf16[3,360,128]{2,1,0:T(8,128)(2,1)}, bf16[3,360,128]{2,1,0:T(8,128)(2,1)}, bf16[3,360,128]{2,1,0:T(8,128)(2,1)}, bf16[3,360,128]{2,1,0:T(8,128)(2,1)}) custom-call(s32[1]{0:T(128)} %bitcast.me_ref, bf16[4,3,360,128]{3,2,1,0:T(8,128)(2,1)} %all-to-all-done.3.refs_0_, f32[768,1]{1,0:T(8,128)} %broadcast_in_dim.12.refs_1_, ...), custom_call_target="tpu_custom_call" | custom-call | flops 1150000000 | bytes 1024 | tf_op jit(solution)/shard_map/mlp/pallas_call | solution.py:230
  232.3 0.1 collective-permute-start.18
  232.4 0.1 collective-permute-start.19
  232.5 2.0 collective-permute-start.20
  234.5 4.4 %add.4.refs_5_ = bf16[192,32,360]{2,1,0:T(8,128)(2,1)} custom-call(s32[1]{0:T(128)} %bitcast.me_ref, bf16[3,360,128]{2,1,0:T(8,128)(2,1)} %get-tuple-element.47.refs_0_, bf16[3,360,128]{2,1,0:T(8,128)(2,1)} %copy-done.13, bf16[3,360,128]{2,1,0:T(8,128)(2,1)} %copy-done.11, bf16[3,360,128]{2,1,0:T(8,128)(2,1)} %copy-done.12, bf16[192,32,360]{2,1,0:T(8,128)(2,1)} %refs_4_.7), custom_call_target="tpu_custom_call" | custom-call | flops 4600000000 | bytes 1024 | tf_op jit(solution)/shard_map/add/pallas_call | solution.py:279
  238.9 4.2 %add.5.refs_5_ = bf16[192,32,360]{2,1,0:T(8,128)(2,1)} custom-call(s32[1]{0:T(128)} %bitcast.me_ref, bf16[3,360,128]{2,1,0:T(8,128)(2,1)} %get-tuple-element.49.refs_0_, bf16[3,360,128]{2,1,0:T(8,128)(2,1)} %copy-done.14, bf16[3,360,128]{2,1,0:T(8,128)(2,1)} %copy-done.15, bf16[3,360,128]{2,1,0:T(8,128)(2,1)} %copy-done.16, ...), custom_call_target="tpu_custom_call", output_to_operand_aliasing={{}: (6, {})} | custom-call | flops 4600000000 | bytes 1024 | tf_op jit(solution)/shard_map/add/pallas_call | solution.py:279
  243.1 4.2 %add.6.refs_5_ = bf16[192,32,360]{2,1,0:T(8,128)(2,1)} custom-call(s32[1]{0:T(128)} %bitcast.me_ref, bf16[3,360,128]{2,1,0:T(8,128)(2,1)} %get-tuple-element.54.refs_0_, bf16[3,360,128]{2,1,0:T(8,128)(2,1)} %copy-done.17, bf16[3,360,128]{2,1,0:T(8,128)(2,1)} %copy-done.18, bf16[3,360,128]{2,1,0:T(8,128)(2,1)} %copy-done.19, ...), custom_call_target="tpu_custom_call", output_to_operand_aliasing={{}: (6, {})} | custom-call | flops 4600000000 | bytes 1024 | tf_op jit(solution)/shard_map/add/pallas_call | solution.py:279
  247.3 9.4 %collective-permute-done.19.refs_2_ = bf16[3,360,128]{2,1,0:T(8,128)(2,1)S(1)} collective-permute-done((bf16[3,360,128]{2,1,0:T(8,128)(2,1)}, bf16[3,360,128]{2,1,0:T(8,128)(2,1)S(1)}, u32[]{:S(2)}, u32[]{:S(2)}) %collective-permute-start.19) | collective-permute-done | bytes 276512 | tf_op jit(solution)/shard_map/out3/ppermute | solution.py:301
  256.7 0.7 copy-done.21
  257.4 0.7 copy-done.22
  258.1 4.2 %add.7 = bf16[192,32,360]{2,1,0:T(8,128)(2,1)} custom-call(s32[1]{0:T(128)} %bitcast.me_ref, bf16[3,360,128]{2,1,0:T(8,128)(2,1)} %get-tuple-element.59.refs_0_, bf16[3,360,128]{2,1,0:T(8,128)(2,1)} %copy-done.20, bf16[3,360,128]{2,1,0:T(8,128)(2,1)} %copy-done.21, bf16[3,360,128]{2,1,0:T(8,128)(2,1)} %copy-done.22, ...), custom_call_target="tpu_custom_call", output_to_operand_aliasing={{}: (6, {})} | custom-call | flops 4600000000 | bytes 1024 | tf_op jit(solution)/shard_map/add/pallas_call | solution.py:279
  (56 shorter events, 0.2 us)
Async XLA Ops:
  2.6 5.0 %copy-start.5 = (bf16[768,192]{0,1:T(8,128)(2,1)S(1)}, bf16[768,192]{0,1:T(8,128)(2,1)}, u32[]{:S(2)}) copy-start(bf16[768,192]{0,1:T(8,128)(2,1)} %param.11) | copy-start | bytes 884740
  4.5 3.1 %copy-start.6 = (bf16[768,192]{0,1:T(8,128)(2,1)S(1)}, bf16[768,192]{0,1:T(8,128)(2,1)}, u32[]{:S(2)}) copy-start(bf16[768,192]{0,1:T(8,128)(2,1)} %param.10) | copy-start | bytes 884740
  4.5 13.3 %collective-permute-start = (bf16[192,32,8]{0,2,1:T(8,128)(2,1)}, bf16[192,32,8]{0,2,1:T(8,128)(2,1)S(1)}, u32[]{:S(2)}, u32[]{:S(2)}) collective-permute-start(bf16[192,32,8]{0,2,1:T(8,128)(2,1)} %copy.35), channel_id=1, source_target_pairs={{0,4},{4,8},{8,12},{12,0},{1,5},{5,9},{9,13},{13,1},{2,6},{6,10},{... | collective-permute-start | bytes 294920 | tf_op jit(solution)/shard_map/halo/ppermute | solution.py:301
  5.8 13.5 %collective-permute-start.1 = (bf16[192,32,8]{0,2,1:T(8,128)(2,1)S(1)}, bf16[192,32,8]{0,2,1:T(8,128)(2,1)S(1)}, u32[]{:S(2)}, u32[]{:S(2)}) collective-permute-start(bf16[192,32,8]{0,2,1:T(8,128)(2,1)S(1)} %copy.36), channel_id=1, source_target_pairs={{0,12},{4,0},{8,4},{12,8},{1,13},{5,1},{9,5},{13,9},{2,14},{6,2},{... | collective-permute-start | bytes 294920 | tf_op jit(solution)/shard_map/halo/ppermute | solution.py:301
  7.7 8.6 %copy-start.3 = (bf16[1,384,768]{2,1,0:T(8,128)(2,1)}, bf16[1,384,768]{2,1,0:T(8,128)(2,1)S(1)}, u32[]{:S(2)}) copy-start(bf16[1,384,768]{2,1,0:T(8,128)(2,1)S(1)} %maximum_bitcast_fusion.refs_0_) | copy-start | bytes 1769476
  7.7 8.6 %copy-start.7 = (f32[9,192]{1,0:T(8,128)S(1)}, f32[9,192]{1,0:T(8,128)}, u32[]{:S(2)}) copy-start(f32[9,192]{1,0:T(8,128)} %param.8) | copy-start | bytes 20740
  7.7 9.4 %copy-start.8 = (f32[9,192]{1,0:T(8,128)S(1)}, f32[9,192]{1,0:T(8,128)}, u32[]{:S(2)}) copy-start(f32[9,192]{1,0:T(8,128)} %param.7) | copy-start | bytes 20740
  7.7 30.1 %collective-permute-start.2 = (bf16[1,384,768]{2,1,0:T(8,128)(2,1)S(1)}, bf16[1,384,768]{2,1,0:T(8,128)(2,1)}, u32[]{:S(2)}, u32[]{:S(2)}) collective-permute-start(bf16[1,384,768]{2,1,0:T(8,128)(2,1)S(1)} %maximum_bitcast_fusion.refs_0_), channel_id=1, source_target_pairs={{0,2},{1,3},{2,0},{3,1},{4,6},{5,7},{6,4},{7,5},{8,10},{9,11},{10,... | collective-permute-start | bytes 1769480 | tf_op jit(solution)/shard_map/wz/ppermute | solution.py:305
  8.1 29.7 %collective-permute-start.3 = (bf16[1,384,768]{2,1,0:T(8,128)(2,1)S(1)}, bf16[1,384,768]{2,1,0:T(8,128)(2,1)}, u32[]{:S(2)}, u32[]{:S(2)}) collective-permute-start(bf16[1,384,768]{2,1,0:T(8,128)(2,1)S(1)} %maximum_bitcast_fusion.refs_0_), channel_id=1, source_target_pairs={{0,1},{1,0},{2,3},{3,2},{4,5},{5,4},{6,7},{7,6},{8,9},{9,8},{10,11... | collective-permute-start | bytes 1769480 | tf_op jit(solution)/shard_map/wz/ppermute | solution.py:305
  8.3 29.5 %collective-permute-start.4 = (bf16[1,384,768]{2,1,0:T(8,128)(2,1)S(1)}, bf16[1,384,768]{2,1,0:T(8,128)(2,1)S(1)}, u32[]{:S(2)}, u32[]{:S(2)}) collective-permute-start(bf16[1,384,768]{2,1,0:T(8,128)(2,1)S(1)} %maximum_bitcast_fusion.refs_0_), channel_id=1, source_target_pairs={{0,8},{4,12},{8,0},{12,4},{1,9},{5,13},{9,1},{13,5},{2,10},{6,14},... | collective-permute-start | bytes 1769480 | tf_op jit(solution)/shard_map/wx0/ppermute | solution.py:305
  30.6 30.3 %all-to-all-start = ((bf16[4,3,360,128]{3,2,1,0:T(8,128)(2,1)}), bf16[4,3,360,128]{3,2,1,0:T(8,128)(2,1)S(1)}, u32[]{:S(2)}, u32[]{:S(2)}) async-start(bf16[4,3,360,128]{3,2,1,0:T(8,128)(2,1)} %conv.4), calls=%async_computation | async-start | bytes 2211840 | tf_op jit(solution)/shard_map/in0/all_to_all | solution.py:375
  37.7 11.0 %copy-start.4 = (bf16[1,384,768]{2,1,0:T(8,128)(2,1)}, bf16[1,384,768]{2,1,0:T(8,128)(2,1)S(1)}, u32[]{:S(2)}) copy-start(bf16[1,384,768]{2,1,0:T(8,128)(2,1)S(1)} %collective-permute-done.4.refs_1_) | copy-start | bytes 1769476
  37.8 30.2 %collective-permute-start.5 = (bf16[1,384,768]{2,1,0:T(8,128)(2,1)}, bf16[1,384,768]{2,1,0:T(8,128)(2,1)S(1)}, u32[]{:S(2)}, u32[]{:S(2)}) collective-permute-start(bf16[1,384,768]{2,1,0:T(8,128)(2,1)} %collective-permute-done.2.refs_0_), channel_id=1, source_target_pairs={{0,1},{1,0},{2,3},{3,2},{4,5},{5,4},{6,7},{7,6},{8,9},{9,8},{10,11... | collective-permute-start | bytes 1769480 | tf_op jit(solution)/shard_map/wz1/ppermute | solution.py:305
  61.0 11.0 %copy-start.1 = (bf16[4,3,360,128]{3,2,1,0:T(8,128)(2,1)}, bf16[4,3,360,128]{3,2,1,0:T(8,128)(2,1)S(1)}, u32[]{:S(2)}) copy-start(bf16[4,3,360,128]{3,2,1,0:T(8,128)(2,1)S(1)} %all-to-all-done.refs_0_) | copy-start | bytes 3317764
  61.0 29.9 %all-to-all-start.2 = ((bf16[4,3,360,128]{3,2,1,0:T(8,128)(2,1)}), bf16[4,3,360,128]{3,2,1,0:T(8,128)(2,1)S(1)}, u32[]{:S(2)}, u32[]{:S(2)}) async-start(bf16[4,3,360,128]{3,2,1,0:T(8,128)(2,1)} %conv.5), calls=%async_computation.2 | async-start | bytes 2211840 | tf_op jit(solution)/shard_map/in1/all_to_all | solution.py:375
  67.9 0.8 copy-start.10
  72.0 40.2 %collective-permute-start.7 = (bf16[3,384,768]{2,1,0:T(8,128)(2,1)}, bf16[3,384,768]{2,1,0:T(8,128)(2,1)}, u32[]{:S(2)}, u32[]{:S(2)}) collective-permute-start(bf16[3,384,768]{2,1,0:T(8,128)(2,1)} %stack.2.refs_2_), channel_id=1, source_target_pairs={{0,8},{4,12},{8,0},{12,4},{1,9},{5,13},{9,1},{13,5},{2,10},{6,14},... | collective-permute-start | bytes 5308424 | tf_op jit(solution)/shard_map/wx1/ppermute | solution.py:305
  90.9 6.6 %copy-start.2 = (bf16[4,3,360,128]{3,2,1,0:T(8,128)(2,1)}, bf16[4,3,360,128]{3,2,1,0:T(8,128)(2,1)S(1)}, u32[]{:S(2)}) copy-start(bf16[4,3,360,128]{3,2,1,0:T(8,128)(2,1)S(1)} %all-to-all-done.2.refs_0_) | copy-start | bytes 3317764
  90.9 30.3 %all-to-all-start.1 = ((bf16[4,3,360,128]{3,2,1,0:T(8,128)(2,1)}), bf16[4,3,360,128]{3,2,1,0:T(8,128)(2,1)}, u32[]{:S(2)}, u32[]{:S(2)}) async-start(bf16[4,3,360,128]{3,2,1,0:T(8,128)(2,1)} %conv.6), calls=%async_computation.1 | async-start | bytes 2211840 | tf_op jit(solution)/shard_map/in2/all_to_all | solution.py:375
  102.1 26.6 %collective-permute-start.6 = (bf16[5,384,768]{2,1,0:T(8,128)(2,1)}, bf16[5,384,768]{2,1,0:T(8,128)(2,1)S(1)}, u32[]{:S(2)}, u32[]{:S(2)}) collective-permute-start(bf16[5,384,768]{2,1,0:T(8,128)(2,1)} %stack.3.refs_2_), channel_id=1, source_target_pairs={{0,4},{4,0},{8,12},{12,8},{1,5},{5,1},{9,13},{13,9},{2,6},{6,2},{1... | collective-permute-start | bytes 8847368 | tf_op jit(solution)/shard_map/wc0/ppermute | solution.py:305
  112.1 15.6 %copy-start.9 = (f32[768]{0:T(1024)S(1)}, f32[768]{0:T(1024)}, u32[]{:S(2)}) copy-start(f32[768]{0:T(1024)} %param.9) | copy-start | bytes 9220
  112.1 16.5 %collective-permute-start.8 = (bf16[3,384,768]{2,1,0:T(8,128)(2,1)}, bf16[3,384,768]{2,1,0:T(8,128)(2,1)}, u32[]{:S(2)}, u32[]{:S(2)}) collective-permute-start(bf16[3,384,768]{2,1,0:T(8,128)(2,1)} %collective-permute-done.7.refs_4_), channel_id=1, source_target_pairs={{0,4},{4,0},{8,12},{12,8},{1,5},{5,1},{9,13},{13,9},{2,6},{6,2},{1... | collective-permute-start | bytes 5308424 | tf_op jit(solution)/shard_map/wc1/ppermute | solution.py:305
  121.1 44.7 %all-to-all-start.3 = ((bf16[4,3,360,128]{3,2,1,0:T(8,128)(2,1)}), bf16[4,3,360,128]{3,2,1,0:T(8,128)(2,1)}, u32[]{:S(2)}, u32[]{:S(2)}) async-start(bf16[4,3,360,128]{3,2,1,0:T(8,128)(2,1)} %conv.7), calls=%async_computation.3 | async-start | bytes 2211840 | tf_op jit(solution)/shard_map/in3/all_to_all | solution.py:375
  128.7 1.6 copy-start
  145.7 35.6 %collective-permute-start.10 = (bf16[3,360,128]{2,1,0:T(8,128)(2,1)}, bf16[3,360,128]{2,1,0:T(8,128)(2,1)S(1)}, u32[]{:S(2)}, u32[]{:S(2)}) collective-permute-start(bf16[3,360,128]{2,1,0:T(8,128)(2,1)} %get-tuple-element.51), channel_id=1, source_target_pairs={{0,2},{1,3},{2,0},{3,1},{4,6},{5,7},{6,4},{7,5},{8,10},{9,11},{10,... | collective-permute-start | bytes 829448 | tf_op jit(solution)/shard_map/out0/ppermute | solution.py:301
  146.3 37.0 %collective-permute-start.11 = (bf16[3,360,128]{2,1,0:T(8,128)(2,1)}, bf16[3,360,128]{2,1,0:T(8,128)(2,1)S(1)}, u32[]{:S(2)}, u32[]{:S(2)}) collective-permute-start(bf16[3,360,128]{2,1,0:T(8,128)(2,1)} %get-tuple-element.52), channel_id=1, source_target_pairs={{0,3},{1,0},{2,1},{3,2},{4,7},{5,4},{6,5},{7,6},{8,11},{9,8},{10,9... | collective-permute-start | bytes 829448 | tf_op jit(solution)/shard_map/out0/ppermute | solution.py:301
  146.5 36.8 %collective-permute-start.9 = (bf16[3,360,128]{2,1,0:T(8,128)(2,1)}, bf16[3,360,128]{2,1,0:T(8,128)(2,1)S(1)}, u32[]{:S(2)}, u32[]{:S(2)}) collective-permute-start(bf16[3,360,128]{2,1,0:T(8,128)(2,1)} %get-tuple-element.50), channel_id=1, source_target_pairs={{0,1},{1,2},{2,3},{3,0},{4,5},{5,6},{6,7},{7,4},{8,9},{9,10},{10,1... | collective-permute-start | bytes 829448 | tf_op jit(solution)/shard_map/out0/ppermute | solution.py:301
  181.2 20.8 %collective-permute-start.12 = (bf16[3,360,128]{2,1,0:T(8,128)(2,1)}, bf16[3,360,128]{2,1,0:T(8,128)(2,1)S(1)}, u32[]{:S(2)}, u32[]{:S(2)}) collective-permute-start(bf16[3,360,128]{2,1,0:T(8,128)(2,1)} %get-tuple-element.55), channel_id=1, source_target_pairs={{0,1},{1,2},{2,3},{3,0},{4,5},{5,6},{6,7},{7,4},{8,9},{9,10},{10,1... | collective-permute-start | bytes 829448 | tf_op jit(solution)/shard_map/out1/ppermute | solution.py:301
  181.2 35.4 %collective-permute-start.13 = (bf16[3,360,128]{2,1,0:T(8,128)(2,1)}, bf16[3,360,128]{2,1,0:T(8,128)(2,1)S(1)}, u32[]{:S(2)}, u32[]{:S(2)}) collective-permute-start(bf16[3,360,128]{2,1,0:T(8,128)(2,1)} %get-tuple-element.56), channel_id=1, source_target_pairs={{0,2},{1,3},{2,0},{3,1},{4,6},{5,7},{6,4},{7,5},{8,10},{9,11},{10,... | collective-permute-start | bytes 829448 | tf_op jit(solution)/shard_map/out1/ppermute | solution.py:301
  181.3 17.6 %copy-start.11 = (bf16[3,360,128]{2,1,0:T(8,128)(2,1)}, bf16[3,360,128]{2,1,0:T(8,128)(2,1)S(1)}, u32[]{:S(2)}) copy-start(bf16[3,360,128]{2,1,0:T(8,128)(2,1)S(1)} %collective-permute-done.10.refs_2_) | copy-start | bytes 829444
  181.3 35.3 %collective-permute-start.14 = (bf16[3,360,128]{2,1,0:T(8,128)(2,1)}, bf16[3,360,128]{2,1,0:T(8,128)(2,1)S(1)}, u32[]{:S(2)}, u32[]{:S(2)}) collective-permute-start(bf16[3,360,128]{2,1,0:T(8,128)(2,1)} %get-tuple-element.57), channel_id=1, source_target_pairs={{0,3},{1,0},{2,1},{3,2},{4,7},{5,4},{6,5},{7,6},{8,11},{9,8},{10,9... | collective-permute-start | bytes 829448 | tf_op jit(solution)/shard_map/out1/ppermute | solution.py:301
  183.3 15.6 %copy-start.12 = (bf16[3,360,128]{2,1,0:T(8,128)(2,1)}, bf16[3,360,128]{2,1,0:T(8,128)(2,1)S(1)}, u32[]{:S(2)}) copy-start(bf16[3,360,128]{2,1,0:T(8,128)(2,1)S(1)} %collective-permute-done.11.refs_3_) | copy-start | bytes 829444
  183.3 15.6 %copy-start.13 = (bf16[3,360,128]{2,1,0:T(8,128)(2,1)}, bf16[3,360,128]{2,1,0:T(8,128)(2,1)S(1)}, u32[]{:S(2)}) copy-start(bf16[3,360,128]{2,1,0:T(8,128)(2,1)S(1)} %collective-permute-done.9.refs_1_) | copy-start | bytes 829444
  199.0 33.5 %collective-permute-start.15 = (bf16[3,360,128]{2,1,0:T(8,128)(2,1)}, bf16[3,360,128]{2,1,0:T(8,128)(2,1)S(1)}, u32[]{:S(2)}, u32[]{:S(2)}) collective-permute-start(bf16[3,360,128]{2,1,0:T(8,128)(2,1)} %get-tuple-element.60), channel_id=1, source_target_pairs={{0,1},{1,2},{2,3},{3,0},{4,5},{5,6},{6,7},{7,4},{8,9},{9,10},{10,1... | collective-permute-start | bytes 829448 | tf_op jit(solution)/shard_map/out2/ppermute | solution.py:301
  201.4 33.0 %collective-permute-start.16 = (bf16[3,360,128]{2,1,0:T(8,128)(2,1)}, bf16[3,360,128]{2,1,0:T(8,128)(2,1)S(1)}, u32[]{:S(2)}, u32[]{:S(2)}) collective-permute-start(bf16[3,360,128]{2,1,0:T(8,128)(2,1)} %get-tuple-element.61), channel_id=1, source_target_pairs={{0,2},{1,3},{2,0},{3,1},{4,6},{5,7},{6,4},{7,5},{8,10},{9,11},{10,... | collective-permute-start | bytes 829448 | tf_op jit(solution)/shard_map/out2/ppermute | solution.py:301
  202.0 30.3 %copy-start.14 = (bf16[3,360,128]{2,1,0:T(8,128)(2,1)}, bf16[3,360,128]{2,1,0:T(8,128)(2,1)S(1)}, u32[]{:S(2)}) copy-start(bf16[3,360,128]{2,1,0:T(8,128)(2,1)S(1)} %collective-permute-done.12.refs_1_) | copy-start | bytes 829444
  202.0 32.5 %collective-permute-start.17 = (bf16[3,360,128]{2,1,0:T(8,128)(2,1)}, bf16[3,360,128]{2,1,0:T(8,128)(2,1)S(1)}, u32[]{:S(2)}, u32[]{:S(2)}) collective-permute-start(bf16[3,360,128]{2,1,0:T(8,128)(2,1)} %get-tuple-element.62), channel_id=1, source_target_pairs={{0,3},{1,0},{2,1},{3,2},{4,7},{5,4},{6,5},{7,6},{8,11},{9,8},{10,9... | collective-permute-start | bytes 829448 | tf_op jit(solution)/shard_map/out2/ppermute | solution.py:301
  216.6 15.6 %copy-start.15 = (bf16[3,360,128]{2,1,0:T(8,128)(2,1)}, bf16[3,360,128]{2,1,0:T(8,128)(2,1)S(1)}, u32[]{:S(2)}) copy-start(bf16[3,360,128]{2,1,0:T(8,128)(2,1)S(1)} %collective-permute-done.13.refs_2_) | copy-start | bytes 829444
  216.6 15.6 %copy-start.16 = (bf16[3,360,128]{2,1,0:T(8,128)(2,1)}, bf16[3,360,128]{2,1,0:T(8,128)(2,1)S(1)}, u32[]{:S(2)}) copy-start(bf16[3,360,128]{2,1,0:T(8,128)(2,1)S(1)} %collective-permute-done.14.refs_3_) | copy-start | bytes 829444
  232.3 15.0 %collective-permute-start.18 = (bf16[3,360,128]{2,1,0:T(8,128)(2,1)}, bf16[3,360,128]{2,1,0:T(8,128)(2,1)S(1)}, u32[]{:S(2)}, u32[]{:S(2)}) collective-permute-start(bf16[3,360,128]{2,1,0:T(8,128)(2,1)} %get-tuple-element.64), channel_id=1, source_target_pairs={{0,1},{1,2},{2,3},{3,0},{4,5},{5,6},{6,7},{7,4},{8,9},{9,10},{10,1... | collective-permute-start | bytes 829448 | tf_op jit(solution)/shard_map/out3/ppermute | solution.py:301
  232.4 24.3 %collective-permute-start.19 = (bf16[3,360,128]{2,1,0:T(8,128)(2,1)}, bf16[3,360,128]{2,1,0:T(8,128)(2,1)S(1)}, u32[]{:S(2)}, u32[]{:S(2)}) collective-permute-start(bf16[3,360,128]{2,1,0:T(8,128)(2,1)} %get-tuple-element.65), channel_id=1, source_target_pairs={{0,2},{1,3},{2,0},{3,1},{4,6},{5,7},{6,4},{7,5},{8,10},{9,11},{10,... | collective-permute-start | bytes 829448 | tf_op jit(solution)/shard_map/out3/ppermute | solution.py:301
  232.4 6.4 %copy-start.17 = (bf16[3,360,128]{2,1,0:T(8,128)(2,1)}, bf16[3,360,128]{2,1,0:T(8,128)(2,1)S(1)}, u32[]{:S(2)}) copy-start(bf16[3,360,128]{2,1,0:T(8,128)(2,1)S(1)} %collective-permute-done.15.refs_1_) | copy-start | bytes 829444
  232.5 24.2 %collective-permute-start.20 = (bf16[3,360,128]{2,1,0:T(8,128)(2,1)}, bf16[3,360,128]{2,1,0:T(8,128)(2,1)S(1)}, u32[]{:S(2)}, u32[]{:S(2)}) collective-permute-start(bf16[3,360,128]{2,1,0:T(8,128)(2,1)} %get-tuple-element.66), channel_id=1, source_target_pairs={{0,3},{1,0},{2,1},{3,2},{4,7},{5,4},{6,5},{7,6},{8,11},{9,8},{10,9... | collective-permute-start | bytes 829448 | tf_op jit(solution)/shard_map/out3/ppermute | solution.py:301
  234.4 4.4 %copy-start.18 = (bf16[3,360,128]{2,1,0:T(8,128)(2,1)}, bf16[3,360,128]{2,1,0:T(8,128)(2,1)S(1)}, u32[]{:S(2)}) copy-start(bf16[3,360,128]{2,1,0:T(8,128)(2,1)S(1)} %collective-permute-done.16.refs_2_) | copy-start | bytes 829444
  234.4 4.4 %copy-start.19 = (bf16[3,360,128]{2,1,0:T(8,128)(2,1)}, bf16[3,360,128]{2,1,0:T(8,128)(2,1)S(1)}, u32[]{:S(2)}) copy-start(bf16[3,360,128]{2,1,0:T(8,128)(2,1)S(1)} %collective-permute-done.17.refs_3_) | copy-start | bytes 829444
  247.3 9.4 %copy-start.20 = (bf16[3,360,128]{2,1,0:T(8,128)(2,1)}, bf16[3,360,128]{2,1,0:T(8,128)(2,1)S(1)}, u32[]{:S(2)}) copy-start(bf16[3,360,128]{2,1,0:T(8,128)(2,1)S(1)} %collective-permute-done.18.refs_1_) | copy-start | bytes 829444
  256.7 0.7 copy-start.21
  257.4 0.7 copy-start.22

commit v4 on v3

--- a/solution.py
+++ b/solution.py
@@ -78,8 +78,11 @@
         store(self.full, tail)
 
 
-def conv_kernel(packing, sources, rows, first_row, low, *refs):
-    *field_refs, lon_ref, lat_ref, out_ref, base_ref, cells_ref = refs
+def conv_kernel(packing, sources, rows, first_row, low, me_ref, *refs):
+    outs = 1 if refs[-3].shape[0] == sources else sources
+    *field_refs, lon_ref, lat_ref = refs[: -outs - 2]
+    out_refs, (base_ref, cells_ref) = refs[-outs - 2 : -2], refs[-2:]
+    start = 0 if outs == 1 else sources - me_ref[0]
     width = field_refs[0].shape[2]
     held_rows, block, wide = base_ref.shape
     group = field_refs[0].shape[0]
@@ -109,15 +112,17 @@
                 term = pltpu.roll(term, turn % wide, 1) if turn else term
                 result = term if result is None else result + term
             receiver, row = divmod(out_row, rows)
-            cells_ref[receiver, chans, row * width : (row + 1) * width] = result[:, 0:width]
+            slot = receiver if outs == 1 else lax.rem(receiver + start, sources)
+            cells_ref[slot, chans, row * width : (row + 1) * width] = result[:, 0:width]
         return 0
 
     lax.fori_loop(0, block // part, some_channels, 0)
-    for receiver in range(sources):
-        packing.store(out_ref.at[receiver], 0, lambda i: cells_ref[receiver, :, i * LANES : (i + 1) * LANES])
-
-
-def convolve(packing, sources, field, before, after, lon_taps, lat_taps, place, row_count):
+    for slot in range(sources):
+        out_ref = out_refs[0].at[slot] if outs == 1 else out_refs[slot].at[0]
+        packing.store(out_ref, 0, lambda i: cells_ref[slot, :, i * LANES : (i + 1) * LANES])
+
+
+def convolve(packing, me, sources, outs, field, before, after, lon_taps, lat_taps, place, row_count):
     row_total, chan_count, width = field.shape
     block = packing.block
     wide = round_up(width + 2 * BORDER, LANES)
@@ -126,30 +131,35 @@
     specs, operands = [], []
     for near in places:
         for array in (field, before, after):
-            specs.append(pl.BlockSpec((row_count, block, array.shape[2]), lambda c, near=near: (near, c, 0)))
+            specs.append(pl.BlockSpec((row_count, block, array.shape[2]), lambda c, me, near=near: (near, c, 0)))
             operands.append(array)
-    taps = pl.BlockSpec((block, KERNEL_TAPS), lambda c: (c, 0))
+    taps = pl.BlockSpec((block, KERNEL_TAPS), lambda c, me: (c, 0))
+    count = sources // outs
+    out = jax.ShapeDtypeStruct((count, packing.blocks, packing.rows, LANES), jnp.bfloat16)
     return pl.pallas_call(
         functools.partial(
             conv_kernel, packing, sources, row_count // sources, place * row_count, places[0] * row_count
         ),
-        grid=(packing.blocks,),
-        in_specs=[*specs, taps, taps],
-        out_specs=pl.BlockSpec((sources, 1, packing.rows, LANES), lambda c: (0, c, 0, 0)),
-        out_shape=jax.ShapeDtypeStruct((sources, packing.blocks, packing.rows, LANES), jnp.bfloat16),
-        scratch_shapes=[
-            pltpu.VMEM((len(places) * row_count, block, wide), jnp.float32),
-            pltpu.VMEM((sources, block, packing.wide), jnp.float32),
-        ],
+        grid_spec=pltpu.PrefetchScalarGridSpec(
+            num_scalar_prefetch=1,
+            grid=(packing.blocks,),
+            in_specs=[*specs, taps, taps],
+            out_specs=[pl.BlockSpec((count, 1, packing.rows, LANES), lambda c, me: (0, c, 0, 0))] * outs,
+            scratch_shapes=[
+                pltpu.VMEM((len(places) * row_count, block, wide), jnp.float32),
+                pltpu.VMEM((sources, block, packing.wide), jnp.float32),
+            ],
+        ),
+        out_shape=[out] * outs,
         compiler_params=PARAMS,
         cost_estimate=microseconds(12),
         name="conv",
-    )(*operands, lon_taps, lat_taps)
-
-
-def mlp_kernel(packing, sources, counts, me_ref, *refs):
-    x_ref, gain_ref = refs[:2]
-    weight_refs = refs[2 : 2 + 2 * len(counts)]
+    )(me, *operands, lon_taps, lat_taps)
+
+
+def mlp_kernel(packing, sources, arrays, counts, me_ref, *refs):
+    x_refs, gain_ref = refs[:arrays], refs[arrays]
+    weight_refs = refs[arrays + 1 : arrays + 1 + 2 * len(counts)]
     out_refs, (values, normed, total) = refs[-sources - 3 : -3], refs[-3:]
     step = pl.program_id(0)
     me = me_ref[0]
@@ -162,13 +172,15 @@
 
     @pl.when(step == 0)
     def _():
-        for sender in range(sources):
+        for slot in range(sources):
+            sender = slot if arrays == 1 else lax.rem(me + sources - slot, sources)
+            x_ref = x_refs[0].at[slot] if arrays == 1 else x_refs[slot].at[0]
             for lead in range(packing.blocks):
 
                 def put(i, piece, at=channels(sender, lead)):
                     values[at, i * LANES : (i + 1) * LANES] = piece
 
-                packing.load(x_ref.at[sender], lead, put)
+                packing.load(x_ref, lead, put)
         as_float = values[...]
         center = jnp.mean(as_float, axis=0, keepdims=True)
         deviation = as_float - center
@@ -209,7 +221,8 @@
 
 
 def mlp(packing, me, by_cell, gain, weights):
-    sources = by_cell.shape[0]
+    arrays = len(by_cell)
+    sources = arrays * by_cell[0].shape[0]
     width_all = gain.shape[0]
     rows = weights[0].shape[1]
     group = 1
@@ -224,15 +237,15 @@
             lambda h, me, start=start, count=count: (jnp.clip(h - start, 0, count - 1), 0, 0),
         )
         specs += [spec, spec]
-    shape = by_cell.shape[1:]
+    shape = by_cell[0].shape[1:]
     whole = pl.BlockSpec(shape, lambda h, me: (0, 0, 0))
-    cells = pl.BlockSpec(by_cell.shape, lambda h, me: (0, 0, 0, 0))
+    cells = pl.BlockSpec(by_cell[0].shape, lambda h, me: (0, 0, 0, 0))
     return pl.pallas_call(
-        functools.partial(mlp_kernel, packing, sources, counts),
+        functools.partial(mlp_kernel, packing, sources, arrays, counts),
         grid_spec=pltpu.PrefetchScalarGridSpec(
             num_scalar_prefetch=1,
             grid=(sum(counts),),
-            in_specs=[cells, pl.BlockSpec((width_all, 1), lambda h, me: (0, 0)), *specs],
+            in_specs=[cells] * arrays + [pl.BlockSpec((width_all, 1), lambda h, me: (0, 0)), *specs],
             out_specs=[whole] * sources,
             scratch_shapes=[
                 pltpu.VMEM((width_all, packing.wide), jnp.float32),
@@ -242,9 +255,9 @@
         ),
         out_shape=[jax.ShapeDtypeStruct(shape, jnp.bfloat16)] * sources,
         compiler_params=PARAMS,
-        cost_estimate=microseconds(1),
+        cost_estimate=microseconds(13),
         name="mlp",
-    )(me, by_cell, gain, *weights)
+    )(me, *by_cell, gain, *weights)
 
 
 def add_kernel(packing, sources, me_ref, *refs):
@@ -331,7 +344,7 @@
         out_specs=pl.BlockSpec(block, lambda i: (i, 0, 0)),
         out_shape=jax.ShapeDtypeStruct((sum(counts), *block[1:]), arrays[0].dtype),
         compiler_params=PARAMS,
-        cost_estimate=microseconds(1),
+        cost_estimate=microseconds(13),
         name="stack",
     )(*arrays)
 
@@ -370,33 +383,37 @@
     packing = Packing(chan_count, rows // sources * width)
 
     def spread(place):
-        spatial = convolve(packing, sources, field, before, after, lon, lat, place, rows)
+        outs = sources if place % 2 else 1
+        spatial = convolve(packing, me, sources, outs, field, before, after, lon, lat, place, rows)
         with jax.named_scope(f"in{place}"):
-            return spatial, lax.all_to_all(spatial, "chan", split_axis=0, concat_axis=0, tiled=True)
+            if outs == 1:
+                return spatial, [lax.all_to_all(spatial[0], "chan", split_axis=0, concat_axis=0, tiled=True)]
+            return spatial, [spatial[0]] + [shifted(spatial[s], "chan", s) for s in range(1, sources)]
 
     by_cell = []
     spatial, cells = spread(0)
     by_cell.append(cells)
-    lon, far, near, across = after_all((lon, far, near, across), spatial)
+    lon, far, near, across = after_all((lon, far, near, across), spatial[0])
     with jax.named_scope("wz1"):
         rest = [exchanged(piece, "chan", 1) for piece in far[1:]]
     spatial, cells = spread(1)
     by_cell.append(cells)
-    lon, rest, across = after_all((lon, rest, across), spatial, by_cell[0])
+    lon = after_all(lon, spatial[0])
+    rest, across = after_all((rest, across), spatial[0])
     others = stacked(*far[1:], near, *rest)
     with jax.named_scope("wx1"):
         others_across = exchanged(others, "tile", bits[0])
     spatial, cells = spread(2)
     by_cell.append(cells)
-    lon, others = after_all((lon, others), spatial, by_cell[1])
     held = stacked(shard, across, others)
     for bit in bits[1:]:
         held = stacked(held, exchanged(held, "tile", bit))
+    lon, held = after_all((lon, held), spatial[0], by_cell[0], by_cell[1][1:])
     with jax.named_scope("wc0"):
         received = exchanged(held, "tile", 1)
     spatial, cells = spread(3)
     by_cell.append(cells)
-    others_across = after_all(others_across, spatial)
+    others_across = after_all(others_across, by_cell[2], by_cell[3][1])
     for bit in bits[1:]:
         others_across = stacked(others_across, exchanged(others_across, "tile", bit))
     with jax.named_scope("wc1"):
@@ -409,7 +426,7 @@
         pieces = mlp(packing, me, by_cell[chunk], gain, weights)
         with jax.named_scope(f"out{chunk}"):
             updates.append([pieces[0]] + [shifted(pieces[s], "chan", s) for s in range(1, sources)])
-        me = after_all(me, pieces[0], updates[chunk - 1][1:] if chunk else by_cell[CHUNKS - 1])
+        me = after_all(me, pieces[0], updates[chunk - 1][1:] if chunk else by_cell[CHUNKS - 1][1:])
     mixed = None
     for chunk in range(CHUNKS):
         mixed = add_rows(packing, me, updates[chunk], weather, mixed, chunk, rows)

time: 263 us -> 254 us (0.966)
  waiting for transfers between devices: 66.6 us -> 54.8 us
  starting transfers between devices: 46.4 us -> 50.2 us
    all_to_all x4 -> x2, waiting for transfers between devices: 43.4 us -> 0.01 us  [spread(): lax.all_to_all(spatial[0], 'chan', split_axis=0, concat_axis=0, tiled=True)]
    ppermute x14 -> x20, waiting for transfers between devices: 22.1 us -> 42.5 us  [shifted(): lax.ppermute(array, axis, [(i, (i + shift) % count) for i in range(count)])]
    ppermute x14 -> x20, starting transfers between devices: 15.3 us -> 27.7 us  [shifted(): lax.ppermute(array, axis, [(i, (i + shift) % count) for i in range(count)])]
    ppermute x7, waiting for transfers between devices: 1.12 us -> 12.2 us  [exchanged(): lax.ppermute(array, axis, [(i, i ^ bit) for i in range(lax.axis_size(axis...]
    all_to_all x4 -> x2, starting transfers between devices: 26.1 us -> 17.6 us  [spread(): lax.all_to_all(spatial[0], 'chan', split_axis=0, concat_axis=0, tiled=True)]
    unnamed x51 -> x63, local copies, waits for them, and re-layouts: 14.8 us -> 13.3 us
  transfers between devices with their start and end apart: 25 -> 29, of which waited for: 7 -> 7; matrix products, arithmetic and copies ran while one was open for 5% -> 5% of each run, Pallas kernels for 47% -> 49%
where the time goes in v4:
time: 254 us; the launch traced here: 253 us
  Pallas kernels  128 us (50%)
  waiting for transfers between devices  54.8 us (22%)
  starting transfers between devices  50.2 us (20%)
  local copies, waits for them, and re-layouts  20.1 us (8%)
    pallas_call x4, Pallas kernels, mlp(): pl.pallas_call(functools.partial(mlp_kernel, packing, sources, arrays, co...  62.2 us
    ppermute x20, waiting for transfers between devices, shifted(): lax.ppermute(array, axis, [(i, (i + shift) % count) for i in range(count)])  42.5 us
    pallas_call x4, Pallas kernels, convolve(): pl.pallas_call(functools.partial(conv_kernel, packing, sources, row_count...  41 us
    ppermute x20, starting transfers between devices, shifted(): lax.ppermute(array, axis, [(i, (i + shift) % count) for i in range(count)])  27.7 us
    all_to_all x2, starting transfers between devices, spread(): lax.all_to_all(spatial[0], 'chan', split_axis=0, concat_axis=0, tiled=True)  17.6 us
    pallas_call x4, Pallas kernels, add_rows(): pl.pallas_call(functools.partial(add_kernel, packing, sources), grid_spec...  17 us
    unnamed x63, local copies, waits for them, and re-layouts  13.3 us
    ppermute x7, waiting for transfers between devices, exchanged(): lax.ppermute(array, axis, [(i, i ^ bit) for i in range(lax.axis_size(axis...  12.2 us
  transfers between devices with their start and end apart: 29, of which 7 were waited for; matrix products, arithmetic and copies ran while one was open for 5% of the time, Pallas kernels for 49%

profile of v4, /device:TPU:24, one launch (start us, length us, event | category | flops | bytes accessed | tf_op | source)
XLA Modules:
  0.0 253.4 jit_solution(1940335210115022051)
XLA Ops:
  0.0 2.6 %fusion = (bf16[192,32,8]{2,1,0:T(8,128)(2,1)S(1)}, bf16[192,32,8]{2,1,0:T(8,128)(2,1)S(1)}) fusion(bf16[192,32,360]{2,1,0:T(8,128)(2,1)} %refs_4_.7), kind=kLoop, calls=%fused_computation.2 | loop fusion | bytes 393216 | tf_op jit(solution)/shard_map/halo/slice | solution.py:362
  2.6 0.0 copy-start.3
  2.6 1.9 copy.35
  4.6 1.3 copy.36
  5.8 1.8 collective-permute-start.1
  7.7 0.4 collective-permute-start.2
  8.1 0.2 collective-permute-start.3
  8.3 1.7 collective-permute-start.4
  10.0 6.3 %copy.38 = bf16[192,32,360]{2,0,1:T(8,128)(2,1)} copy(bf16[192,32,360]{2,1,0:T(8,128)(2,1)} %refs_4_.7) | data formatting | bytes 8847360 | tf_op args[0]
  16.3 0.8 copy.30
  17.1 0.8 copy.29
  17.8 0.0 collective-permute-done
  17.8 1.5 copy.26
  19.3 0.0 collective-permute-done.1
  19.3 1.6 copy.28
  20.9 9.8 %conv.4 = bf16[4,3,360,128]{3,2,1,0:T(8,128)(2,1)} custom-call(s32[1]{0:T(128)} %bitcast.me_ref, bf16[32,192,360]{2,1,0:T(8,128)(2,1)} %bitcast.12, bf16[32,192,8]{2,1,0:T(8,128)(2,1)} %bitcast.22, bf16[32,192,8]{2,1,0:T(8,128)(2,1)} %bitcast.32, bf16[32,192,360]{2,1,0:T(8,128)(2,1)} %bitcast.13, bf16[32,192,8]{2,1,0:T(8,128)(2,1)} %bitcast.23, ...), custom_call_target="tpu_custom_call" | custom-call | flops 13799999488 | bytes 1024 | tf_op jit(solution)/shard_map/conv/pallas_call | solution.py:139
  30.6 7.1 %all-to-all-start.1 = ((bf16[4,3,360,128]{3,2,1,0:T(8,128)(2,1)}), bf16[4,3,360,128]{3,2,1,0:T(8,128)(2,1)S(1)}, u32[]{:S(2)}, u32[]{:S(2)}) async-start(bf16[4,3,360,128]{3,2,1,0:T(8,128)(2,1)} %conv.4), calls=%async_computation.1 | async-start | bytes 2211840 | tf_op jit(solution)/shard_map/in0/all_to_all | solution.py:390
  37.8 10.6 %conv.5 = (bf16[1,3,360,128]{3,2,1,0:T(8,128)(2,1)}, bf16[1,3,360,128]{3,2,1,0:T(8,128)(2,1)}, bf16[1,3,360,128]{3,2,1,0:T(8,128)(2,1)}, bf16[1,3,360,128]{3,2,1,0:T(8,128)(2,1)}) custom-call(s32[1]{0:T(128)} %bitcast.me_ref, bf16[32,192,360]{2,1,0:T(8,128)(2,1)} %bitcast.14, bf16[32,192,8]{2,1,0:T(8,128)(2,1)} %bitcast.24, bf16[32,192,8]{2,1,0:T(8,128)(2,1)} %bitcast.34, ...), custom_call_target="tpu_custom_call" | custom-call | flops 13799999488 | bytes 1024 | tf_op jit(solution)/shard_map/conv/pallas_call | solution.py:139
  48.4 0.6 collective-permute-start.5
  49.0 10.4 %conv.6 = bf16[4,3,360,128]{3,2,1,0:T(8,128)(2,1)} custom-call(s32[1]{0:T(128)} %bitcast.me_ref, bf16[32,192,360]{2,1,0:T(8,128)(2,1)} %bitcast.17, bf16[32,192,8]{2,1,0:T(8,128)(2,1)} %bitcast.27, bf16[32,192,8]{2,1,0:T(8,128)(2,1)} %bitcast.37, bf16[32,192,360]{2,1,0:T(8,128)(2,1)} %bitcast.18, bf16[32,192,8]{2,1,0:T(8,128)(2,1)} %bitcast.28, ...), custom_call_target="tpu_custom_call" | custom-call | flops 13799999488 | bytes 1024 | tf_op jit(solution)/shard_map/conv/pallas_call | solution.py:139
  59.4 1.5 collective-permute-start.6
  60.9 1.5 collective-permute-start.7
  62.3 0.0 collective-permute-start.8
  62.4 12.2 %collective-permute-done.5.refs_2_ = bf16[1,384,768]{2,1,0:T(8,128)(2,1)S(1)} collective-permute-done((bf16[1,384,768]{2,1,0:T(8,128)(2,1)}, bf16[1,384,768]{2,1,0:T(8,128)(2,1)S(1)}, u32[]{:S(2)}, u32[]{:S(2)}) %collective-permute-start.5) | collective-permute-done | bytes 589856 | tf_op jit(solution)/shard_map/wz1/ppermute | solution.py:318
  74.6 0.8 copy-done.9
  75.4 3.2 %stack.2.refs_2_ = bf16[3,384,768]{2,1,0:T(8,128)(2,1)} custom-call(bf16[1,384,768]{2,1,0:T(8,128)(2,1)} %collective-permute-done.2.refs_0_, bf16[1,384,768]{2,1,0:T(8,128)(2,1)} %collective-permute-done.3.refs_1_, bf16[1,384,768]{2,1,0:T(8,128)(2,1)} %copy-done.9), custom_call_target="tpu_custom_call" | custom-call | flops 14949999616 | bytes 1024 | tf_op jit(solution)/shard_map/stack/pallas_call | solution.py:340
  78.6 1.8 collective-permute-start.10
  80.4 0.0 all-to-all-done.1.refs_0_
  80.4 10.5 %all-to-all-start = ((bf16[4,3,360,128]{3,2,1,0:T(8,128)(2,1)}), bf16[4,3,360,128]{3,2,1,0:T(8,128)(2,1)S(1)}, u32[]{:S(2)}, u32[]{:S(2)}) async-start(bf16[4,3,360,128]{3,2,1,0:T(8,128)(2,1)} %conv.6), calls=%async_computation | async-start | bytes 2211840 | tf_op jit(solution)/shard_map/in2/all_to_all | solution.py:390
  90.9 4.6 %stack.3.refs_2_.refs_5_ = bf16[5,384,768]{2,1,0:T(8,128)(2,1)} custom-call(bf16[1,384,768]{2,1,0:T(8,128)(2,1)} %copy-done.2, bf16[1,384,768]{2,1,0:T(8,128)(2,1)} %copy-done.8, bf16[3,384,768]{2,1,0:T(8,128)(2,1)} %stack.2.refs_2_), custom_call_target="tpu_custom_call" | custom-call | flops 14949999616 | bytes 1024 | tf_op jit(solution)/shard_map/stack/pallas_call | solution.py:340
  95.5 0.0 collective-permute-done.7.refs_2_
  95.6 0.1 collective-permute-start.9
  95.6 10.2 %conv.7 = (bf16[1,3,360,128]{3,2,1,0:T(8,128)(2,1)}, bf16[1,3,360,128]{3,2,1,0:T(8,128)(2,1)}, bf16[1,3,360,128]{3,2,1,0:T(8,128)(2,1)}, bf16[1,3,360,128]{3,2,1,0:T(8,128)(2,1)}) custom-call(s32[1]{0:T(128)} %bitcast.me_ref, bf16[32,192,360]{2,1,0:T(8,128)(2,1)} %bitcast.20, bf16[32,192,8]{2,1,0:T(8,128)(2,1)} %bitcast.30, bf16[32,192,8]{2,1,0:T(8,128)(2,1)} %bitcast.40, ...), custom_call_target="tpu_custom_call" | custom-call | flops 13799999488 | bytes 1024 | tf_op jit(solution)/shard_map/conv/pallas_call | solution.py:139
  105.9 0.1 collective-permute-start.11
  106.0 12.8 %collective-permute-done.11.refs_1_ = bf16[1,3,360,128]{3,2,1,0:T(8,128)(2,1)S(1)} collective-permute-done((bf16[1,3,360,128]{3,2,1,0:T(8,128)(2,1)}, bf16[1,3,360,128]{3,2,1,0:T(8,128)(2,1)S(1)}, u32[]{:S(2)}, u32[]{:S(2)}) %collective-permute-start.11) | collective-permute-done | bytes 276512 | tf_op jit(solution)/shard_map/in3/ppermute | solution.py:314
  118.8 0.1 collective-permute-start.12
  118.9 1.1 broadcast_in_dim.12.refs_1_.refs_4_
  120.0 3.7 %collective-permute-start.13 = (bf16[1,3,360,128]{3,2,1,0:T(8,128)(2,1)}, bf16[1,3,360,128]{3,2,1,0:T(8,128)(2,1)S(1)}, u32[]{:S(2)}, u32[]{:S(2)}) collective-permute-start(bf16[1,3,360,128]{3,2,1,0:T(8,128)(2,1)} %get-tuple-element.61), channel_id=1, source_target_pairs={{0,2},{1,3},{2,0},{3,1},{4,6},{5,7},{6,4},{7,5},{8,10},{9,11},{10,... | collective-permute-start | bytes 829448 | tf_op jit(solution)/shard_map/in3/ppermute | solution.py:314
  123.7 2.4 collective-permute-start.14
  126.1 15.4 %mlp.4 = (bf16[3,360,128]{2,1,0:T(8,128)(2,1)}, bf16[3,360,128]{2,1,0:T(8,128)(2,1)}, bf16[3,360,128]{2,1,0:T(8,128)(2,1)}, bf16[3,360,128]{2,1,0:T(8,128)(2,1)}) custom-call(s32[1]{0:T(128)} %bitcast.me_ref, bf16[4,3,360,128]{3,2,1,0:T(8,128)(2,1)} %copy-done.1, f32[768,1]{1,0:T(8,128)} %broadcast_in_dim.12.refs_1_.refs_4_, ...), custom_call_target="tpu_custom_call" | custom-call | flops 14949999616 | bytes 1024 | tf_op jit(solution)/shard_map/mlp/pallas_call | solution.py:243
  141.5 1.5 collective-permute-done.13.refs_2_
  143.0 1.1 collective-permute-start.15
  144.1 1.6 collective-permute-start.16
  145.7 2.0 collective-permute-start.17
  147.7 15.6 %mlp.5 = (bf16[3,360,128]{2,1,0:T(8,128)(2,1)}, bf16[3,360,128]{2,1,0:T(8,128)(2,1)}, bf16[3,360,128]{2,1,0:T(8,128)(2,1)}, bf16[3,360,128]{2,1,0:T(8,128)(2,1)}) custom-call(s32[1]{0:T(128)} %bitcast.me_ref, bf16[1,3,360,128]{3,2,1,0:T(8,128)(2,1)} %get-tuple-element.45.refs_0_, bf16[1,3,360,128]{3,2,1,0:T(8,128)(2,1)} %copy-done.11, ...), custom_call_target="tpu_custom_call" | custom-call | flops 14949999616 | bytes 1024 | tf_op jit(solution)/shard_map/mlp/pallas_call | solution.py:243
  163.3 1.9 collective-permute-start.18
  165.1 0.6 collective-permute-start.20
  165.8 5.8 %collective-permute-done.16.refs_2_ = bf16[3,360,128]{2,1,0:T(8,128)(2,1)S(1)} collective-permute-done((bf16[3,360,128]{2,1,0:T(8,128)(2,1)}, bf16[3,360,128]{2,1,0:T(8,128)(2,1)S(1)}, u32[]{:S(2)}, u32[]{:S(2)}) %collective-permute-start.16) | collective-permute-done | bytes 276512 | tf_op jit(solution)/shard_map/out0/ppermute | solution.py:314
  171.6 15.7 %mlp.6 = (bf16[3,360,128]{2,1,0:T(8,128)(2,1)}, bf16[3,360,128]{2,1,0:T(8,128)(2,1)}, bf16[3,360,128]{2,1,0:T(8,128)(2,1)}, bf16[3,360,128]{2,1,0:T(8,128)(2,1)}) custom-call(s32[1]{0:T(128)} %bitcast.me_ref, bf16[4,3,360,128]{3,2,1,0:T(8,128)(2,1)} %copy-done, f32[768,1]{1,0:T(8,128)} %broadcast_in_dim.12.refs_1_.refs_4_, ...), custom_call_target="tpu_custom_call" | custom-call | flops 14949999616 | bytes 1024 | tf_op jit(solution)/shard_map/mlp/pallas_call | solution.py:243
  187.3 7.0 %collective-permute-done.19.refs_2_ = bf16[3,360,128]{2,1,0:T(8,128)(2,1)S(1)} collective-permute-done((bf16[3,360,128]{2,1,0:T(8,128)(2,1)}, bf16[3,360,128]{2,1,0:T(8,128)(2,1)S(1)}, u32[]{:S(2)}, u32[]{:S(2)}) %collective-permute-start.19) | collective-permute-done | bytes 276512 | tf_op jit(solution)/shard_map/out1/ppermute | solution.py:314
  194.3 0.1 collective-permute-start.21
  194.3 5.1 %collective-permute-start.22 = (bf16[3,360,128]{2,1,0:T(8,128)(2,1)}, bf16[3,360,128]{2,1,0:T(8,128)(2,1)S(1)}, u32[]{:S(2)}, u32[]{:S(2)}) collective-permute-start(bf16[3,360,128]{2,1,0:T(8,128)(2,1)} %get-tuple-element.77), channel_id=1, source_target_pairs={{0,2},{1,3},{2,0},{3,1},{4,6},{5,7},{6,4},{7,5},{8,10},{9,11},{10,... | collective-permute-start | bytes 829448 | tf_op jit(solution)/shard_map/out2/ppermute | solution.py:314
  199.4 1.9 collective-permute-start.23
  201.4 15.5 %mlp.7 = (bf16[3,360,128]{2,1,0:T(8,128)(2,1)}, bf16[3,360,128]{2,1,0:T(8,128)(2,1)}, bf16[3,360,128]{2,1,0:T(8,128)(2,1)}, bf16[3,360,128]{2,1,0:T(8,128)(2,1)}) custom-call(s32[1]{0:T(128)} %bitcast.me_ref, bf16[1,3,360,128]{3,2,1,0:T(8,128)(2,1)} %get-tuple-element.74.refs_0_, bf16[1,3,360,128]{3,2,1,0:T(8,128)(2,1)} %copy-done.10, ...), custom_call_target="tpu_custom_call" | custom-call | flops 14949999616 | bytes 1024 | tf_op jit(solution)/shard_map/mlp/pallas_call | solution.py:243
  216.9 1.9 collective-permute-start.24
  218.9 0.6 collective-permute-start.26
  219.5 6.2 %collective-permute-done.22.refs_2_ = bf16[3,360,128]{2,1,0:T(8,128)(2,1)S(1)} collective-permute-done((bf16[3,360,128]{2,1,0:T(8,128)(2,1)}, bf16[3,360,128]{2,1,0:T(8,128)(2,1)S(1)}, u32[]{:S(2)}, u32[]{:S(2)}) %collective-permute-start.22) | collective-permute-done | bytes 276512 | tf_op jit(solution)/shard_map/out2/ppermute | solution.py:314
  225.7 4.4 %add.4.refs_5_ = bf16[192,32,360]{2,1,0:T(8,128)(2,1)} custom-call(s32[1]{0:T(128)} %bitcast.me_ref, bf16[3,360,128]{2,1,0:T(8,128)(2,1)} %get-tuple-element.60.refs_0_, bf16[3,360,128]{2,1,0:T(8,128)(2,1)} %copy-done.14, bf16[3,360,128]{2,1,0:T(8,128)(2,1)} %copy-done.16, bf16[3,360,128]{2,1,0:T(8,128)(2,1)} %copy-done.18, bf16[192,32,360]{2,1,0:T(8,128)(2,1)} %refs_4_.7), custom_call_target="tpu_custom_call" | custom-call | flops 4600000000 | bytes 1024 | tf_op jit(solution)/shard_map/add/pallas_call | solution.py:292
  230.1 4.2 %add.5.refs_5_ = bf16[192,32,360]{2,1,0:T(8,128)(2,1)} custom-call(s32[1]{0:T(128)} %bitcast.me_ref, bf16[3,360,128]{2,1,0:T(8,128)(2,1)} %get-tuple-element.64.refs_0_, bf16[3,360,128]{2,1,0:T(8,128)(2,1)} %copy-done.19, bf16[3,360,128]{2,1,0:T(8,128)(2,1)} %copy-done.20, bf16[3,360,128]{2,1,0:T(8,128)(2,1)} %copy-done.21, ...), custom_call_target="tpu_custom_call", output_to_operand_aliasing={{}: (6, {})} | custom-call | flops 4600000000 | bytes 1024 | tf_op jit(solution)/shard_map/add/pallas_call | solution.py:292
  234.3 4.2 %add.6.refs_5_ = bf16[192,32,360]{2,1,0:T(8,128)(2,1)} custom-call(s32[1]{0:T(128)} %bitcast.me_ref, bf16[3,360,128]{2,1,0:T(8,128)(2,1)} %get-tuple-element.69.refs_0_, bf16[3,360,128]{2,1,0:T(8,128)(2,1)} %copy-done.22, bf16[3,360,128]{2,1,0:T(8,128)(2,1)} %copy-done.23, bf16[3,360,128]{2,1,0:T(8,128)(2,1)} %copy-done.24, ...), custom_call_target="tpu_custom_call", output_to_operand_aliasing={{}: (6, {})} | custom-call | flops 4600000000 | bytes 1024 | tf_op jit(solution)/shard_map/add/pallas_call | solution.py:292
  238.5 9.2 %collective-permute-done.25.refs_2_ = bf16[3,360,128]{2,1,0:T(8,128)(2,1)S(1)} collective-permute-done((bf16[3,360,128]{2,1,0:T(8,128)(2,1)}, bf16[3,360,128]{2,1,0:T(8,128)(2,1)S(1)}, u32[]{:S(2)}, u32[]{:S(2)}) %collective-permute-start.25) | collective-permute-done | bytes 276512 | tf_op jit(solution)/shard_map/out3/ppermute | solution.py:314
  247.8 0.7 copy-done.27
  248.5 0.7 copy-done.28
  249.2 4.2 %add.7 = bf16[192,32,360]{2,1,0:T(8,128)(2,1)} custom-call(s32[1]{0:T(128)} %bitcast.me_ref, bf16[3,360,128]{2,1,0:T(8,128)(2,1)} %get-tuple-element.75.refs_0_, bf16[3,360,128]{2,1,0:T(8,128)(2,1)} %copy-done.25, bf16[3,360,128]{2,1,0:T(8,128)(2,1)} %copy-done.27, bf16[3,360,128]{2,1,0:T(8,128)(2,1)} %copy-done.28, ...), custom_call_target="tpu_custom_call", output_to_operand_aliasing={{}: (6, {})} | custom-call | flops 4600000000 | bytes 1024 | tf_op jit(solution)/shard_map/add/pallas_call | solution.py:292
  (76 shorter events, 0.2 us)
Async XLA Ops:
  2.6 5.0 %copy-start.3 = (bf16[768,192]{0,1:T(8,128)(2,1)S(1)}, bf16[768,192]{0,1:T(8,128)(2,1)}, u32[]{:S(2)}) copy-start(bf16[768,192]{0,1:T(8,128)(2,1)} %param.11) | copy-start | bytes 884740
  4.6 3.1 %copy-start.4 = (bf16[768,192]{0,1:T(8,128)(2,1)S(1)}, bf16[768,192]{0,1:T(8,128)(2,1)}, u32[]{:S(2)}) copy-start(bf16[768,192]{0,1:T(8,128)(2,1)} %param.10) | copy-start | bytes 884740
  4.6 13.3 %collective-permute-start = (bf16[192,32,8]{0,2,1:T(8,128)(2,1)}, bf16[192,32,8]{0,2,1:T(8,128)(2,1)S(1)}, u32[]{:S(2)}, u32[]{:S(2)}) collective-permute-start(bf16[192,32,8]{0,2,1:T(8,128)(2,1)} %copy.35), channel_id=1, source_target_pairs={{0,4},{4,8},{8,12},{12,0},{1,5},{5,9},{9,13},{13,1},{2,6},{6,10},{... | collective-permute-start | bytes 294920 | tf_op jit(solution)/shard_map/halo/ppermute | solution.py:314
  5.8 13.5 %collective-permute-start.1 = (bf16[192,32,8]{0,2,1:T(8,128)(2,1)S(1)}, bf16[192,32,8]{0,2,1:T(8,128)(2,1)S(1)}, u32[]{:S(2)}, u32[]{:S(2)}) collective-permute-start(bf16[192,32,8]{0,2,1:T(8,128)(2,1)S(1)} %copy.36), channel_id=1, source_target_pairs={{0,12},{4,0},{8,4},{12,8},{1,13},{5,1},{9,5},{13,9},{2,14},{6,2},{... | collective-permute-start | bytes 294920 | tf_op jit(solution)/shard_map/halo/ppermute | solution.py:314
  7.7 8.6 %copy-start.2 = (bf16[1,384,768]{2,1,0:T(8,128)(2,1)}, bf16[1,384,768]{2,1,0:T(8,128)(2,1)S(1)}, u32[]{:S(2)}) copy-start(bf16[1,384,768]{2,1,0:T(8,128)(2,1)S(1)} %maximum_bitcast_fusion.refs_0_) | copy-start | bytes 1769476
  7.7 30.0 %collective-permute-start.2 = (bf16[1,384,768]{2,1,0:T(8,128)(2,1)S(1)}, bf16[1,384,768]{2,1,0:T(8,128)(2,1)}, u32[]{:S(2)}, u32[]{:S(2)}) collective-permute-start(bf16[1,384,768]{2,1,0:T(8,128)(2,1)S(1)} %maximum_bitcast_fusion.refs_0_), channel_id=1, source_target_pairs={{0,2},{1,3},{2,0},{3,1},{4,6},{5,7},{6,4},{7,5},{8,10},{9,11},{10,... | collective-permute-start | bytes 1769480 | tf_op jit(solution)/shard_map/wz/ppermute | solution.py:318
  8.1 29.7 %collective-permute-start.3 = (bf16[1,384,768]{2,1,0:T(8,128)(2,1)S(1)}, bf16[1,384,768]{2,1,0:T(8,128)(2,1)}, u32[]{:S(2)}, u32[]{:S(2)}) collective-permute-start(bf16[1,384,768]{2,1,0:T(8,128)(2,1)S(1)} %maximum_bitcast_fusion.refs_0_), channel_id=1, source_target_pairs={{0,1},{1,0},{2,3},{3,2},{4,5},{5,4},{6,7},{7,6},{8,9},{9,8},{10,11... | collective-permute-start | bytes 1769480 | tf_op jit(solution)/shard_map/wz/ppermute | solution.py:318
  8.3 29.5 %collective-permute-start.4 = (bf16[1,384,768]{2,1,0:T(8,128)(2,1)S(1)}, bf16[1,384,768]{2,1,0:T(8,128)(2,1)S(1)}, u32[]{:S(2)}, u32[]{:S(2)}) collective-permute-start(bf16[1,384,768]{2,1,0:T(8,128)(2,1)S(1)} %maximum_bitcast_fusion.refs_0_), channel_id=1, source_target_pairs={{0,8},{4,12},{8,0},{12,4},{1,9},{5,13},{9,1},{13,5},{2,10},{6,14},... | collective-permute-start | bytes 1769480 | tf_op jit(solution)/shard_map/wx0/ppermute | solution.py:318
  10.0 6.3 %copy-start.5 = (f32[9,192]{1,0:T(8,128)S(1)}, f32[9,192]{1,0:T(8,128)}, u32[]{:S(2)}) copy-start(f32[9,192]{1,0:T(8,128)} %param.8) | copy-start | bytes 20740
  10.0 7.0 %copy-start.6 = (f32[9,192]{1,0:T(8,128)S(1)}, f32[9,192]{1,0:T(8,128)}, u32[]{:S(2)}) copy-start(f32[9,192]{1,0:T(8,128)} %param.7) | copy-start | bytes 20740
  30.6 49.8 %all-to-all-start.1 = ((bf16[4,3,360,128]{3,2,1,0:T(8,128)(2,1)}), bf16[4,3,360,128]{3,2,1,0:T(8,128)(2,1)S(1)}, u32[]{:S(2)}, u32[]{:S(2)}) async-start(bf16[4,3,360,128]{3,2,1,0:T(8,128)(2,1)} %conv.4), calls=%async_computation.1 | async-start | bytes 2211840 | tf_op jit(solution)/shard_map/in0/all_to_all | solution.py:390
  37.7 10.6 %copy-start.8 = (bf16[1,384,768]{2,1,0:T(8,128)(2,1)}, bf16[1,384,768]{2,1,0:T(8,128)(2,1)S(1)}, u32[]{:S(2)}) copy-start(bf16[1,384,768]{2,1,0:T(8,128)(2,1)S(1)} %collective-permute-done.4.refs_1_) | copy-start | bytes 1769476
  48.4 26.2 %collective-permute-start.5 = (bf16[1,384,768]{2,1,0:T(8,128)(2,1)}, bf16[1,384,768]{2,1,0:T(8,128)(2,1)S(1)}, u32[]{:S(2)}, u32[]{:S(2)}) collective-permute-start(bf16[1,384,768]{2,1,0:T(8,128)(2,1)} %collective-permute-done.2.refs_0_), channel_id=1, source_target_pairs={{0,1},{1,0},{2,3},{3,2},{4,5},{5,4},{6,7},{7,6},{8,9},{9,8},{10,11... | collective-permute-start | bytes 1769480 | tf_op jit(solution)/shard_map/wz1/ppermute | solution.py:318
  49.0 13.4 %copy-start.26 = (bf16[1,3,360,128]{3,2,1,0:T(8,128)(2,1)S(1)}, bf16[1,3,360,128]{3,2,1,0:T(8,128)(2,1)}, u32[]{:S(2)}) copy-start(bf16[1,3,360,128]{3,2,1,0:T(8,128)(2,1)} %get-tuple-element.55) | copy-start | bytes 829444
  59.4 36.1 %collective-permute-start.6 = (bf16[1,3,360,128]{3,2,1,0:T(8,128)(2,1)}, bf16[1,3,360,128]{3,2,1,0:T(8,128)(2,1)S(1)}, u32[]{:S(2)}, u32[]{:S(2)}) collective-permute-start(bf16[1,3,360,128]{3,2,1,0:T(8,128)(2,1)} %get-tuple-element.53), channel_id=1, source_target_pairs={{0,1},{1,2},{2,3},{3,0},{4,5},{5,6},{6,7},{7,4},{8,9},{9,10},{10,1... | collective-permute-start | bytes 829448 | tf_op jit(solution)/shard_map/in1/ppermute | solution.py:314
  60.9 34.7 %collective-permute-start.7 = (bf16[1,3,360,128]{3,2,1,0:T(8,128)(2,1)}, bf16[1,3,360,128]{3,2,1,0:T(8,128)(2,1)S(1)}, u32[]{:S(2)}, u32[]{:S(2)}) collective-permute-start(bf16[1,3,360,128]{3,2,1,0:T(8,128)(2,1)} %get-tuple-element.54), channel_id=1, source_target_pairs={{0,2},{1,3},{2,0},{3,1},{4,6},{5,7},{6,4},{7,5},{8,10},{9,11},{10,... | collective-permute-start | bytes 829448 | tf_op jit(solution)/shard_map/in1/ppermute | solution.py:314
  62.3 33.2 %collective-permute-start.8 = (bf16[1,3,360,128]{3,2,1,0:T(8,128)(2,1)S(1)}, bf16[1,3,360,128]{3,2,1,0:T(8,128)(2,1)S(1)}, u32[]{:S(2)}, u32[]{:S(2)}) collective-permute-start(bf16[1,3,360,128]{3,2,1,0:T(8,128)(2,1)S(1)} %copy-done.26), channel_id=1, source_target_pairs={{0,3},{1,0},{2,1},{3,2},{4,7},{5,4},{6,5},{7,6},{8,11},{9,8},{10,9... | collective-permute-start | bytes 829448 | tf_op jit(solution)/shard_map/in1/ppermute | solution.py:314
  74.6 0.8 copy-start.9
  78.6 40.2 %collective-permute-start.10 = (bf16[3,384,768]{2,1,0:T(8,128)(2,1)}, bf16[3,384,768]{2,1,0:T(8,128)(2,1)}, u32[]{:S(2)}, u32[]{:S(2)}) collective-permute-start(bf16[3,384,768]{2,1,0:T(8,128)(2,1)} %stack.2.refs_2_), channel_id=1, source_target_pairs={{0,8},{4,12},{8,0},{12,4},{1,9},{5,13},{9,1},{13,5},{2,10},{6,14},... | collective-permute-start | bytes 5308424 | tf_op jit(solution)/shard_map/wx1/ppermute | solution.py:318
  80.4 15.1 %copy-start.1 = (bf16[4,3,360,128]{3,2,1,0:T(8,128)(2,1)}, bf16[4,3,360,128]{3,2,1,0:T(8,128)(2,1)S(1)}, u32[]{:S(2)}) copy-start(bf16[4,3,360,128]{3,2,1,0:T(8,128)(2,1)S(1)} %all-to-all-done.1.refs_0_) | copy-start | bytes 3317764
  80.4 38.4 %all-to-all-start = ((bf16[4,3,360,128]{3,2,1,0:T(8,128)(2,1)}), bf16[4,3,360,128]{3,2,1,0:T(8,128)(2,1)S(1)}, u32[]{:S(2)}, u32[]{:S(2)}) async-start(bf16[4,3,360,128]{3,2,1,0:T(8,128)(2,1)} %conv.6), calls=%async_computation | async-start | bytes 2211840 | tf_op jit(solution)/shard_map/in2/all_to_all | solution.py:390
  95.5 23.4 %copy-start.7 = (f32[768]{0:T(1024)S(1)}, f32[768]{0:T(1024)}, u32[]{:S(2)}) copy-start(f32[768]{0:T(1024)} %param.9) | copy-start | bytes 9220
  95.5 10.3 %copy-start.11 = (bf16[1,3,360,128]{3,2,1,0:T(8,128)(2,1)}, bf16[1,3,360,128]{3,2,1,0:T(8,128)(2,1)S(1)}, u32[]{:S(2)}) copy-start(bf16[1,3,360,128]{3,2,1,0:T(8,128)(2,1)S(1)} %collective-permute-done.6.refs_1_) | copy-start | bytes 829444
  95.5 10.3 %copy-start.12 = (bf16[1,3,360,128]{3,2,1,0:T(8,128)(2,1)}, bf16[1,3,360,128]{3,2,1,0:T(8,128)(2,1)S(1)}, u32[]{:S(2)}) copy-start(bf16[1,3,360,128]{3,2,1,0:T(8,128)(2,1)S(1)} %collective-permute-done.7.refs_2_) | copy-start | bytes 829444
  95.6 10.3 %copy-start.13 = (bf16[1,3,360,128]{3,2,1,0:T(8,128)(2,1)}, bf16[1,3,360,128]{3,2,1,0:T(8,128)(2,1)S(1)}, u32[]{:S(2)}) copy-start(bf16[1,3,360,128]{3,2,1,0:T(8,128)(2,1)S(1)} %collective-permute-done.8.refs_3_) | copy-start | bytes 829444
  95.6 30.5 %collective-permute-start.9 = (bf16[5,384,768]{2,1,0:T(8,128)(2,1)}, bf16[5,384,768]{2,1,0:T(8,128)(2,1)}, u32[]{:S(2)}, u32[]{:S(2)}) collective-permute-start(bf16[5,384,768]{2,1,0:T(8,128)(2,1)} %stack.3.refs_2_.refs_5_), channel_id=1, source_target_pairs={{0,4},{4,0},{8,12},{12,8},{1,5},{5,1},{9,13},{13,9},{2,6},{6,2},{1... | collective-permute-start | bytes 8847368 | tf_op jit(solution)/shard_map/wc0/ppermute | solution.py:318
  105.9 12.9 %collective-permute-start.11 = (bf16[1,3,360,128]{3,2,1,0:T(8,128)(2,1)}, bf16[1,3,360,128]{3,2,1,0:T(8,128)(2,1)S(1)}, u32[]{:S(2)}, u32[]{:S(2)}) collective-permute-start(bf16[1,3,360,128]{3,2,1,0:T(8,128)(2,1)} %get-tuple-element.58), channel_id=1, source_target_pairs={{0,1},{1,2},{2,3},{3,0},{4,5},{5,6},{6,7},{7,4},{8,9},{9,10},{10,1... | collective-permute-start | bytes 829448 | tf_op jit(solution)/shard_map/in3/ppermute | solution.py:314
  118.8 22.7 %copy-start.10 = (bf16[1,3,360,128]{3,2,1,0:T(8,128)(2,1)}, bf16[1,3,360,128]{3,2,1,0:T(8,128)(2,1)S(1)}, u32[]{:S(2)}) copy-start(bf16[1,3,360,128]{3,2,1,0:T(8,128)(2,1)S(1)} %collective-permute-done.11.refs_1_) | copy-start | bytes 829444
  118.8 22.7 %copy-start = (bf16[4,3,360,128]{3,2,1,0:T(8,128)(2,1)}, bf16[4,3,360,128]{3,2,1,0:T(8,128)(2,1)S(1)}, u32[]{:S(2)}) copy-start(bf16[4,3,360,128]{3,2,1,0:T(8,128)(2,1)S(1)} %all-to-all-done.refs_0_) | copy-start | bytes 3317764
  118.8 7.3 %collective-permute-start.12 = (bf16[3,384,768]{2,1,0:T(8,128)(2,1)}, bf16[3,384,768]{2,1,0:T(8,128)(2,1)}, u32[]{:S(2)}, u32[]{:S(2)}) collective-permute-start(bf16[3,384,768]{2,1,0:T(8,128)(2,1)} %collective-permute-done.10.refs_4_.refs_7_), channel_id=1, source_target_pairs={{0,4},{4,0},{8,12},{12,8},{1,5},{5,1},{9,13},{13,9},{2,6},{6,2},{1... | collective-permute-start | bytes 5308424 | tf_op jit(solution)/shard_map/wc1/ppermute | solution.py:318
  120.0 23.0 %collective-permute-start.13 = (bf16[1,3,360,128]{3,2,1,0:T(8,128)(2,1)}, bf16[1,3,360,128]{3,2,1,0:T(8,128)(2,1)S(1)}, u32[]{:S(2)}, u32[]{:S(2)}) collective-permute-start(bf16[1,3,360,128]{3,2,1,0:T(8,128)(2,1)} %get-tuple-element.61), channel_id=1, source_target_pairs={{0,2},{1,3},{2,0},{3,1},{4,6},{5,7},{6,4},{7,5},{8,10},{9,11},{10,... | collective-permute-start | bytes 829448 | tf_op jit(solution)/shard_map/in3/ppermute | solution.py:314
  123.7 19.3 %collective-permute-start.14 = (bf16[1,3,360,128]{3,2,1,0:T(8,128)(2,1)}, bf16[1,3,360,128]{3,2,1,0:T(8,128)(2,1)S(1)}, u32[]{:S(2)}, u32[]{:S(2)}) collective-permute-start(bf16[1,3,360,128]{3,2,1,0:T(8,128)(2,1)} %get-tuple-element.62), channel_id=1, source_target_pairs={{0,3},{1,0},{2,1},{3,2},{4,7},{5,4},{6,5},{7,6},{8,11},{9,8},{10,9... | collective-permute-start | bytes 829448 | tf_op jit(solution)/shard_map/in3/ppermute | solution.py:314
  143.0 20.2 %copy-start.15 = (bf16[1,3,360,128]{3,2,1,0:T(8,128)(2,1)}, bf16[1,3,360,128]{3,2,1,0:T(8,128)(2,1)S(1)}, u32[]{:S(2)}) copy-start(bf16[1,3,360,128]{3,2,1,0:T(8,128)(2,1)S(1)} %collective-permute-done.13.refs_2_) | copy-start | bytes 829444
  143.0 20.2 %copy-start.17 = (bf16[1,3,360,128]{3,2,1,0:T(8,128)(2,1)}, bf16[1,3,360,128]{3,2,1,0:T(8,128)(2,1)S(1)}, u32[]{:S(2)}) copy-start(bf16[1,3,360,128]{3,2,1,0:T(8,128)(2,1)S(1)} %collective-permute-done.14.refs_3_) | copy-start | bytes 829444
  143.0 22.1 %collective-permute-start.15 = (bf16[3,360,128]{2,1,0:T(8,128)(2,1)}, bf16[3,360,128]{2,1,0:T(8,128)(2,1)S(1)}, u32[]{:S(2)}, u32[]{:S(2)}) collective-permute-start(bf16[3,360,128]{2,1,0:T(8,128)(2,1)} %get-tuple-element.65), channel_id=1, source_target_pairs={{0,1},{1,2},{2,3},{3,0},{4,5},{5,6},{6,7},{7,4},{8,9},{9,10},{10,1... | collective-permute-start | bytes 829448 | tf_op jit(solution)/shard_map/out0/ppermute | solution.py:314
  144.1 27.5 %collective-permute-start.16 = (bf16[3,360,128]{2,1,0:T(8,128)(2,1)}, bf16[3,360,128]{2,1,0:T(8,128)(2,1)S(1)}, u32[]{:S(2)}, u32[]{:S(2)}) collective-permute-start(bf16[3,360,128]{2,1,0:T(8,128)(2,1)} %get-tuple-element.66), channel_id=1, source_target_pairs={{0,2},{1,3},{2,0},{3,1},{4,6},{5,7},{6,4},{7,5},{8,10},{9,11},{10,... | collective-permute-start | bytes 829448 | tf_op jit(solution)/shard_map/out0/ppermute | solution.py:314
  145.7 25.9 %collective-permute-start.17 = (bf16[3,360,128]{2,1,0:T(8,128)(2,1)}, bf16[3,360,128]{2,1,0:T(8,128)(2,1)S(1)}, u32[]{:S(2)}, u32[]{:S(2)}) collective-permute-start(bf16[3,360,128]{2,1,0:T(8,128)(2,1)} %get-tuple-element.67), channel_id=1, source_target_pairs={{0,3},{1,0},{2,1},{3,2},{4,7},{5,4},{6,5},{7,6},{8,11},{9,8},{10,9... | collective-permute-start | bytes 829448 | tf_op jit(solution)/shard_map/out0/ppermute | solution.py:314
  163.3 24.0 %collective-permute-start.18 = (bf16[3,360,128]{2,1,0:T(8,128)(2,1)}, bf16[3,360,128]{2,1,0:T(8,128)(2,1)S(1)}, u32[]{:S(2)}, u32[]{:S(2)}) collective-permute-start(bf16[3,360,128]{2,1,0:T(8,128)(2,1)} %get-tuple-element.70), channel_id=1, source_target_pairs={{0,1},{1,2},{2,3},{3,0},{4,5},{5,6},{6,7},{7,4},{8,9},{9,10},{10,1... | collective-permute-start | bytes 829448 | tf_op jit(solution)/shard_map/out1/ppermute | solution.py:314
  165.1 29.1 %collective-permute-start.19 = (bf16[3,360,128]{2,1,0:T(8,128)(2,1)}, bf16[3,360,128]{2,1,0:T(8,128)(2,1)S(1)}, u32[]{:S(2)}, u32[]{:S(2)}) collective-permute-start(bf16[3,360,128]{2,1,0:T(8,128)(2,1)} %get-tuple-element.71), channel_id=1, source_target_pairs={{0,2},{1,3},{2,0},{3,1},{4,6},{5,7},{6,4},{7,5},{8,10},{9,11},{10,... | collective-permute-start | bytes 829448 | tf_op jit(solution)/shard_map/out1/ppermute | solution.py:314
  165.1 22.1 %copy-start.14 = (bf16[3,360,128]{2,1,0:T(8,128)(2,1)}, bf16[3,360,128]{2,1,0:T(8,128)(2,1)S(1)}, u32[]{:S(2)}) copy-start(bf16[3,360,128]{2,1,0:T(8,128)(2,1)S(1)} %collective-permute-done.15.refs_1_) | copy-start | bytes 829444
  165.1 29.1 %collective-permute-start.20 = (bf16[3,360,128]{2,1,0:T(8,128)(2,1)}, bf16[3,360,128]{2,1,0:T(8,128)(2,1)S(1)}, u32[]{:S(2)}, u32[]{:S(2)}) collective-permute-start(bf16[3,360,128]{2,1,0:T(8,128)(2,1)} %get-tuple-element.72), channel_id=1, source_target_pairs={{0,3},{1,0},{2,1},{3,2},{4,7},{5,4},{6,5},{7,6},{8,11},{9,8},{10,9... | collective-permute-start | bytes 829448 | tf_op jit(solution)/shard_map/out1/ppermute | solution.py:314
  171.6 15.7 %copy-start.16 = (bf16[3,360,128]{2,1,0:T(8,128)(2,1)}, bf16[3,360,128]{2,1,0:T(8,128)(2,1)S(1)}, u32[]{:S(2)}) copy-start(bf16[3,360,128]{2,1,0:T(8,128)(2,1)S(1)} %collective-permute-done.16.refs_2_) | copy-start | bytes 829444
  171.6 15.7 %copy-start.18 = (bf16[3,360,128]{2,1,0:T(8,128)(2,1)}, bf16[3,360,128]{2,1,0:T(8,128)(2,1)S(1)}, u32[]{:S(2)}) copy-start(bf16[3,360,128]{2,1,0:T(8,128)(2,1)S(1)} %collective-permute-done.17.refs_3_) | copy-start | bytes 829444
  187.3 29.6 %copy-start.19 = (bf16[3,360,128]{2,1,0:T(8,128)(2,1)}, bf16[3,360,128]{2,1,0:T(8,128)(2,1)S(1)}, u32[]{:S(2)}) copy-start(bf16[3,360,128]{2,1,0:T(8,128)(2,1)S(1)} %collective-permute-done.18.refs_1_) | copy-start | bytes 829444
  194.2 22.7 %copy-start.20 = (bf16[3,360,128]{2,1,0:T(8,128)(2,1)}, bf16[3,360,128]{2,1,0:T(8,128)(2,1)S(1)}, u32[]{:S(2)}) copy-start(bf16[3,360,128]{2,1,0:T(8,128)(2,1)S(1)} %collective-permute-done.19.refs_2_) | copy-start | bytes 829444
  194.3 22.7 %copy-start.21 = (bf16[3,360,128]{2,1,0:T(8,128)(2,1)}, bf16[3,360,128]{2,1,0:T(8,128)(2,1)S(1)}, u32[]{:S(2)}) copy-start(bf16[3,360,128]{2,1,0:T(8,128)(2,1)S(1)} %collective-permute-done.20.refs_3_) | copy-start | bytes 829444
  194.3 24.6 %collective-permute-start.21 = (bf16[3,360,128]{2,1,0:T(8,128)(2,1)}, bf16[3,360,128]{2,1,0:T(8,128)(2,1)S(1)}, u32[]{:S(2)}, u32[]{:S(2)}) collective-permute-start(bf16[3,360,128]{2,1,0:T(8,128)(2,1)} %get-tuple-element.76), channel_id=1, source_target_pairs={{0,1},{1,2},{2,3},{3,0},{4,5},{5,6},{6,7},{7,4},{8,9},{9,10},{10,1... | collective-permute-start | bytes 829448 | tf_op jit(solution)/shard_map/out2/ppermute | solution.py:314
  194.3 31.4 %collective-permute-start.22 = (bf16[3,360,128]{2,1,0:T(8,128)(2,1)}, bf16[3,360,128]{2,1,0:T(8,128)(2,1)S(1)}, u32[]{:S(2)}, u32[]{:S(2)}) collective-permute-start(bf16[3,360,128]{2,1,0:T(8,128)(2,1)} %get-tuple-element.77), channel_id=1, source_target_pairs={{0,2},{1,3},{2,0},{3,1},{4,6},{5,7},{6,4},{7,5},{8,10},{9,11},{10,... | collective-permute-start | bytes 829448 | tf_op jit(solution)/shard_map/out2/ppermute | solution.py:314
  199.4 26.3 %collective-permute-start.23 = (bf16[3,360,128]{2,1,0:T(8,128)(2,1)}, bf16[3,360,128]{2,1,0:T(8,128)(2,1)S(1)}, u32[]{:S(2)}, u32[]{:S(2)}) collective-permute-start(bf16[3,360,128]{2,1,0:T(8,128)(2,1)} %get-tuple-element.78), channel_id=1, source_target_pairs={{0,3},{1,0},{2,1},{3,2},{4,7},{5,4},{6,5},{7,6},{8,11},{9,8},{10,9... | collective-permute-start | bytes 829448 | tf_op jit(solution)/shard_map/out2/ppermute | solution.py:314
  216.9 21.6 %collective-permute-start.24 = (bf16[3,360,128]{2,1,0:T(8,128)(2,1)}, bf16[3,360,128]{2,1,0:T(8,128)(2,1)S(1)}, u32[]{:S(2)}, u32[]{:S(2)}) collective-permute-start(bf16[3,360,128]{2,1,0:T(8,128)(2,1)} %get-tuple-element.80), channel_id=1, source_target_pairs={{0,1},{1,2},{2,3},{3,0},{4,5},{5,6},{6,7},{7,4},{8,9},{9,10},{10,1... | collective-permute-start | bytes 829448 | tf_op jit(solution)/shard_map/out3/ppermute | solution.py:314
  218.9 28.9 %collective-permute-start.25 = (bf16[3,360,128]{2,1,0:T(8,128)(2,1)}, bf16[3,360,128]{2,1,0:T(8,128)(2,1)S(1)}, u32[]{:S(2)}, u32[]{:S(2)}) collective-permute-start(bf16[3,360,128]{2,1,0:T(8,128)(2,1)} %get-tuple-element.81), channel_id=1, source_target_pairs={{0,2},{1,3},{2,0},{3,1},{4,6},{5,7},{6,4},{7,5},{8,10},{9,11},{10,... | collective-permute-start | bytes 829448 | tf_op jit(solution)/shard_map/out3/ppermute | solution.py:314
  218.9 11.2 %copy-start.22 = (bf16[3,360,128]{2,1,0:T(8,128)(2,1)}, bf16[3,360,128]{2,1,0:T(8,128)(2,1)S(1)}, u32[]{:S(2)}) copy-start(bf16[3,360,128]{2,1,0:T(8,128)(2,1)S(1)} %collective-permute-done.21.refs_1_) | copy-start | bytes 829444
  218.9 28.9 %collective-permute-start.26 = (bf16[3,360,128]{2,1,0:T(8,128)(2,1)}, bf16[3,360,128]{2,1,0:T(8,128)(2,1)S(1)}, u32[]{:S(2)}, u32[]{:S(2)}) collective-permute-start(bf16[3,360,128]{2,1,0:T(8,128)(2,1)} %get-tuple-element.82), channel_id=1, source_target_pairs={{0,3},{1,0},{2,1},{3,2},{4,7},{5,4},{6,5},{7,6},{8,11},{9,8},{10,9... | collective-permute-start | bytes 829448 | tf_op jit(solution)/shard_map/out3/ppermute | solution.py:314
  225.7 4.4 %copy-start.23 = (bf16[3,360,128]{2,1,0:T(8,128)(2,1)}, bf16[3,360,128]{2,1,0:T(8,128)(2,1)S(1)}, u32[]{:S(2)}) copy-start(bf16[3,360,128]{2,1,0:T(8,128)(2,1)S(1)} %collective-permute-done.22.refs_2_) | copy-start | bytes 829444
  225.7 4.4 %copy-start.24 = (bf16[3,360,128]{2,1,0:T(8,128)(2,1)}, bf16[3,360,128]{2,1,0:T(8,128)(2,1)S(1)}, u32[]{:S(2)}) copy-start(bf16[3,360,128]{2,1,0:T(8,128)(2,1)S(1)} %collective-permute-done.23.refs_3_) | copy-start | bytes 829444
  238.5 9.2 %copy-start.25 = (bf16[3,360,128]{2,1,0:T(8,128)(2,1)}, bf16[3,360,128]{2,1,0:T(8,128)(2,1)S(1)}, u32[]{:S(2)}) copy-start(bf16[3,360,128]{2,1,0:T(8,128)(2,1)S(1)} %collective-permute-done.24.refs_1_) | copy-start | bytes 829444
  247.8 0.7 copy-start.27
  248.5 0.7 copy-start.28

commit v5 on v4

--- a/solution.py
+++ b/solution.py
@@ -373,8 +373,6 @@
     while bit > 1:
         bits.append(bit)
         bit //= 2
-    with jax.named_scope("wx0"):
-        across = exchanged(shard, "tile", bits[0])
     field = jnp.transpose(weather, (1, 0, 2))
     before = jnp.transpose(before, (1, 0, 2))
     after = jnp.transpose(after, (1, 0, 2))
@@ -393,7 +391,9 @@
     by_cell = []
     spatial, cells = spread(0)
     by_cell.append(cells)
-    lon, far, near, across = after_all((lon, far, near, across), spatial[0])
+    lon, far, near = after_all((lon, far, near), spatial[0])
+    with jax.named_scope("wx0"):
+        across = exchanged(after_all(shard, spatial[0]), "tile", bits[0])
     with jax.named_scope("wz1"):
         rest = [exchanged(piece, "chan", 1) for piece in far[1:]]
     spatial, cells = spread(1)

time: 254 us -> 253 us (level)
    unnamed x63 -> x55, local copies, waits for them, and re-layouts: 13.3 us -> 12.5 us
where the time goes in v5:
time: 253 us; the launch traced here: 252 us
  Pallas kernels  128 us (51%)
  waiting for transfers between devices  55 us (22%)
  starting transfers between devices  49.5 us (20%)
  local copies, waits for them, and re-layouts  19.2 us (8%)
    pallas_call x4, Pallas kernels, mlp(): pl.pallas_call(functools.partial(mlp_kernel, packing, sources, arrays, co...  62.2 us
    ppermute x20, waiting for transfers between devices, shifted(): lax.ppermute(array, axis, [(i, (i + shift) % count) for i in range(count)])  41.5 us
    pallas_call x4, Pallas kernels, convolve(): pl.pallas_call(functools.partial(conv_kernel, packing, sources, row_count...  40.9 us
    ppermute x20, starting transfers between devices, shifted(): lax.ppermute(array, axis, [(i, (i + shift) % count) for i in range(count)])  28.7 us
    all_to_all x2, starting transfers between devices, spread(): lax.all_to_all(spatial[0], 'chan', split_axis=0, concat_axis=0, tiled=True)  17.9 us
    pallas_call x4, Pallas kernels, add_rows(): pl.pallas_call(functools.partial(add_kernel, packing, sources), grid_spec...  17 us
    ppermute x7, waiting for transfers between devices, exchanged(): lax.ppermute(array, axis, [(i, i ^ bit) for i in range(lax.axis_size(axis...  13.5 us
    unnamed x55, local copies, waits for them, and re-layouts  12.5 us
  transfers between devices with their start and end apart: 29, of which 7 were waited for; matrix products, arithmetic and copies ran while one was open for 5% of the time, Pallas kernels for 49%

profile of v5, /device:TPU:24, one launch (start us, length us, event | category | flops | bytes accessed | tf_op | source)
XLA Modules:
  0.0 251.9 jit_solution(8179583708212103636)
XLA Ops:
  0.0 2.6 %fusion = (bf16[192,32,8]{2,1,0:T(8,128)(2,1)S(1)}, bf16[192,32,8]{2,1,0:T(8,128)(2,1)S(1)}) fusion(bf16[192,32,360]{2,1,0:T(8,128)(2,1)} %refs_4_.7), kind=kLoop, calls=%fused_computation.2 | loop fusion | bytes 393216 | tf_op jit(solution)/shard_map/halo/slice | solution.py:362
  2.6 0.0 copy-start.3
  2.6 1.9 copy.35
  4.5 0.0 collective-permute-start
  4.5 1.3 copy.36
  5.8 1.8 collective-permute-start.1
  7.7 0.4 collective-permute-start.2
  8.1 0.2 collective-permute-start.3
  8.3 6.3 %copy.38 = bf16[192,32,360]{2,0,1:T(8,128)(2,1)} copy(bf16[192,32,360]{2,1,0:T(8,128)(2,1)} %refs_4_.7) | data formatting | bytes 8847360 | tf_op args[0]
  14.5 0.8 copy.30
  15.3 0.7 copy.29
  16.0 1.5 copy.26
  17.5 1.6 copy.28
  19.1 9.8 %conv.4 = bf16[4,3,360,128]{3,2,1,0:T(8,128)(2,1)} custom-call(s32[1]{0:T(128)} %bitcast.me_ref, bf16[32,192,360]{2,1,0:T(8,128)(2,1)} %bitcast.12, bf16[32,192,8]{2,1,0:T(8,128)(2,1)} %bitcast.22, bf16[32,192,8]{2,1,0:T(8,128)(2,1)} %bitcast.32, bf16[32,192,360]{2,1,0:T(8,128)(2,1)} %bitcast.13, bf16[32,192,8]{2,1,0:T(8,128)(2,1)} %bitcast.23, ...), custom_call_target="tpu_custom_call" | custom-call | flops 13799999488 | bytes 1024 | tf_op jit(solution)/shard_map/conv/pallas_call | solution.py:139
  28.9 7.4 %all-to-all-start.1 = ((bf16[4,3,360,128]{3,2,1,0:T(8,128)(2,1)}), bf16[4,3,360,128]{3,2,1,0:T(8,128)(2,1)S(1)}, u32[]{:S(2)}, u32[]{:S(2)}) async-start(bf16[4,3,360,128]{3,2,1,0:T(8,128)(2,1)} %conv.4), calls=%async_computation.1 | async-start | bytes 2211840 | tf_op jit(solution)/shard_map/in0/all_to_all | solution.py:388
  36.2 1.5 collective-permute-start.5
  37.7 0.0 collective-permute-done.2.refs_0_
  37.7 0.0 collective-permute-done.3.refs_1_
  37.7 10.6 %conv.5 = (bf16[1,3,360,128]{3,2,1,0:T(8,128)(2,1)}, bf16[1,3,360,128]{3,2,1,0:T(8,128)(2,1)}, bf16[1,3,360,128]{3,2,1,0:T(8,128)(2,1)}, bf16[1,3,360,128]{3,2,1,0:T(8,128)(2,1)}) custom-call(s32[1]{0:T(128)} %bitcast.me_ref, bf16[32,192,360]{2,1,0:T(8,128)(2,1)} %bitcast.14, bf16[32,192,8]{2,1,0:T(8,128)(2,1)} %bitcast.24, bf16[32,192,8]{2,1,0:T(8,128)(2,1)} %bitcast.34, ...), custom_call_target="tpu_custom_call" | custom-call | flops 13799999488 | bytes 1024 | tf_op jit(solution)/shard_map/conv/pallas_call | solution.py:139
  48.4 0.6 collective-permute-start.4
  49.0 10.4 %conv.6 = bf16[4,3,360,128]{3,2,1,0:T(8,128)(2,1)} custom-call(s32[1]{0:T(128)} %bitcast.me_ref, bf16[32,192,360]{2,1,0:T(8,128)(2,1)} %bitcast.17, bf16[32,192,8]{2,1,0:T(8,128)(2,1)} %bitcast.27, bf16[32,192,8]{2,1,0:T(8,128)(2,1)} %bitcast.37, bf16[32,192,360]{2,1,0:T(8,128)(2,1)} %bitcast.18, bf16[32,192,8]{2,1,0:T(8,128)(2,1)} %bitcast.28, ...), custom_call_target="tpu_custom_call" | custom-call | flops 13799999488 | bytes 1024 | tf_op jit(solution)/shard_map/conv/pallas_call | solution.py:139
  59.4 1.5 collective-permute-start.6
  60.8 1.5 collective-permute-start.7
  62.3 0.0 collective-permute-start.8
  62.3 0.0 collective-permute-done.5.refs_1_
  62.3 13.4 %collective-permute-done.4.refs_2_ = bf16[1,384,768]{2,1,0:T(8,128)(2,1)} collective-permute-done((bf16[1,384,768]{2,1,0:T(8,128)(2,1)S(1)}, bf16[1,384,768]{2,1,0:T(8,128)(2,1)}, u32[]{:S(2)}, u32[]{:S(2)}) %collective-permute-start.4) | collective-permute-done | bytes 589856 | tf_op jit(solution)/shard_map/wz1/ppermute | solution.py:318
  75.8 3.2 %stack.2.refs_2_ = bf16[3,384,768]{2,1,0:T(8,128)(2,1)} custom-call(bf16[1,384,768]{2,1,0:T(8,128)(2,1)} %copy-done.8, bf16[1,384,768]{2,1,0:T(8,128)(2,1)} %collective-permute-done.3.refs_1_, bf16[1,384,768]{2,1,0:T(8,128)(2,1)} %collective-permute-done.4.refs_2_), custom_call_target="tpu_custom_call" | custom-call | flops 14949999616 | bytes 1024 | tf_op jit(solution)/shard_map/stack/pallas_call | solution.py:340
  79.0 0.0 collective-permute-start.10
  79.0 10.6 %all-to-all-start = ((bf16[4,3,360,128]{3,2,1,0:T(8,128)(2,1)}), bf16[4,3,360,128]{3,2,1,0:T(8,128)(2,1)S(1)}, u32[]{:S(2)}, u32[]{:S(2)}) async-start(bf16[4,3,360,128]{3,2,1,0:T(8,128)(2,1)} %conv.6), calls=%async_computation | async-start | bytes 2211840 | tf_op jit(solution)/shard_map/in2/all_to_all | solution.py:388
  89.6 4.6 %stack.3.refs_2_.refs_5_ = bf16[5,384,768]{2,1,0:T(8,128)(2,1)} custom-call(bf16[1,384,768]{2,1,0:T(8,128)(2,1)} %copy-done.2, bf16[1,384,768]{2,1,0:T(8,128)(2,1)} %copy-done.9, bf16[3,384,768]{2,1,0:T(8,128)(2,1)} %stack.2.refs_2_), custom_call_target="tpu_custom_call" | custom-call | flops 14949999616 | bytes 1024 | tf_op jit(solution)/shard_map/stack/pallas_call | solution.py:340
  94.2 0.0 collective-permute-done.6.refs_1_
  94.2 0.1 collective-permute-start.9
  94.3 10.1 %conv.7 = (bf16[1,3,360,128]{3,2,1,0:T(8,128)(2,1)}, bf16[1,3,360,128]{3,2,1,0:T(8,128)(2,1)}, bf16[1,3,360,128]{3,2,1,0:T(8,128)(2,1)}, bf16[1,3,360,128]{3,2,1,0:T(8,128)(2,1)}) custom-call(s32[1]{0:T(128)} %bitcast.me_ref, bf16[32,192,360]{2,1,0:T(8,128)(2,1)} %bitcast.20, bf16[32,192,8]{2,1,0:T(8,128)(2,1)} %bitcast.30, bf16[32,192,8]{2,1,0:T(8,128)(2,1)} %bitcast.40, ...), custom_call_target="tpu_custom_call" | custom-call | flops 13799999488 | bytes 1024 | tf_op jit(solution)/shard_map/conv/pallas_call | solution.py:139
  104.4 0.1 collective-permute-start.11
  104.4 12.2 %collective-permute-done.11.refs_1_ = bf16[1,3,360,128]{3,2,1,0:T(8,128)(2,1)S(1)} collective-permute-done((bf16[1,3,360,128]{3,2,1,0:T(8,128)(2,1)}, bf16[1,3,360,128]{3,2,1,0:T(8,128)(2,1)S(1)}, u32[]{:S(2)}, u32[]{:S(2)}) %collective-permute-start.11) | collective-permute-done | bytes 276512 | tf_op jit(solution)/shard_map/in3/ppermute | solution.py:314
  116.7 0.1 collective-permute-start.12
  116.8 1.1 broadcast_in_dim.12.refs_1_.refs_4_
  117.9 4.0 %collective-permute-start.13 = (bf16[1,3,360,128]{3,2,1,0:T(8,128)(2,1)}, bf16[1,3,360,128]{3,2,1,0:T(8,128)(2,1)S(1)}, u32[]{:S(2)}, u32[]{:S(2)}) collective-permute-start(bf16[1,3,360,128]{3,2,1,0:T(8,128)(2,1)} %get-tuple-element.61), channel_id=1, source_target_pairs={{0,2},{1,3},{2,0},{3,1},{4,6},{5,7},{6,4},{7,5},{8,10},{9,11},{10,... | collective-permute-start | bytes 829448 | tf_op jit(solution)/shard_map/in3/ppermute | solution.py:314
  121.9 2.7 %collective-permute-start.14 = (bf16[1,3,360,128]{3,2,1,0:T(8,128)(2,1)}, bf16[1,3,360,128]{3,2,1,0:T(8,128)(2,1)S(1)}, u32[]{:S(2)}, u32[]{:S(2)}) collective-permute-start(bf16[1,3,360,128]{3,2,1,0:T(8,128)(2,1)} %get-tuple-element.62), channel_id=1, source_target_pairs={{0,3},{1,0},{2,1},{3,2},{4,7},{5,4},{6,5},{7,6},{8,11},{9,8},{10,9... | collective-permute-start | bytes 829448 | tf_op jit(solution)/shard_map/in3/ppermute | solution.py:314
  124.7 15.4 %mlp.4 = (bf16[3,360,128]{2,1,0:T(8,128)(2,1)}, bf16[3,360,128]{2,1,0:T(8,128)(2,1)}, bf16[3,360,128]{2,1,0:T(8,128)(2,1)}, bf16[3,360,128]{2,1,0:T(8,128)(2,1)}) custom-call(s32[1]{0:T(128)} %bitcast.me_ref, bf16[4,3,360,128]{3,2,1,0:T(8,128)(2,1)} %copy-done.1, f32[768,1]{1,0:T(8,128)} %broadcast_in_dim.12.refs_1_.refs_4_, ...), custom_call_target="tpu_custom_call" | custom-call | flops 14949999616 | bytes 1024 | tf_op jit(solution)/shard_map/mlp/pallas_call | solution.py:243
  140.1 1.2 collective-permute-done.13.refs_2_
  141.3 1.4 collective-permute-start.15
  142.7 1.3 collective-permute-start.16
  144.0 2.0 collective-permute-start.17
  146.0 15.6 %mlp.5 = (bf16[3,360,128]{2,1,0:T(8,128)(2,1)}, bf16[3,360,128]{2,1,0:T(8,128)(2,1)}, bf16[3,360,128]{2,1,0:T(8,128)(2,1)}, bf16[3,360,128]{2,1,0:T(8,128)(2,1)}) custom-call(s32[1]{0:T(128)} %bitcast.me_ref, bf16[1,3,360,128]{3,2,1,0:T(8,128)(2,1)} %get-tuple-element.45.refs_0_, bf16[1,3,360,128]{3,2,1,0:T(8,128)(2,1)} %collective-permute-done.6.refs_1_, ...), custom_call_target="tpu_custom_call" | custom-call | flops 14949999616 | bytes 1024 | tf_op jit(solution)/shard_map/mlp/pallas_call | solution.py:243
  161.6 1.9 collective-permute-start.18
  163.5 0.6 collective-permute-start.20
  164.1 5.8 %collective-permute-done.16.refs_2_ = bf16[3,360,128]{2,1,0:T(8,128)(2,1)S(1)} collective-permute-done((bf16[3,360,128]{2,1,0:T(8,128)(2,1)}, bf16[3,360,128]{2,1,0:T(8,128)(2,1)S(1)}, u32[]{:S(2)}, u32[]{:S(2)}) %collective-permute-start.16) | collective-permute-done | bytes 276512 | tf_op jit(solution)/shard_map/out0/ppermute | solution.py:314
  170.0 15.6 %mlp.6 = (bf16[3,360,128]{2,1,0:T(8,128)(2,1)}, bf16[3,360,128]{2,1,0:T(8,128)(2,1)}, bf16[3,360,128]{2,1,0:T(8,128)(2,1)}, bf16[3,360,128]{2,1,0:T(8,128)(2,1)}) custom-call(s32[1]{0:T(128)} %bitcast.me_ref, bf16[4,3,360,128]{3,2,1,0:T(8,128)(2,1)} %copy-done, f32[768,1]{1,0:T(8,128)} %broadcast_in_dim.12.refs_1_.refs_4_, ...), custom_call_target="tpu_custom_call" | custom-call | flops 14949999616 | bytes 1024 | tf_op jit(solution)/shard_map/mlp/pallas_call | solution.py:243
  185.6 6.9 %collective-permute-done.19.refs_2_ = bf16[3,360,128]{2,1,0:T(8,128)(2,1)S(1)} collective-permute-done((bf16[3,360,128]{2,1,0:T(8,128)(2,1)}, bf16[3,360,128]{2,1,0:T(8,128)(2,1)S(1)}, u32[]{:S(2)}, u32[]{:S(2)}) %collective-permute-start.19) | collective-permute-done | bytes 276512 | tf_op jit(solution)/shard_map/out1/ppermute | solution.py:314
  192.6 0.1 collective-permute-start.21
  192.6 5.3 %collective-permute-start.22 = (bf16[3,360,128]{2,1,0:T(8,128)(2,1)}, bf16[3,360,128]{2,1,0:T(8,128)(2,1)S(1)}, u32[]{:S(2)}, u32[]{:S(2)}) collective-permute-start(bf16[3,360,128]{2,1,0:T(8,128)(2,1)} %get-tuple-element.77), channel_id=1, source_target_pairs={{0,2},{1,3},{2,0},{3,1},{4,6},{5,7},{6,4},{7,5},{8,10},{9,11},{10,... | collective-permute-start | bytes 829448 | tf_op jit(solution)/shard_map/out2/ppermute | solution.py:314
  197.9 1.9 collective-permute-start.23
  199.9 15.6 %mlp.7 = (bf16[3,360,128]{2,1,0:T(8,128)(2,1)}, bf16[3,360,128]{2,1,0:T(8,128)(2,1)}, bf16[3,360,128]{2,1,0:T(8,128)(2,1)}, bf16[3,360,128]{2,1,0:T(8,128)(2,1)}) custom-call(s32[1]{0:T(128)} %bitcast.me_ref, bf16[1,3,360,128]{3,2,1,0:T(8,128)(2,1)} %get-tuple-element.74.refs_0_, bf16[1,3,360,128]{3,2,1,0:T(8,128)(2,1)} %copy-done.10, ...), custom_call_target="tpu_custom_call" | custom-call | flops 14949999616 | bytes 1024 | tf_op jit(solution)/shard_map/mlp/pallas_call | solution.py:243
  215.5 1.9 collective-permute-start.24
  217.4 0.6 collective-permute-start.26
  218.1 6.2 %collective-permute-done.22.refs_2_ = bf16[3,360,128]{2,1,0:T(8,128)(2,1)S(1)} collective-permute-done((bf16[3,360,128]{2,1,0:T(8,128)(2,1)}, bf16[3,360,128]{2,1,0:T(8,128)(2,1)S(1)}, u32[]{:S(2)}, u32[]{:S(2)}) %collective-permute-start.22) | collective-permute-done | bytes 276512 | tf_op jit(solution)/shard_map/out2/ppermute | solution.py:314
  224.2 4.4 %add.4.refs_5_ = bf16[192,32,360]{2,1,0:T(8,128)(2,1)} custom-call(s32[1]{0:T(128)} %bitcast.me_ref, bf16[3,360,128]{2,1,0:T(8,128)(2,1)} %get-tuple-element.60.refs_0_, bf16[3,360,128]{2,1,0:T(8,128)(2,1)} %copy-done.11, bf16[3,360,128]{2,1,0:T(8,128)(2,1)} %copy-done.13, bf16[3,360,128]{2,1,0:T(8,128)(2,1)} %copy-done.15, bf16[192,32,360]{2,1,0:T(8,128)(2,1)} %refs_4_.7), custom_call_target="tpu_custom_call" | custom-call | flops 4600000000 | bytes 1024 | tf_op jit(solution)/shard_map/add/pallas_call | solution.py:292
  228.7 4.2 %add.5.refs_5_ = bf16[192,32,360]{2,1,0:T(8,128)(2,1)} custom-call(s32[1]{0:T(128)} %bitcast.me_ref, bf16[3,360,128]{2,1,0:T(8,128)(2,1)} %get-tuple-element.64.refs_0_, bf16[3,360,128]{2,1,0:T(8,128)(2,1)} %copy-done.16, bf16[3,360,128]{2,1,0:T(8,128)(2,1)} %copy-done.17, bf16[3,360,128]{2,1,0:T(8,128)(2,1)} %copy-done.18, ...), custom_call_target="tpu_custom_call", output_to_operand_aliasing={{}: (6, {})} | custom-call | flops 4600000000 | bytes 1024 | tf_op jit(solution)/shard_map/add/pallas_call | solution.py:292
  232.9 4.2 %add.6.refs_5_ = bf16[192,32,360]{2,1,0:T(8,128)(2,1)} custom-call(s32[1]{0:T(128)} %bitcast.me_ref, bf16[3,360,128]{2,1,0:T(8,128)(2,1)} %get-tuple-element.69.refs_0_, bf16[3,360,128]{2,1,0:T(8,128)(2,1)} %copy-done.19, bf16[3,360,128]{2,1,0:T(8,128)(2,1)} %copy-done.20, bf16[3,360,128]{2,1,0:T(8,128)(2,1)} %copy-done.21, ...), custom_call_target="tpu_custom_call", output_to_operand_aliasing={{}: (6, {})} | custom-call | flops 4600000000 | bytes 1024 | tf_op jit(solution)/shard_map/add/pallas_call | solution.py:292
  237.1 9.2 %collective-permute-done.25.refs_2_ = bf16[3,360,128]{2,1,0:T(8,128)(2,1)S(1)} collective-permute-done((bf16[3,360,128]{2,1,0:T(8,128)(2,1)}, bf16[3,360,128]{2,1,0:T(8,128)(2,1)S(1)}, u32[]{:S(2)}, u32[]{:S(2)}) %collective-permute-start.25) | collective-permute-done | bytes 276512 | tf_op jit(solution)/shard_map/out3/ppermute | solution.py:314
  246.3 0.7 copy-done.23
  247.0 0.7 copy-done.24
  247.7 4.2 %add.7 = bf16[192,32,360]{2,1,0:T(8,128)(2,1)} custom-call(s32[1]{0:T(128)} %bitcast.me_ref, bf16[3,360,128]{2,1,0:T(8,128)(2,1)} %get-tuple-element.75.refs_0_, bf16[3,360,128]{2,1,0:T(8,128)(2,1)} %copy-done.22, bf16[3,360,128]{2,1,0:T(8,128)(2,1)} %copy-done.23, bf16[3,360,128]{2,1,0:T(8,128)(2,1)} %copy-done.24, ...), custom_call_target="tpu_custom_call", output_to_operand_aliasing={{}: (6, {})} | custom-call | flops 4600000000 | bytes 1024 | tf_op jit(solution)/shard_map/add/pallas_call | solution.py:292
  (68 shorter events, 0.2 us)
Async XLA Ops:
  2.6 5.0 %copy-start.3 = (bf16[768,192]{0,1:T(8,128)(2,1)S(1)}, bf16[768,192]{0,1:T(8,128)(2,1)}, u32[]{:S(2)}) copy-start(bf16[768,192]{0,1:T(8,128)(2,1)} %param.11) | copy-start | bytes 884740
  4.5 3.1 %copy-start.4 = (bf16[768,192]{0,1:T(8,128)(2,1)S(1)}, bf16[768,192]{0,1:T(8,128)(2,1)}, u32[]{:S(2)}) copy-start(bf16[768,192]{0,1:T(8,128)(2,1)} %param.10) | copy-start | bytes 884740
  4.5 11.5 %collective-permute-start = (bf16[192,32,8]{0,2,1:T(8,128)(2,1)}, bf16[192,32,8]{0,2,1:T(8,128)(2,1)S(1)}, u32[]{:S(2)}, u32[]{:S(2)}) collective-permute-start(bf16[192,32,8]{0,2,1:T(8,128)(2,1)} %copy.35), channel_id=1, source_target_pairs={{0,4},{4,8},{8,12},{12,0},{1,5},{5,9},{9,13},{13,1},{2,6},{6,10},{... | collective-permute-start | bytes 294920 | tf_op jit(solution)/shard_map/halo/ppermute | solution.py:314
  5.8 11.7 %collective-permute-start.1 = (bf16[192,32,8]{0,2,1:T(8,128)(2,1)S(1)}, bf16[192,32,8]{0,2,1:T(8,128)(2,1)S(1)}, u32[]{:S(2)}, u32[]{:S(2)}) collective-permute-start(bf16[192,32,8]{0,2,1:T(8,128)(2,1)S(1)} %copy.36), channel_id=1, source_target_pairs={{0,12},{4,0},{8,4},{12,8},{1,13},{5,1},{9,5},{13,9},{2,14},{6,2},{... | collective-permute-start | bytes 294920 | tf_op jit(solution)/shard_map/halo/ppermute | solution.py:314
  7.7 28.6 %copy-start.2 = (bf16[1,384,768]{2,1,0:T(8,128)(2,1)}, bf16[1,384,768]{2,1,0:T(8,128)(2,1)S(1)}, u32[]{:S(2)}) copy-start(bf16[1,384,768]{2,1,0:T(8,128)(2,1)S(1)} %maximum_bitcast_fusion.refs_0_) | copy-start | bytes 1769476
  7.7 30.1 %collective-permute-start.2 = (bf16[1,384,768]{2,1,0:T(8,128)(2,1)S(1)}, bf16[1,384,768]{2,1,0:T(8,128)(2,1)S(1)}, u32[]{:S(2)}, u32[]{:S(2)}) collective-permute-start(bf16[1,384,768]{2,1,0:T(8,128)(2,1)S(1)} %maximum_bitcast_fusion.refs_0_), channel_id=1, source_target_pairs={{0,2},{1,3},{2,0},{3,1},{4,6},{5,7},{6,4},{7,5},{8,10},{9,11},{10,... | collective-permute-start | bytes 1769480 | tf_op jit(solution)/shard_map/wz/ppermute | solution.py:318
  8.1 29.7 %collective-permute-start.3 = (bf16[1,384,768]{2,1,0:T(8,128)(2,1)S(1)}, bf16[1,384,768]{2,1,0:T(8,128)(2,1)}, u32[]{:S(2)}, u32[]{:S(2)}) collective-permute-start(bf16[1,384,768]{2,1,0:T(8,128)(2,1)S(1)} %maximum_bitcast_fusion.refs_0_), channel_id=1, source_target_pairs={{0,1},{1,0},{2,3},{3,2},{4,5},{5,4},{6,7},{7,6},{8,9},{9,8},{10,11... | collective-permute-start | bytes 1769480 | tf_op jit(solution)/shard_map/wz/ppermute | solution.py:318
  8.3 6.3 %copy-start.5 = (f32[9,192]{1,0:T(8,128)S(1)}, f32[9,192]{1,0:T(8,128)}, u32[]{:S(2)}) copy-start(f32[9,192]{1,0:T(8,128)} %param.8) | copy-start | bytes 20740
  8.3 7.0 %copy-start.6 = (f32[9,192]{1,0:T(8,128)S(1)}, f32[9,192]{1,0:T(8,128)}, u32[]{:S(2)}) copy-start(f32[9,192]{1,0:T(8,128)} %param.7) | copy-start | bytes 20740
  28.9 50.1 %all-to-all-start.1 = ((bf16[4,3,360,128]{3,2,1,0:T(8,128)(2,1)}), bf16[4,3,360,128]{3,2,1,0:T(8,128)(2,1)S(1)}, u32[]{:S(2)}, u32[]{:S(2)}) async-start(bf16[4,3,360,128]{3,2,1,0:T(8,128)(2,1)} %conv.4), calls=%async_computation.1 | async-start | bytes 2211840 | tf_op jit(solution)/shard_map/in0/all_to_all | solution.py:388
  36.2 26.1 %collective-permute-start.5 = (bf16[1,384,768]{2,1,0:T(8,128)(2,1)S(1)}, bf16[1,384,768]{2,1,0:T(8,128)(2,1)S(1)}, u32[]{:S(2)}, u32[]{:S(2)}) collective-permute-start(bf16[1,384,768]{2,1,0:T(8,128)(2,1)S(1)} %maximum_bitcast_fusion.refs_0_), channel_id=1, source_target_pairs={{0,8},{4,12},{8,0},{12,4},{1,9},{5,13},{9,1},{13,5},{2,10},{6,14},... | collective-permute-start | bytes 1769480 | tf_op jit(solution)/shard_map/wx0/ppermute | solution.py:318
  37.7 10.6 %copy-start.8 = (bf16[1,384,768]{2,1,0:T(8,128)(2,1)}, bf16[1,384,768]{2,1,0:T(8,128)(2,1)S(1)}, u32[]{:S(2)}) copy-start(bf16[1,384,768]{2,1,0:T(8,128)(2,1)S(1)} %collective-permute-done.2.refs_0_) | copy-start | bytes 1769476
  48.4 27.4 %collective-permute-start.4 = (bf16[1,384,768]{2,1,0:T(8,128)(2,1)S(1)}, bf16[1,384,768]{2,1,0:T(8,128)(2,1)}, u32[]{:S(2)}, u32[]{:S(2)}) collective-permute-start(bf16[1,384,768]{2,1,0:T(8,128)(2,1)S(1)} %collective-permute-done.2.refs_0_), channel_id=1, source_target_pairs={{0,1},{1,0},{2,3},{3,2},{4,5},{5,4},{6,7},{7,6},{8,9},{9,8},{10,11... | collective-permute-start | bytes 1769480 | tf_op jit(solution)/shard_map/wz1/ppermute | solution.py:318
  59.4 34.8 %collective-permute-start.6 = (bf16[1,3,360,128]{3,2,1,0:T(8,128)(2,1)}, bf16[1,3,360,128]{3,2,1,0:T(8,128)(2,1)}, u32[]{:S(2)}, u32[]{:S(2)}) collective-permute-start(bf16[1,3,360,128]{3,2,1,0:T(8,128)(2,1)} %get-tuple-element.53), channel_id=1, source_target_pairs={{0,1},{1,2},{2,3},{3,0},{4,5},{5,6},{6,7},{7,4},{8,9},{9,10},{10,1... | collective-permute-start | bytes 829448 | tf_op jit(solution)/shard_map/in1/ppermute | solution.py:314
  60.8 33.4 %collective-permute-start.7 = (bf16[1,3,360,128]{3,2,1,0:T(8,128)(2,1)}, bf16[1,3,360,128]{3,2,1,0:T(8,128)(2,1)}, u32[]{:S(2)}, u32[]{:S(2)}) collective-permute-start(bf16[1,3,360,128]{3,2,1,0:T(8,128)(2,1)} %get-tuple-element.54), channel_id=1, source_target_pairs={{0,2},{1,3},{2,0},{3,1},{4,6},{5,7},{6,4},{7,5},{8,10},{9,11},{10,... | collective-permute-start | bytes 829448 | tf_op jit(solution)/shard_map/in1/ppermute | solution.py:314
  62.3 31.9 %collective-permute-start.8 = (bf16[1,3,360,128]{3,2,1,0:T(8,128)(2,1)}, bf16[1,3,360,128]{3,2,1,0:T(8,128)(2,1)}, u32[]{:S(2)}, u32[]{:S(2)}) collective-permute-start(bf16[1,3,360,128]{3,2,1,0:T(8,128)(2,1)} %get-tuple-element.55), channel_id=1, source_target_pairs={{0,3},{1,0},{2,1},{3,2},{4,7},{5,4},{6,5},{7,6},{8,11},{9,8},{10,9... | collective-permute-start | bytes 829448 | tf_op jit(solution)/shard_map/in1/ppermute | solution.py:314
  62.3 16.7 %copy-start.9 = (bf16[1,384,768]{2,1,0:T(8,128)(2,1)}, bf16[1,384,768]{2,1,0:T(8,128)(2,1)S(1)}, u32[]{:S(2)}) copy-start(bf16[1,384,768]{2,1,0:T(8,128)(2,1)S(1)} %collective-permute-done.5.refs_1_) | copy-start | bytes 1769476
  79.0 37.7 %collective-permute-start.10 = (bf16[3,384,768]{2,1,0:T(8,128)(2,1)}, bf16[3,384,768]{2,1,0:T(8,128)(2,1)}, u32[]{:S(2)}, u32[]{:S(2)}) collective-permute-start(bf16[3,384,768]{2,1,0:T(8,128)(2,1)} %stack.2.refs_2_), channel_id=1, source_target_pairs={{0,8},{4,12},{8,0},{12,4},{1,9},{5,13},{9,1},{13,5},{2,10},{6,14},... | collective-permute-start | bytes 5308424 | tf_op jit(solution)/shard_map/wx1/ppermute | solution.py:318
  79.0 15.2 %copy-start.1 = (bf16[4,3,360,128]{3,2,1,0:T(8,128)(2,1)}, bf16[4,3,360,128]{3,2,1,0:T(8,128)(2,1)S(1)}, u32[]{:S(2)}) copy-start(bf16[4,3,360,128]{3,2,1,0:T(8,128)(2,1)S(1)} %all-to-all-done.1.refs_0_) | copy-start | bytes 3317764
  79.0 37.7 %all-to-all-start = ((bf16[4,3,360,128]{3,2,1,0:T(8,128)(2,1)}), bf16[4,3,360,128]{3,2,1,0:T(8,128)(2,1)S(1)}, u32[]{:S(2)}, u32[]{:S(2)}) async-start(bf16[4,3,360,128]{3,2,1,0:T(8,128)(2,1)} %conv.6), calls=%async_computation | async-start | bytes 2211840 | tf_op jit(solution)/shard_map/in2/all_to_all | solution.py:388
  94.2 22.6 %copy-start.7 = (f32[768]{0:T(1024)S(1)}, f32[768]{0:T(1024)}, u32[]{:S(2)}) copy-start(f32[768]{0:T(1024)} %param.9) | copy-start | bytes 9220
  94.2 30.4 %collective-permute-start.9 = (bf16[5,384,768]{2,1,0:T(8,128)(2,1)}, bf16[5,384,768]{2,1,0:T(8,128)(2,1)}, u32[]{:S(2)}, u32[]{:S(2)}) collective-permute-start(bf16[5,384,768]{2,1,0:T(8,128)(2,1)} %stack.3.refs_2_.refs_5_), channel_id=1, source_target_pairs={{0,4},{4,0},{8,12},{12,8},{1,5},{5,1},{9,13},{13,9},{2,6},{6,2},{1... | collective-permute-start | bytes 8847368 | tf_op jit(solution)/shard_map/wc0/ppermute | solution.py:318
  104.4 12.3 %collective-permute-start.11 = (bf16[1,3,360,128]{3,2,1,0:T(8,128)(2,1)}, bf16[1,3,360,128]{3,2,1,0:T(8,128)(2,1)S(1)}, u32[]{:S(2)}, u32[]{:S(2)}) collective-permute-start(bf16[1,3,360,128]{3,2,1,0:T(8,128)(2,1)} %get-tuple-element.58), channel_id=1, source_target_pairs={{0,1},{1,2},{2,3},{3,0},{4,5},{5,6},{6,7},{7,4},{8,9},{9,10},{10,1... | collective-permute-start | bytes 829448 | tf_op jit(solution)/shard_map/in3/ppermute | solution.py:314
  116.6 23.5 %copy-start.10 = (bf16[1,3,360,128]{3,2,1,0:T(8,128)(2,1)}, bf16[1,3,360,128]{3,2,1,0:T(8,128)(2,1)S(1)}, u32[]{:S(2)}) copy-start(bf16[1,3,360,128]{3,2,1,0:T(8,128)(2,1)S(1)} %collective-permute-done.11.refs_1_) | copy-start | bytes 829444
  116.7 23.5 %copy-start = (bf16[4,3,360,128]{3,2,1,0:T(8,128)(2,1)}, bf16[4,3,360,128]{3,2,1,0:T(8,128)(2,1)S(1)}, u32[]{:S(2)}) copy-start(bf16[4,3,360,128]{3,2,1,0:T(8,128)(2,1)S(1)} %all-to-all-done.refs_0_) | copy-start | bytes 3317764
  116.7 8.0 %collective-permute-start.12 = (bf16[3,384,768]{2,1,0:T(8,128)(2,1)}, bf16[3,384,768]{2,1,0:T(8,128)(2,1)}, u32[]{:S(2)}, u32[]{:S(2)}) collective-permute-start(bf16[3,384,768]{2,1,0:T(8,128)(2,1)} %collective-permute-done.10.refs_4_.refs_7_), channel_id=1, source_target_pairs={{0,4},{4,0},{8,12},{12,8},{1,5},{5,1},{9,13},{13,9},{2,6},{6,2},{1... | collective-permute-start | bytes 5308424 | tf_op jit(solution)/shard_map/wc1/ppermute | solution.py:318
  117.9 23.4 %collective-permute-start.13 = (bf16[1,3,360,128]{3,2,1,0:T(8,128)(2,1)}, bf16[1,3,360,128]{3,2,1,0:T(8,128)(2,1)S(1)}, u32[]{:S(2)}, u32[]{:S(2)}) collective-permute-start(bf16[1,3,360,128]{3,2,1,0:T(8,128)(2,1)} %get-tuple-element.61), channel_id=1, source_target_pairs={{0,2},{1,3},{2,0},{3,1},{4,6},{5,7},{6,4},{7,5},{8,10},{9,11},{10,... | collective-permute-start | bytes 829448 | tf_op jit(solution)/shard_map/in3/ppermute | solution.py:314
  121.9 19.3 %collective-permute-start.14 = (bf16[1,3,360,128]{3,2,1,0:T(8,128)(2,1)}, bf16[1,3,360,128]{3,2,1,0:T(8,128)(2,1)S(1)}, u32[]{:S(2)}, u32[]{:S(2)}) collective-permute-start(bf16[1,3,360,128]{3,2,1,0:T(8,128)(2,1)} %get-tuple-element.62), channel_id=1, source_target_pairs={{0,3},{1,0},{2,1},{3,2},{4,7},{5,4},{6,5},{7,6},{8,11},{9,8},{10,9... | collective-permute-start | bytes 829448 | tf_op jit(solution)/shard_map/in3/ppermute | solution.py:314
  141.3 20.4 %copy-start.12 = (bf16[1,3,360,128]{3,2,1,0:T(8,128)(2,1)}, bf16[1,3,360,128]{3,2,1,0:T(8,128)(2,1)S(1)}, u32[]{:S(2)}) copy-start(bf16[1,3,360,128]{3,2,1,0:T(8,128)(2,1)S(1)} %collective-permute-done.13.refs_2_) | copy-start | bytes 829444
  141.3 20.4 %copy-start.14 = (bf16[1,3,360,128]{3,2,1,0:T(8,128)(2,1)}, bf16[1,3,360,128]{3,2,1,0:T(8,128)(2,1)S(1)}, u32[]{:S(2)}) copy-start(bf16[1,3,360,128]{3,2,1,0:T(8,128)(2,1)S(1)} %collective-permute-done.14.refs_3_) | copy-start | bytes 829444
  141.3 22.2 %collective-permute-start.15 = (bf16[3,360,128]{2,1,0:T(8,128)(2,1)}, bf16[3,360,128]{2,1,0:T(8,128)(2,1)S(1)}, u32[]{:S(2)}, u32[]{:S(2)}) collective-permute-start(bf16[3,360,128]{2,1,0:T(8,128)(2,1)} %get-tuple-element.65), channel_id=1, source_target_pairs={{0,1},{1,2},{2,3},{3,0},{4,5},{5,6},{6,7},{7,4},{8,9},{9,10},{10,1... | collective-permute-start | bytes 829448 | tf_op jit(solution)/shard_map/out0/ppermute | solution.py:314
  142.7 27.3 %collective-permute-start.16 = (bf16[3,360,128]{2,1,0:T(8,128)(2,1)}, bf16[3,360,128]{2,1,0:T(8,128)(2,1)S(1)}, u32[]{:S(2)}, u32[]{:S(2)}) collective-permute-start(bf16[3,360,128]{2,1,0:T(8,128)(2,1)} %get-tuple-element.66), channel_id=1, source_target_pairs={{0,2},{1,3},{2,0},{3,1},{4,6},{5,7},{6,4},{7,5},{8,10},{9,11},{10,... | collective-permute-start | bytes 829448 | tf_op jit(solution)/shard_map/out0/ppermute | solution.py:314
  144.0 26.0 %collective-permute-start.17 = (bf16[3,360,128]{2,1,0:T(8,128)(2,1)}, bf16[3,360,128]{2,1,0:T(8,128)(2,1)S(1)}, u32[]{:S(2)}, u32[]{:S(2)}) collective-permute-start(bf16[3,360,128]{2,1,0:T(8,128)(2,1)} %get-tuple-element.67), channel_id=1, source_target_pairs={{0,3},{1,0},{2,1},{3,2},{4,7},{5,4},{6,5},{7,6},{8,11},{9,8},{10,9... | collective-permute-start | bytes 829448 | tf_op jit(solution)/shard_map/out0/ppermute | solution.py:314
  161.6 23.9 %collective-permute-start.18 = (bf16[3,360,128]{2,1,0:T(8,128)(2,1)}, bf16[3,360,128]{2,1,0:T(8,128)(2,1)S(1)}, u32[]{:S(2)}, u32[]{:S(2)}) collective-permute-start(bf16[3,360,128]{2,1,0:T(8,128)(2,1)} %get-tuple-element.70), channel_id=1, source_target_pairs={{0,1},{1,2},{2,3},{3,0},{4,5},{5,6},{6,7},{7,4},{8,9},{9,10},{10,1... | collective-permute-start | bytes 829448 | tf_op jit(solution)/shard_map/out1/ppermute | solution.py:314
  163.5 29.0 %collective-permute-start.19 = (bf16[3,360,128]{2,1,0:T(8,128)(2,1)}, bf16[3,360,128]{2,1,0:T(8,128)(2,1)S(1)}, u32[]{:S(2)}, u32[]{:S(2)}) collective-permute-start(bf16[3,360,128]{2,1,0:T(8,128)(2,1)} %get-tuple-element.71), channel_id=1, source_target_pairs={{0,2},{1,3},{2,0},{3,1},{4,6},{5,7},{6,4},{7,5},{8,10},{9,11},{10,... | collective-permute-start | bytes 829448 | tf_op jit(solution)/shard_map/out1/ppermute | solution.py:314
  163.5 22.1 %copy-start.11 = (bf16[3,360,128]{2,1,0:T(8,128)(2,1)}, bf16[3,360,128]{2,1,0:T(8,128)(2,1)S(1)}, u32[]{:S(2)}) copy-start(bf16[3,360,128]{2,1,0:T(8,128)(2,1)S(1)} %collective-permute-done.15.refs_1_) | copy-start | bytes 829444
  163.5 29.0 %collective-permute-start.20 = (bf16[3,360,128]{2,1,0:T(8,128)(2,1)}, bf16[3,360,128]{2,1,0:T(8,128)(2,1)S(1)}, u32[]{:S(2)}, u32[]{:S(2)}) collective-permute-start(bf16[3,360,128]{2,1,0:T(8,128)(2,1)} %get-tuple-element.72), channel_id=1, source_target_pairs={{0,3},{1,0},{2,1},{3,2},{4,7},{5,4},{6,5},{7,6},{8,11},{9,8},{10,9... | collective-permute-start | bytes 829448 | tf_op jit(solution)/shard_map/out1/ppermute | solution.py:314
  170.0 15.6 %copy-start.13 = (bf16[3,360,128]{2,1,0:T(8,128)(2,1)}, bf16[3,360,128]{2,1,0:T(8,128)(2,1)S(1)}, u32[]{:S(2)}) copy-start(bf16[3,360,128]{2,1,0:T(8,128)(2,1)S(1)} %collective-permute-done.16.refs_2_) | copy-start | bytes 829444
  170.0 15.6 %copy-start.15 = (bf16[3,360,128]{2,1,0:T(8,128)(2,1)}, bf16[3,360,128]{2,1,0:T(8,128)(2,1)S(1)}, u32[]{:S(2)}) copy-start(bf16[3,360,128]{2,1,0:T(8,128)(2,1)S(1)} %collective-permute-done.17.refs_3_) | copy-start | bytes 829444
  185.6 29.9 %copy-start.16 = (bf16[3,360,128]{2,1,0:T(8,128)(2,1)}, bf16[3,360,128]{2,1,0:T(8,128)(2,1)S(1)}, u32[]{:S(2)}) copy-start(bf16[3,360,128]{2,1,0:T(8,128)(2,1)S(1)} %collective-permute-done.18.refs_1_) | copy-start | bytes 829444
  192.5 22.9 %copy-start.17 = (bf16[3,360,128]{2,1,0:T(8,128)(2,1)}, bf16[3,360,128]{2,1,0:T(8,128)(2,1)S(1)}, u32[]{:S(2)}) copy-start(bf16[3,360,128]{2,1,0:T(8,128)(2,1)S(1)} %collective-permute-done.19.refs_2_) | copy-start | bytes 829444
  192.5 22.9 %copy-start.18 = (bf16[3,360,128]{2,1,0:T(8,128)(2,1)}, bf16[3,360,128]{2,1,0:T(8,128)(2,1)S(1)}, u32[]{:S(2)}) copy-start(bf16[3,360,128]{2,1,0:T(8,128)(2,1)S(1)} %collective-permute-done.20.refs_3_) | copy-start | bytes 829444
  192.6 24.9 %collective-permute-start.21 = (bf16[3,360,128]{2,1,0:T(8,128)(2,1)}, bf16[3,360,128]{2,1,0:T(8,128)(2,1)S(1)}, u32[]{:S(2)}, u32[]{:S(2)}) collective-permute-start(bf16[3,360,128]{2,1,0:T(8,128)(2,1)} %get-tuple-element.76), channel_id=1, source_target_pairs={{0,1},{1,2},{2,3},{3,0},{4,5},{5,6},{6,7},{7,4},{8,9},{9,10},{10,1... | collective-permute-start | bytes 829448 | tf_op jit(solution)/shard_map/out2/ppermute | solution.py:314
  192.6 31.6 %collective-permute-start.22 = (bf16[3,360,128]{2,1,0:T(8,128)(2,1)}, bf16[3,360,128]{2,1,0:T(8,128)(2,1)S(1)}, u32[]{:S(2)}, u32[]{:S(2)}) collective-permute-start(bf16[3,360,128]{2,1,0:T(8,128)(2,1)} %get-tuple-element.77), channel_id=1, source_target_pairs={{0,2},{1,3},{2,0},{3,1},{4,6},{5,7},{6,4},{7,5},{8,10},{9,11},{10,... | collective-permute-start | bytes 829448 | tf_op jit(solution)/shard_map/out2/ppermute | solution.py:314
  197.9 26.3 %collective-permute-start.23 = (bf16[3,360,128]{2,1,0:T(8,128)(2,1)}, bf16[3,360,128]{2,1,0:T(8,128)(2,1)S(1)}, u32[]{:S(2)}, u32[]{:S(2)}) collective-permute-start(bf16[3,360,128]{2,1,0:T(8,128)(2,1)} %get-tuple-element.78), channel_id=1, source_target_pairs={{0,3},{1,0},{2,1},{3,2},{4,7},{5,4},{6,5},{7,6},{8,11},{9,8},{10,9... | collective-permute-start | bytes 829448 | tf_op jit(solution)/shard_map/out2/ppermute | solution.py:314
  215.5 21.6 %collective-permute-start.24 = (bf16[3,360,128]{2,1,0:T(8,128)(2,1)}, bf16[3,360,128]{2,1,0:T(8,128)(2,1)S(1)}, u32[]{:S(2)}, u32[]{:S(2)}) collective-permute-start(bf16[3,360,128]{2,1,0:T(8,128)(2,1)} %get-tuple-element.80), channel_id=1, source_target_pairs={{0,1},{1,2},{2,3},{3,0},{4,5},{5,6},{6,7},{7,4},{8,9},{9,10},{10,1... | collective-permute-start | bytes 829448 | tf_op jit(solution)/shard_map/out3/ppermute | solution.py:314
  217.4 28.9 %collective-permute-start.25 = (bf16[3,360,128]{2,1,0:T(8,128)(2,1)}, bf16[3,360,128]{2,1,0:T(8,128)(2,1)S(1)}, u32[]{:S(2)}, u32[]{:S(2)}) collective-permute-start(bf16[3,360,128]{2,1,0:T(8,128)(2,1)} %get-tuple-element.81), channel_id=1, source_target_pairs={{0,2},{1,3},{2,0},{3,1},{4,6},{5,7},{6,4},{7,5},{8,10},{9,11},{10,... | collective-permute-start | bytes 829448 | tf_op jit(solution)/shard_map/out3/ppermute | solution.py:314
  217.4 11.2 %copy-start.19 = (bf16[3,360,128]{2,1,0:T(8,128)(2,1)}, bf16[3,360,128]{2,1,0:T(8,128)(2,1)S(1)}, u32[]{:S(2)}) copy-start(bf16[3,360,128]{2,1,0:T(8,128)(2,1)S(1)} %collective-permute-done.21.refs_1_) | copy-start | bytes 829444
  217.4 28.9 %collective-permute-start.26 = (bf16[3,360,128]{2,1,0:T(8,128)(2,1)}, bf16[3,360,128]{2,1,0:T(8,128)(2,1)S(1)}, u32[]{:S(2)}, u32[]{:S(2)}) collective-permute-start(bf16[3,360,128]{2,1,0:T(8,128)(2,1)} %get-tuple-element.82), channel_id=1, source_target_pairs={{0,3},{1,0},{2,1},{3,2},{4,7},{5,4},{6,5},{7,6},{8,11},{9,8},{10,9... | collective-permute-start | bytes 829448 | tf_op jit(solution)/shard_map/out3/ppermute | solution.py:314
  224.2 4.4 %copy-start.20 = (bf16[3,360,128]{2,1,0:T(8,128)(2,1)}, bf16[3,360,128]{2,1,0:T(8,128)(2,1)S(1)}, u32[]{:S(2)}) copy-start(bf16[3,360,128]{2,1,0:T(8,128)(2,1)S(1)} %collective-permute-done.22.refs_2_) | copy-start | bytes 829444
  224.2 4.4 %copy-start.21 = (bf16[3,360,128]{2,1,0:T(8,128)(2,1)}, bf16[3,360,128]{2,1,0:T(8,128)(2,1)S(1)}, u32[]{:S(2)}) copy-start(bf16[3,360,128]{2,1,0:T(8,128)(2,1)S(1)} %collective-permute-done.23.refs_3_) | copy-start | bytes 829444
  237.1 9.2 %copy-start.22 = (bf16[3,360,128]{2,1,0:T(8,128)(2,1)}, bf16[3,360,128]{2,1,0:T(8,128)(2,1)S(1)}, u32[]{:S(2)}) copy-start(bf16[3,360,128]{2,1,0:T(8,128)(2,1)S(1)} %collective-permute-done.24.refs_1_) | copy-start | bytes 829444
  246.3 0.7 copy-start.23
  247.0 0.7 copy-start.24
